TPU v7x, 32 devices: a whole 2x2x4 slice. The times are simulated.
32 devices in a mesh: clips: 2 (over x), gx: 4 (over y, core), gy: 4 (over z).
Axes of the slice: x: 2, y: 2, z: 4, core: 2. Of those that a mesh axis runs over, the one named last changes fastest.
Arguments:
- fields: float32 [12, 32, 32, 512], P('clips', None, 'gx', 'gy'), parts along dimension 0, may hold values from -6 to 6
- material_map: int32 [64, 32, 512], P('clips', 'gx', 'gy'), parts along dimension 0, may hold values from 0 to 3
- material_eps: float32 [4], replicated, may hold values from 1 to 4
- material_loss: float32 [4], replicated, may hold values from 0 to 0.4
- source_shift: int32 [64, 2], P(('gx', 'gy')), may hold values from -8 to 8
- source_mask: int32 [64, 96, 96], P(('gx', 'gy')), may hold values 0 or 1
- source_weight: float32 [64], P(('gx', 'gy')), may hold values from 0.25 to 4
Outputs:
- final_fields: float32 [12, 32, 32, 512], P('clips', None, 'gx', 'gy'), parts along dimension 0
- image: float32 [512, 1024], P(('gx', 'gy'), 'clips'), parts along dimension 1
There are 2 independent parts, one for each index of `clips`. A program takes and returns all parts, laid end to end along the dimension named above; an argument that names none is the same for every part. Nothing has to cross between parts.
All inputs are finite; a program needn't handle non-finite values. No bound on the sum of `source_mask` on one device may be relied on, other than what follows from the above.
Results may differ from a plain program's by a relative error of at most 0.0014.
The roundings to bfloat16 on the way count: a program that leaves them out, or rounds other values in their place, can miss the bound.
Values sent between devices are 32-bit elements; how exact they have to be, the bound alone decides.
No kernel may reach another device: no remote copies, remote signals or barrier semaphores. Data moves between devices by JAX's collectives and lax.ppermute only.
A program may use at most 64 MiB of HBM per device.

v0:
```python
import functools
import math

import jax
import jax.numpy as jnp
import numpy as np
from jax import lax
from jax.experimental import pallas as pl
from jax.experimental.pallas import tpu as pltpu
from jax.sharding import PartitionSpec as P

STEPS = 12
ROUNDS = 2
M = 512
REACH = 8

COURANT = 0.55
ANGULAR = 0.7
PRECISE = lax.Precision.HIGHEST


F32 = jnp.float32
BF16 = jnp.bfloat16


def vmem():
    return pl.BlockSpec(memory_space=pltpu.VMEM)


def smem():
    return pl.BlockSpec(memory_space=pltpu.SMEM)


def call(kernel, ins, outs, scratch=(), limit=16):
    spaces = {"h": vmem, "v": vmem, "s": smem}

    def out_spec(out):
        return vmem() if not isinstance(out, jax.ShapeDtypeStruct) else pl.BlockSpec(memory_space=pl.ANY)

    held = [
        pltpu.with_memory_space_constraint(array, pltpu.VMEM) if space == "v" else array
        for array, space in ins
    ]
    return pl.pallas_call(
        kernel,
        out_shape=outs,
        in_specs=[spaces[space]() for _, space in ins],
        out_specs=[out_spec(out) for out in outs],
        scratch_shapes=list(scratch),
        compiler_params=pltpu.CompilerParams(vmem_limit_bytes=limit << 20),
    )(*held)


def shape(*dims, dtype=F32):
    return pltpu.VMEM(dims, dtype)


def swap(values, axis, first):
    count = lax.axis_size(axis)
    pairs = []
    for low in range(first, count - 1, 2):
        pairs += [(low, low + 1), (low + 1, low)]
    if not pairs:
        return jnp.zeros_like(values)
    return lax.ppermute(values, axis, pairs)


def cyclic(values, axis, by):
    count = lax.axis_size(axis)
    return lax.ppermute(values, axis, [(i, (i + by) % count) for i in range(count)])


def waves(order_ids, cell_ids, period):
    wrapped = (order_ids[:, None] * cell_ids[None, :]) % period
    angles = 2.0 * math.pi / period * wrapped
    return np.cos(angles), np.sin(angles)


def pack_kernel(
    fields, materials, shifts, weights, masks, send_a, send_b, send_c, send_d, source_pack, rows, *, geo
):
    depth, cells_x, lanes, halo, slot = geo
    even_x = lax.axis_index("gx") % 2 == 0
    even_y = lax.axis_index("gy") % 2 == 0
    lane = lax.broadcasted_iota(jnp.int32, (depth, lanes), 1)
    for comp in range(7):
        high = jnp.zeros((depth, lanes), F32)
        low = jnp.zeros((depth, lanes), F32)
        for x in range(cells_x):
            if comp < 6:
                values = fields[comp, pl.ds(x, depth, stride=cells_x), :]
            else:
                values = materials[pl.ds(x, depth, stride=cells_x), :].astype(F32)
            rows[x, comp] = values
            here = (lane >= slot * x) & (lane < slot * (x + 1))
            high = jnp.where(here, pltpu.roll(values, (slot * x + slot) % lanes, 1), high)
            low = jnp.where(here, pltpu.roll(values, slot * x, 1) if x else values, low)
        send_c[comp] = jnp.where(even_y, high, low)
        send_d[comp] = jnp.where(even_y, low, high)
    far = cells_x - halo
    send_a[...] = rows[pl.ds(jnp.where(even_x, far, 0), halo)]
    send_b[...] = rows[pl.ds(jnp.where(even_x, 0, far), halo)]
    orders_p, orders_q = masks.shape[1:]
    source_pack[...] = jnp.zeros(source_pack.shape, F32)
    for source in range(masks.shape[0]):
        source_pack[source, 0:orders_p, 0:orders_q] = masks[source].astype(F32)
        for at, fact in enumerate((shifts[0, source], shifts[1, source], weights[source])):
            source_pack[source, orders_p : orders_p + 1, at : at + 1] = jnp.full((1, 1), fact).astype(F32)


def inside_lanes(lane, cells_y, total_y, slot):
    start = lax.axis_index("gy") * cells_y
    ring = 2 * cells_y
    place = start + jnp.where(lane < cells_y + slot, lane, lane - ring)
    held = (lane < cells_y + slot) | (lane >= ring - slot)
    return held & (place >= 0) & (place < total_y)


def run_steps(state, keep, curl, gate, phase, moments, first_step, geo, count):
    depth, cells_x, lanes, halo, _ = geo
    ring = 2 * lanes
    middle = depth // 2
    level = lax.broadcasted_iota(jnp.int32, (depth, ring), 0)
    at_top = level == depth - 1
    at_bottom = level == 0

    def next_y(values):
        return pltpu.roll(values, ring - 1, 1)

    def last_y(values):
        return pltpu.roll(values, 1, 1)

    def next_z(values):
        return jnp.where(at_top, 0.0, pltpu.roll(values, depth - 1, 0))

    def last_z(values):
        return jnp.where(at_bottom, 0.0, pltpu.roll(values, 1, 0))

    def step(index, carry):
        def row(i, inner):
            ex, ey, ez = state[0, i], state[1, i], state[2, i]
            open_h = gate[i]
            hx = state[3, i] - open_h * ((next_y(ez) - ez) - (next_z(ey) - ey))
            hy = state[4, i] - open_h * ((next_z(ex) - ex) - (state[2, i + 1] - ez))
            hz = state[5, i] - open_h * ((state[1, i + 1] - ey) - (next_y(ex) - ex))
            state[3, i] = hx
            state[4, i] = hy
            state[5, i] = hz
            before = jnp.maximum(i - 1, 0)
            kept, turned = keep[i], curl[i]
            state[0, i] = kept * ex + turned * ((hz - last_y(hz)) - (hy - last_z(hy)))
            state[1, i] = kept * ey + turned * ((hx - last_z(hx)) - (hz - state[5, before]))
            state[2, i] = kept * ez + turned * ((hy - state[4, before]) - (hx - last_y(hx)))
            return inner

        lax.fori_loop(index, cells_x + 2 * halo - 1 - index, row, 0)
        at = first_step + index
        cosine, sine = moments[at, 0], moments[at, 1]
        for comp in range(2):
            monitor = state[comp, halo : halo + cells_x, middle, 0:lanes]
            low = comp * cells_x
            phase[low : low + cells_x, :] = phase[low : low + cells_x, :] + monitor * cosine
            low = (2 + comp) * cells_x
            phase[low : low + cells_x, :] = phase[low : low + cells_x, :] - monitor * sine
        return carry

    lax.fori_loop(0, count, step, 0)


def set_gate(gate, geo, total_x, total_y):
    _, cells_x, lanes, halo, slot = geo
    lane = lax.broadcasted_iota(jnp.int32, (1, 2 * lanes), 1)
    held = jnp.where(inside_lanes(lane, lanes, total_y, slot), COURANT, 0.0).astype(F32)
    start = lax.axis_index("gx") * cells_x - halo
    for i in range(cells_x + 2 * halo):
        place = start + i
        gate[i] = jnp.where((place >= 0) & (place < total_x), held, 0.0)


def first_kernel(
    fields, materials, got_a, got_b, got_c, got_d, edge_a, edge_b, tables, moments,
    own, keep, curl, phase, send_a, send_b,
    state, gate, *, geo, total_x, total_y, count,
):
    depth, cells_x, lanes, halo, slot = geo
    odd_x = lax.axis_index("gx") % 2 == 1
    even_y = lax.axis_index("gy") % 2 == 0
    lane = lax.broadcasted_iota(jnp.int32, (depth, lanes), 1)
    all_lane = lax.broadcasted_iota(jnp.int32, (1, 2 * lanes), 1)
    inside_y = inside_lanes(all_lane, lanes, total_y, slot)
    start_x = lax.axis_index("gx") * cells_x - halo
    set_gate(gate, geo, total_x, total_y)

    def side(left, right, row):
        right = pltpu.roll(right, (-slot * row) % lanes, 1)
        left = pltpu.roll(left, (lanes - slot - slot * row) % lanes, 1)
        return jnp.where(lane < slot, right, jnp.where(lane >= lanes - slot, left, 0.0))

    def place(comp, i, main, more):
        if comp < 6:
            state[comp, i, :, 0:lanes] = main
            state[comp, i, :, lanes : 2 * lanes] = more
            return
        kind = jnp.concatenate((main, more), 1)
        row_in = (start_x + i >= 0) & (start_x + i < total_x)
        kept = jnp.zeros(kind.shape, F32)
        turned = jnp.zeros(kind.shape, F32)
        here = inside_y & row_in
        for material in range(tables.shape[1]):
            match = (kind == float(material)) & here
            kept = jnp.where(match, tables[0, material], kept)
            turned = jnp.where(match, tables[1, material], turned)
        keep[i] = kept
        curl[i] = turned

    base_a = jnp.where(odd_x, 0, cells_x + halo)
    base_b = jnp.where(odd_x, cells_x + halo, 0)
    from_a = jnp.where(odd_x, cells_x - halo, 0)
    from_b = jnp.where(odd_x, 0, cells_x - halo)
    for comp in range(7):
        c_pack, d_pack = got_c[comp], got_d[comp]
        left = jnp.where(even_y, d_pack, c_pack)
        right = jnp.where(even_y, c_pack, d_pack)
        for x in range(cells_x):
            if comp < 6:
                main = fields[comp, pl.ds(x, depth, stride=cells_x), :]
            else:
                main = materials[pl.ds(x, depth, stride=cells_x), :].astype(F32)
            place(comp, halo + x, main, side(left, right, x))
        for got, edge, base, origin in (
            (got_a, edge_a, base_a, from_a),
            (got_b, edge_b, base_b, from_b),
        ):
            c_pack, d_pack = edge[0, comp], edge[1, comp]
            left = jnp.where(even_y, d_pack, c_pack)
            right = jnp.where(even_y, c_pack, d_pack)
            for r in range(halo):
                place(comp, base + r, got[r, comp], side(left, right, origin + r))

    phase[...] = jnp.zeros(phase.shape, F32)
    run_steps(state, keep, curl, gate, phase, moments, 0, geo, count)

    for comp in range(6):
        own[comp] = state[comp, halo : halo + cells_x]
    width = lanes // cells_x
    for send, first in ((send_a, base_b), (send_b, base_a)):
        origin = jnp.where(first == 0, cells_x, halo)
        for comp in range(6):
            edges = jnp.zeros((depth, lanes), F32)
            for r in range(halo):
                send[r, comp] = state[comp, origin + r, :, 0:lanes]
                more = state[comp, origin + r, :, lanes : 2 * lanes]
                here = (lane >= width * r) & (lane < width * (r + 1))
                edges = jnp.where(here, pltpu.roll(more, (width * r + width // 2) % lanes, 1), edges)
            send[halo, comp] = edges


def second_kernel(
    own, keep, curl, phase_in, got_a, got_b, moments,
    final, phase,
    state, gate, *, geo, total_x, total_y, count,
):
    depth, cells_x, lanes, halo, _ = geo
    odd_x = lax.axis_index("gx") % 2 == 1
    lane = lax.broadcasted_iota(jnp.int32, (depth, lanes), 1)
    set_gate(gate, geo, total_x, total_y)
    base_a = jnp.where(odd_x, 0, cells_x + halo)
    base_b = jnp.where(odd_x, cells_x + halo, 0)
    width = lanes // cells_x
    half = width // 2
    edge = (lane < half) | (lane >= lanes - half)
    for comp in range(6):
        state[comp, halo : halo + cells_x] = own[comp]
        for got, base in ((got_a, base_a), (got_b, base_b)):
            pack = got[halo, comp]
            for r in range(halo):
                state[comp, base + r, :, 0:lanes] = got[r, comp]
                more = pltpu.roll(pack, (-(width * r + half)) % lanes, 1)
                state[comp, base + r, :, lanes : 2 * lanes] = jnp.where(edge, more, 0.0)
    phase[...] = phase_in[...]
    run_steps(state, keep, curl, gate, phase, moments, count, geo, count)
    for comp in range(6):
        for x in range(cells_x):
            final[comp, pl.ds(x, depth, stride=cells_x), :] = state[comp, halo + x, :, 0:lanes]


def along_y_kernel(*refs, count):
    pieces, (table, fields, part, kept, done) = refs[:count], refs[count:]
    keeping = pltpu.make_async_copy(fields, kept, done)
    keeping.start()
    me = lax.axis_index("gy")
    total = None
    for back, piece in enumerate(pieces):
        origin = (me - back + count) % count
        term = jnp.dot(piece[...], table[origin], precision=PRECISE, preferred_element_type=F32)
        total = term if total is None else total + term
    rows, width = total.shape[0] // 2, total.shape[1] // 2
    re_cos, re_sin = total[:rows, :width], total[:rows, width:]
    im_cos, im_sin = total[rows:, :width], total[rows:, width:]
    part[:, 0:width] = re_cos + im_sin
    part[:, width : 2 * width] = im_cos - re_sin
    keeping.wait()


def image_kernel(*refs, tiles_x, tiles_y, cells_x, scaling, sources_all):
    parts, refs = refs[:tiles_x], refs[tiles_x:]
    packs, refs = refs[:tiles_y], refs[tiles_y:]
    table_x, g_matrix, row_table, shifts, weights = refs[:5]
    strips, refs = refs[5 : 5 + tiles_x], refs[5 + tiles_x :]
    gathered, orders, columns, rows, total = refs
    me_x = lax.axis_index("gx")
    me_y = lax.axis_index("gy")
    width = orders.shape[2]
    reach = orders.shape[1]
    for back, part in enumerate(parts):
        origin = pl.multiple_of((me_x - back + tiles_x) % tiles_x * cells_x, cells_x)
        for comp in range(2):
            gathered[comp, pl.ds(origin, cells_x), :] = part[comp * cells_x : (comp + 1) * cells_x, :]
    for comp in range(2):
        re, im = gathered[comp, :, 0:width], gathered[comp, :, width : 2 * width]
        dot = functools.partial(jnp.dot, precision=PRECISE, preferred_element_type=F32)
        cos_x, sin_x = table_x[0:reach, :], table_x[reach : 2 * reach, :]
        order_re = dot(cos_x, re) + dot(sin_x, im)
        order_im = dot(cos_x, im) - dot(sin_x, re)
        orders[2 * comp] = (order_re * scaling).astype(BF16).astype(F32)
        orders[2 * comp + 1] = (order_im * scaling).astype(BF16).astype(F32)
    strip = row_table.shape[1]
    for ahead in range(tiles_x):
        owner = (me_x + ahead) % tiles_x * tiles_y + me_y
        rows[strip * ahead : strip * (ahead + 1), :] = row_table[owner]
    pixels = g_matrix.shape[1] // 2
    orders_p = rows.shape[1] // 2
    local = packs[0].shape[0]
    total[...] = jnp.zeros(total.shape, F32)
    for at, pack in enumerate(packs):

        def source(index, carry, at=at, pack=pack):
            number = at * local + index
            down = shifts[number, 0] + REACH
            across = width - (shifts[number, 1] + REACH)
            passed = pack[index, 0:orders_p, :]
            masked = []
            for plane in range(4):
                window = orders[plane, pl.ds(down, orders_p), :]
                masked.append((pltpu.roll(window, across, 1) * passed).astype(BF16))
            halves = jnp.concatenate(
                (jnp.concatenate(masked[:2], 1), jnp.concatenate(masked[2:], 1)), 0
            )
            spread = jnp.dot(halves, g_matrix[...], preferred_element_type=F32).astype(BF16)
            for comp in range(2):
                part = spread[comp * orders_p : (comp + 1) * orders_p]
                real, imag = part[:, :pixels], part[:, pixels:]
                low = 2 * comp * pixels
                columns[0:orders_p, low : low + pixels] = real
                columns[0:orders_p, low + pixels : low + 2 * pixels] = imag
                columns[orders_p : 2 * orders_p, low : low + pixels] = -imag
                columns[orders_p : 2 * orders_p, low + pixels : low + 2 * pixels] = real
            bright = None
            for block in range(4):
                value = jnp.dot(
                    rows[...],
                    columns[:, block * pixels : (block + 1) * pixels],
                    preferred_element_type=F32,
                )
                bright = value * value if bright is None else bright + value * value
            total[...] = total[...] + (weights[number] / sources_all) * bright
            return carry

        lax.fori_loop(0, local, source, 0)
    for ahead in range(tiles_x):
        strips[ahead][...] = total[strip * ahead : strip * (ahead + 1), :]


def body(
    fields, material_map, material_eps, material_loss, source_shift, source_mask, source_weight
):
    tiles_x = lax.axis_size("gx")
    tiles_y = lax.axis_size("gy")
    _, depth, cells_x, lanes = fields.shape
    total_x, total_y = cells_x * tiles_x, lanes * tiles_y
    count = STEPS // ROUNDS
    halo = count
    slot = lanes // cells_x
    assert halo <= cells_x and slot >= STEPS and slot // 2 >= halo
    geo = (depth, cells_x, lanes, halo, slot)
    flat_fields = fields.reshape(6, depth * cells_x, lanes)
    flat_map = material_map.reshape(depth * cells_x, lanes)
    local, orders_p, orders_q = source_mask.shape
    wide = 128

    keep_table = (1.0 - material_loss) / (1.0 + material_loss)
    curl_table = COURANT / (material_eps * (1.0 + material_loss))
    tables = jnp.stack((keep_table, curl_table))
    angle = np.float32(ANGULAR) * np.arange(1, STEPS + 1, dtype=np.float32)
    moments = jnp.asarray(np.stack((np.cos(angle), np.sin(angle)), 1).astype(np.float32))

    row_shape = shape(halo, 7, depth, lanes)
    edge_shape = shape(7, depth, lanes)
    to_a, to_b, to_c, to_d, my_pack = call(
        functools.partial(pack_kernel, geo=geo),
        [(flat_fields, "h"), (flat_map, "h"), (source_shift.T, "s"), (source_weight, "s"), (source_mask, "h")],
        [row_shape, row_shape, edge_shape, edge_shape, shape(local, orders_p + 8, wide)],
        [pltpu.VMEM((cells_x, 7, depth, lanes), F32)],
    )
    got_c = swap(to_c, "gy", 0)
    got_d = swap(to_d, "gy", 1)
    got_a = swap(to_a, "gx", 0)
    got_b = swap(to_b, "gx", 1)
    edges = jnp.stack((got_c, got_d))
    edge_a = swap(edges, "gx", 0)
    edge_b = swap(edges, "gx", 1)
    packs = [my_pack]
    for by in range(1, tiles_y):
        packs.append(cyclic(my_pack, "gy", by))

    span = cells_x + 2 * halo
    state = pltpu.VMEM((6, span, depth, 2 * lanes), F32)
    gate = pltpu.VMEM((span, 1, 2 * lanes), F32)
    coef_shape = shape(span, depth, 2 * lanes)
    phase_shape = shape(4 * cells_x, lanes)
    send_shape = shape(halo + 1, 6, depth, lanes)
    own, keep, curl, phase, to_a, to_b = call(
        functools.partial(first_kernel, geo=geo, total_x=total_x, total_y=total_y, count=count),
        [(flat_fields, "h"), (flat_map, "h"), (got_a, "v"), (got_b, "v"), (got_c, "v"), (got_d, "v"),
         (edge_a, "v"), (edge_b, "v"), (tables, "s"), (moments, "s")],
        [shape(6, cells_x, depth, 2 * lanes), coef_shape, coef_shape, phase_shape, send_shape, send_shape],
        [state, gate],
    )
    got_a = swap(to_a, "gx", 0)
    got_b = swap(to_b, "gx", 1)
    final, phase = call(
        functools.partial(second_kernel, geo=geo, total_x=total_x, total_y=total_y, count=count),
        [(own, "v"), (keep, "v"), (curl, "v"), (phase, "v"), (got_a, "v"), (got_b, "v"), (moments, "s")],
        [shape(6, depth * cells_x, lanes), phase_shape],
        [state, gate],
    )
    reach = orders_p + 2 * REACH
    ids_p = np.arange(-REACH, orders_p + REACH) % orders_p - orders_p // 2
    ids_q = np.arange(-REACH, orders_q + REACH) % orders_q - orders_q // 2
    cos_y, sin_y = waves(ids_q, np.arange(total_y), total_y)
    table_y = np.zeros((total_y, 2 * wide), np.float32)
    table_y[:, : len(ids_q)] = cos_y.T
    table_y[:, wide : wide + len(ids_q)] = sin_y.T
    cos_x, sin_x = waves(ids_p, np.arange(total_x), total_x)
    table_x = np.concatenate((cos_x, sin_x), 0).astype(np.float32)
    pixels = M
    cos_u, sin_u = waves(np.arange(orders_p) - orders_p // 2, np.arange(pixels), pixels)
    strip = pixels // (tiles_x * tiles_y)
    row_table = (np.concatenate((cos_u, sin_u), 0).T / math.sqrt(orders_p)).astype(np.float32)
    row_table = row_table.reshape(tiles_x * tiles_y, strip, 2 * orders_p).astype(jnp.bfloat16)
    cos_v, sin_v = waves(np.arange(orders_q) - orders_q // 2, np.arange(pixels), pixels)
    g_matrix = np.zeros((2 * wide, 2 * pixels), np.float32)
    g_matrix[:orders_q, :pixels] = cos_v / math.sqrt(orders_q)
    g_matrix[:orders_q, pixels:] = sin_v / math.sqrt(orders_q)
    g_matrix[wide : wide + orders_q, :pixels] = -sin_v / math.sqrt(orders_q)
    g_matrix[wide : wide + orders_q, pixels:] = cos_v / math.sqrt(orders_q)
    g_matrix = g_matrix.astype(jnp.bfloat16)

    pieces = [phase] + [cyclic(phase, "gy", by) for by in range(1, tiles_y)]
    part, final = call(
        functools.partial(along_y_kernel, count=tiles_y),
        [(piece, "v") for piece in pieces]
        + [(jnp.asarray(table_y.reshape(tiles_y, lanes, 2 * wide)), "h"), (final, "v")],
        [shape(2 * cells_x, 2 * wide), jax.ShapeDtypeStruct(final.shape, F32)],
        [pltpu.SemaphoreType.DMA],
    )
    parts = [part] + [cyclic(part, "gx", by) for by in range(1, tiles_x)]

    facts = jnp.concatenate([pack[:, orders_p, 0:3] for pack in packs], 0)
    shifts = facts[:, 0:2].astype(jnp.int32)
    weights = facts[:, 2]
    strips = call(
        functools.partial(
            image_kernel,
            tiles_x=tiles_x,
            tiles_y=tiles_y,
            cells_x=cells_x,
            scaling=1.0 / math.sqrt(total_x * total_y * STEPS),
            sources_all=local * tiles_x * tiles_y,
        ),
        [(piece, "v") for piece in parts]
        + [(pack, "v") for pack in packs]
        + [(jnp.asarray(table_x), "h"), (jnp.asarray(g_matrix), "h"), (jnp.asarray(row_table), "h"),
           (shifts, "s"), (weights, "s")],
        [shape(strip, pixels) for _ in range(tiles_x)],
        [
            pltpu.VMEM((2, total_x, 2 * wide), F32),
            pltpu.VMEM((4, reach, wide), F32),
            pltpu.VMEM((2 * orders_p, 4 * pixels), BF16),
            pltpu.VMEM((tiles_x * strip, 2 * orders_p), BF16),
            pltpu.VMEM((tiles_x * strip, pixels), F32),
        ],
    )
    image = strips[0]
    for by in range(1, tiles_x):
        image = image + cyclic(strips[by], "gx", by)
    return (final.reshape(fields.shape), image)


def solution(mesh):
    placed = (
        P("clips", None, "gx", "gy"),
        P("clips", "gx", "gy"),
        P(),
        P(),
        P(("gx", "gy"), None),
        P(("gx", "gy"), None, None),
        P(("gx", "gy")),
    )

    return jax.shard_map(
        body,
        mesh=mesh,
        in_specs=placed,
        out_specs=(P("clips", None, "gx", "gy"), P(("gx", "gy"), "clips")),
        check_vma=False,
    )
```

profile of v0, /device:TPU:0, one launch (start us, length us, event | category | flops | bytes accessed | tf_op | source)
XLA Modules:
  0.0 110.3 jit_solution(11700324196211205520)
XLA Ops:
  0.7 1.1 %copy-done = f32[6,32,8,128]{3,2,1,0:T(8,128)S(1)} copy-done((f32[6,32,8,128]{3,2,1,0:T(8,128)S(1)}, f32[6,32,8,128]{3,2,1,0:T(8,128)}, u32[]{:S(2)}) %copy-start) | copy-done | bytes 786456
  1.8 0.9 copy-done.1
  2.7 0.9 copy-done.5
  3.7 0.7 copy-done.8
  4.3 0.7 copy-done.9
  5.0 1.2 %shard_map.131 = (f32[6,7,32,128]{3,2,1,0:T(8,128)S(1)}, f32[6,7,32,128]{3,2,1,0:T(8,128)S(1)}, f32[7,32,128]{2,1,0:T(8,128)S(1)}, f32[7,32,128]{2,1,0:T(8,128)S(1)}, f32[4,104,128]{2,1,0:T(8,128)S(1)}) custom-call(f32[6,256,128]{2,1,0:T(8,128)S(1)} %bitcast.14, s32[256,128]{1,0:T(8,128)S(1)} %bitcast.16, s32[2,4]{1,0:T(2,128)S(1)} %bitcast.20, ...), custom_call_target="tpu_custom_call" | custom-call | tf_op jit(solution)/shard_map/pallas_call | solution.py:44
  6.7 0.7 collective-permute-start.1
  7.4 2.7 %collective-permute-start.2 = (f32[7,32,128]{2,1,0:T(8,128)S(1)}, f32[7,32,128]{2,1,0:T(8,128)S(1)}, u32[]{:S(2)}, u32[]{:S(2)}) collective-permute-start(f32[7,32,128]{2,1,0:T(8,128)S(1)} %get-tuple-element.23), channel_id=1, source_target_pairs={{0,1},{1,0},{2,3},{3,2},{4,5},{5,4},{6,7},{7,6},{8,9},{9,8},{10,11... | collective-permute-start | bytes 344072 | tf_op jit(solution)/shard_map/ppermute | solution.py:65
  10.1 0.7 collective-permute-start.3
  10.8 2.1 %collective-permute-done.2.got_c = f32[7,32,128]{2,1,0:T(8,128)S(1)} collective-permute-done((f32[7,32,128]{2,1,0:T(8,128)S(1)}, f32[7,32,128]{2,1,0:T(8,128)S(1)}, u32[]{:S(2)}, u32[]{:S(2)}) %collective-permute-start.2) | collective-permute-done | bytes 114720 | tf_op jit(solution)/shard_map/ppermute | solution.py:65
  12.9 2.2 %collective-permute-start.4 = (f32[2,7,32,128]{3,2,1,0:T(8,128)S(1)}, f32[2,7,32,128]{3,2,1,0:T(8,128)S(1)}, u32[]{:S(2)}, u32[]{:S(2)}) collective-permute-start(f32[2,7,32,128]{3,2,1,0:T(8,128)S(1)} %pad_maximum_fusion), channel_id=1, source_target_pairs={{0,4},{4,0},{8,12},{12,8},{1,5},{5,1},{9,13},{13,9},{2,6},{6,2},{1... | collective-permute-start | bytes 688136 | tf_op jit(solution)/shard_map/ppermute | solution.py:65
  15.1 0.7 collective-permute-start.5
  16.2 17.8 %shard_map.132 = (f32[6,8,32,256]{3,2,1,0:T(8,128)S(1)}, f32[20,32,256]{2,1,0:T(8,128)S(1)}, f32[20,32,256]{2,1,0:T(8,128)S(1)}, f32[32,128]{1,0:T(8,128)S(1)}, ...) custom-call(f32[6,256,128]{2,1,0:T(8,128)S(1)} %bitcast.15, s32[256,128]{1,0:T(8,128)S(1)} %bitcast.17, ...), custom_call_target="tpu_custom_call" | custom-call | tf_op jit(solution)/shard_map/pallas_call | solution.py:44
  34.0 6.3 %collective-permute-start.6 = (f32[7,6,32,128]{3,2,1,0:T(8,128)S(1)}, f32[7,6,32,128]{3,2,1,0:T(8,128)S(1)}, u32[]{:S(2)}, u32[]{:S(2)}) collective-permute-start(f32[7,6,32,128]{3,2,1,0:T(8,128)S(1)} %get-tuple-element.29), channel_id=1, source_target_pairs={{0,4},{4,0},{8,12},{12,8},{1,5},{5,1},{9,13},{13,9},{2,6},{6,2},{1... | collective-permute-start | bytes 2064392 | tf_op jit(solution)/shard_map/ppermute | solution.py:65
  40.3 0.7 collective-permute-start.7
  41.0 6.1 %collective-permute-start.15 = (f32[4,104,128]{2,1,0:T(8,128)S(1)}, f32[4,104,128]{2,1,0:T(8,128)S(1)}, u32[]{:S(2)}, u32[]{:S(2)}) collective-permute-start(f32[4,104,128]{2,1,0:T(8,128)S(1)} %get-tuple-element.35.refs_4_), channel_id=1, source_target_pairs={{0,2},{1,3},{2,0},{3,1},{4,6},{5,7},{6,4},{7,5},{8,10},{9,11},{10,... | collective-permute-start | bytes 638984 | tf_op jit(solution)/shard_map/ppermute | solution.py:70
  47.2 0.9 collective-permute-start.16
  48.1 1.1 %collective-permute-start.14 = (f32[4,104,128]{2,1,0:T(8,128)S(1)}, f32[4,104,128]{2,1,0:T(8,128)S(1)}, u32[]{:S(2)}, u32[]{:S(2)}) collective-permute-start(f32[4,104,128]{2,1,0:T(8,128)S(1)} %get-tuple-element.35.refs_4_), channel_id=1, source_target_pairs={{0,1},{1,2},{2,3},{3,0},{4,5},{5,6},{6,7},{7,4},{8,9},{9,10},{10,1... | collective-permute-start | bytes 638984 | tf_op jit(solution)/shard_map/ppermute | solution.py:70
  49.2 7.7 %collective-permute-done.15.refs_6_ = f32[4,104,128]{2,1,0:T(8,128)S(1)} collective-permute-done((f32[4,104,128]{2,1,0:T(8,128)S(1)}, f32[4,104,128]{2,1,0:T(8,128)S(1)}, u32[]{:S(2)}, u32[]{:S(2)}) %collective-permute-start.15) | collective-permute-done | bytes 213024 | tf_op jit(solution)/shard_map/ppermute | solution.py:70
  56.9 4.6 %collective-permute-done.14.refs_5_ = f32[4,104,128]{2,1,0:T(8,128)S(1)} collective-permute-done((f32[4,104,128]{2,1,0:T(8,128)S(1)}, f32[4,104,128]{2,1,0:T(8,128)S(1)}, u32[]{:S(2)}, u32[]{:S(2)}) %collective-permute-start.14) | collective-permute-done | bytes 213024 | tf_op jit(solution)/shard_map/ppermute | solution.py:70
  61.6 16.4 %shard_map.133 = (f32[6,256,128]{2,1,0:T(8,128)S(1)}, f32[32,128]{1,0:T(8,128)S(1)}) custom-call(f32[6,8,32,256]{3,2,1,0:T(8,128)S(1)} %get-tuple-element.25.own, f32[20,32,256]{2,1,0:T(8,128)S(1)} %get-tuple-element.26.keep, f32[20,32,256]{2,1,0:T(8,128)S(1)} %get-tuple-element.27.curl, f32[32,128]{1,0:T(8,128)S(1)} %get-tuple-element.28.phase_in, ...), custom_call_target="tpu_custom_call" | custom-call | tf_op jit(solution)/shard_map/pallas_call | solution.py:44
  78.0 5.1 %collective-permute-start.8 = (f32[32,128]{1,0:T(8,128)S(1)}, f32[32,128]{1,0:T(8,128)S(1)}, u32[]{:S(2)}, u32[]{:S(2)}) collective-permute-start(f32[32,128]{1,0:T(8,128)S(1)} %get-tuple-element.31.refs_0_), channel_id=1, source_target_pairs={{0,1},{1,2},{2,3},{3,0},{4,5},{5,6},{6,7},{7,4},{8,9},{9,10},{10,1... | collective-permute-start | bytes 49160 | tf_op jit(solution)/shard_map/ppermute | solution.py:70
  83.1 1.4 %collective-permute-start.9 = (f32[32,128]{1,0:T(8,128)S(1)}, f32[32,128]{1,0:T(8,128)S(1)}, u32[]{:S(2)}, u32[]{:S(2)}) collective-permute-start(f32[32,128]{1,0:T(8,128)S(1)} %get-tuple-element.31.refs_0_), channel_id=1, source_target_pairs={{0,2},{1,3},{2,0},{3,1},{4,6},{5,7},{6,4},{7,5},{8,10},{9,11},{10,... | collective-permute-start | bytes 49160 | tf_op jit(solution)/shard_map/ppermute | solution.py:70
  85.4 2.4 %collective-permute-done.9.refs_2_ = f32[32,128]{1,0:T(8,128)S(1)} collective-permute-done((f32[32,128]{1,0:T(8,128)S(1)}, f32[32,128]{1,0:T(8,128)S(1)}, u32[]{:S(2)}, u32[]{:S(2)}) %collective-permute-start.9) | collective-permute-done | bytes 16416 | tf_op jit(solution)/shard_map/ppermute | solution.py:70
  87.8 0.9 shard_map.134
  88.7 2.6 %collective-permute-start.12 = (f32[16,256]{1,0:T(8,128)S(1)}, f32[16,256]{1,0:T(8,128)S(1)}, u32[]{:S(2)}, u32[]{:S(2)}) collective-permute-start(f32[16,256]{1,0:T(8,128)S(1)} %get-tuple-element.34.refs_0_), channel_id=1, source_target_pairs={{0,8},{4,12},{8,0},{12,4},{1,9},{5,13},{9,1},{13,5},{2,10},{6,14},... | collective-permute-start | bytes 49160 | tf_op jit(solution)/shard_map/ppermute | solution.py:70
  91.3 1.4 %collective-permute-start.13 = (f32[16,256]{1,0:T(8,128)S(1)}, f32[16,256]{1,0:T(8,128)S(1)}, u32[]{:S(2)}, u32[]{:S(2)}) collective-permute-start(f32[16,256]{1,0:T(8,128)S(1)} %get-tuple-element.34.refs_0_), channel_id=1, source_target_pairs={{0,12},{4,0},{8,4},{12,8},{1,13},{5,1},{9,5},{13,9},{2,14},{6,2},{... | collective-permute-start | bytes 49160 | tf_op jit(solution)/shard_map/ppermute | solution.py:70
  93.0 1.1 %collective-permute-done.13.refs_3_ = f32[16,256]{1,0:T(8,128)S(1)} collective-permute-done((f32[16,256]{1,0:T(8,128)S(1)}, f32[16,256]{1,0:T(8,128)S(1)}, u32[]{:S(2)}, u32[]{:S(2)}) %collective-permute-start.13) | collective-permute-done | bytes 16416 | tf_op jit(solution)/shard_map/ppermute | solution.py:70
  94.1 10.4 %shard_map.135 = (f32[32,512]{1,0:T(8,128)S(1)}, f32[32,512]{1,0:T(8,128)S(1)}, f32[32,512]{1,0:T(8,128)S(1)}, f32[32,512]{1,0:T(8,128)S(1)}) custom-call(f32[16,256]{1,0:T(8,128)S(1)} %get-tuple-element.34.refs_0_, f32[16,256]{1,0:T(8,128)S(1)} %collective-permute-done.11.refs_1_, f32[16,256]{1,0:T(8,128)S(1)} %collective-permute-done.12.refs_2_, ...), custom_call_target="tpu_custom_call" | custom-call | tf_op jit(solution)/shard_map/pallas_call | solution.py:44
  104.9 1.7 %collective-permute-start.18 = (f32[32,512]{1,0:T(8,128)S(1)}, f32[32,512]{1,0:T(8,128)S(1)}, u32[]{:S(2)}, u32[]{:S(2)}) collective-permute-start(f32[32,512]{1,0:T(8,128)S(1)} %get-tuple-element.38), channel_id=1, source_target_pairs={{0,8},{4,12},{8,0},{12,4},{1,9},{5,13},{9,1},{13,5},{2,10},{6,14},... | collective-permute-start | bytes 196616 | tf_op jit(solution)/shard_map/ppermute | solution.py:70
  107.0 1.3 %collective-permute-done.17 = f32[32,512]{1,0:T(8,128)S(1)} collective-permute-done((f32[32,512]{1,0:T(8,128)S(1)}, f32[32,512]{1,0:T(8,128)S(1)}, u32[]{:S(2)}, u32[]{:S(2)}) %collective-permute-start.17) | collective-permute-done | bytes 65568 | tf_op jit(solution)/shard_map/ppermute | solution.py:70
  108.3 1.4 %collective-permute-done.18 = f32[32,512]{1,0:T(8,128)S(1)} collective-permute-done((f32[32,512]{1,0:T(8,128)S(1)}, f32[32,512]{1,0:T(8,128)S(1)}, u32[]{:S(2)}, u32[]{:S(2)}) %collective-permute-start.18) | collective-permute-done | bytes 65568 | tf_op jit(solution)/shard_map/ppermute | solution.py:70
  (48 shorter events, 3.7 us)
Async XLA Ops:
  0.6 15.6 %copy-start.7 = (f32[12,2]{1,0:T(8,128)S(1)}, f32[12,2]{1,0:T(8,128)}, u32[]{:S(2)}) copy-start(f32[12,2]{1,0:T(8,128)} %constant.14.clone.moments) | copy-start | bytes 292
  0.6 15.1 %copy-start.11 = (f32[4]{0:T(128)S(1)}, f32[4]{0:T(128)}, u32[]{:S(2)}) copy-start(f32[4]{0:T(128)} %param.14) | copy-start | bytes 52
  0.7 15.1 %copy-start.10 = (f32[4]{0:T(128)S(1)}, f32[4]{0:T(128)}, u32[]{:S(2)}) copy-start(f32[4]{0:T(128)} %param.15) | copy-start | bytes 52
  0.7 1.2 %copy-start = (f32[6,32,8,128]{3,2,1,0:T(8,128)S(1)}, f32[6,32,8,128]{3,2,1,0:T(8,128)}, u32[]{:S(2)}) copy-start(f32[6,32,8,128]{3,2,1,0:T(8,128)} %param.12) | copy-start | bytes 2359300
  1.8 0.9 copy-start.1
  2.7 0.9 copy-start.5
  3.6 0.7 copy-start.8
  4.3 0.7 copy-start.9
  6.2 10.0 %collective-permute-start = (f32[6,7,32,128]{3,2,1,0:T(8,128)S(1)}, f32[6,7,32,128]{3,2,1,0:T(8,128)S(1)}, u32[]{:S(2)}, u32[]{:S(2)}) collective-permute-start(f32[6,7,32,128]{3,2,1,0:T(8,128)S(1)} %get-tuple-element.21), channel_id=1, source_target_pairs={{0,4},{4,0},{8,12},{12,8},{1,5},{5,1},{9,13},{13,9},{2,6},{6,2},{1... | collective-permute-start | bytes 2064392 | tf_op jit(solution)/shard_map/ppermute | solution.py:65
  6.7 9.5 %collective-permute-start.1 = (f32[6,7,32,128]{3,2,1,0:T(8,128)S(1)}, f32[6,7,32,128]{3,2,1,0:T(8,128)S(1)}, u32[]{:S(2)}, u32[]{:S(2)}) collective-permute-start(f32[6,7,32,128]{3,2,1,0:T(8,128)S(1)} %get-tuple-element.22), channel_id=1, source_target_pairs={{4,8},{8,4},{5,9},{9,5},{6,10},{10,6},{7,11},{11,7},{20,24},{24,20... | collective-permute-start | bytes 2064392 | tf_op jit(solution)/shard_map/ppermute | solution.py:65
  7.4 5.4 %collective-permute-start.2 = (f32[7,32,128]{2,1,0:T(8,128)S(1)}, f32[7,32,128]{2,1,0:T(8,128)S(1)}, u32[]{:S(2)}, u32[]{:S(2)}) collective-permute-start(f32[7,32,128]{2,1,0:T(8,128)S(1)} %get-tuple-element.23), channel_id=1, source_target_pairs={{0,1},{1,0},{2,3},{3,2},{4,5},{5,4},{6,7},{7,6},{8,9},{9,8},{10,11... | collective-permute-start | bytes 344072 | tf_op jit(solution)/shard_map/ppermute | solution.py:65
  10.1 2.8 %collective-permute-start.3 = (f32[7,32,128]{2,1,0:T(8,128)S(1)}, f32[7,32,128]{2,1,0:T(8,128)S(1)}, u32[]{:S(2)}, u32[]{:S(2)}) collective-permute-start(f32[7,32,128]{2,1,0:T(8,128)S(1)} %get-tuple-element.24), channel_id=1, source_target_pairs={{1,2},{2,1},{5,6},{6,5},{9,10},{10,9},{13,14},{14,13},{17,18},{18,... | collective-permute-start | bytes 344072 | tf_op jit(solution)/shard_map/ppermute | solution.py:65
  12.9 3.3 %collective-permute-start.4 = (f32[2,7,32,128]{3,2,1,0:T(8,128)S(1)}, f32[2,7,32,128]{3,2,1,0:T(8,128)S(1)}, u32[]{:S(2)}, u32[]{:S(2)}) collective-permute-start(f32[2,7,32,128]{3,2,1,0:T(8,128)S(1)} %pad_maximum_fusion), channel_id=1, source_target_pairs={{0,4},{4,0},{8,12},{12,8},{1,5},{5,1},{9,13},{13,9},{2,6},{6,2},{1... | collective-permute-start | bytes 688136 | tf_op jit(solution)/shard_map/ppermute | solution.py:65
  15.1 1.1 %collective-permute-start.5 = (f32[2,7,32,128]{3,2,1,0:T(8,128)S(1)}, f32[2,7,32,128]{3,2,1,0:T(8,128)S(1)}, u32[]{:S(2)}, u32[]{:S(2)}) collective-permute-start(f32[2,7,32,128]{3,2,1,0:T(8,128)S(1)} %pad_maximum_fusion), channel_id=1, source_target_pairs={{4,8},{8,4},{5,9},{9,5},{6,10},{10,6},{7,11},{11,7},{20,24},{24,20... | collective-permute-start | bytes 688136 | tf_op jit(solution)/shard_map/ppermute | solution.py:65
  34.0 27.5 %collective-permute-start.6 = (f32[7,6,32,128]{3,2,1,0:T(8,128)S(1)}, f32[7,6,32,128]{3,2,1,0:T(8,128)S(1)}, u32[]{:S(2)}, u32[]{:S(2)}) collective-permute-start(f32[7,6,32,128]{3,2,1,0:T(8,128)S(1)} %get-tuple-element.29), channel_id=1, source_target_pairs={{0,4},{4,0},{8,12},{12,8},{1,5},{5,1},{9,13},{13,9},{2,6},{6,2},{1... | collective-permute-start | bytes 2064392 | tf_op jit(solution)/shard_map/ppermute | solution.py:65
  40.3 21.2 %collective-permute-start.7 = (f32[7,6,32,128]{3,2,1,0:T(8,128)S(1)}, f32[7,6,32,128]{3,2,1,0:T(8,128)S(1)}, u32[]{:S(2)}, u32[]{:S(2)}) collective-permute-start(f32[7,6,32,128]{3,2,1,0:T(8,128)S(1)} %get-tuple-element.30), channel_id=1, source_target_pairs={{4,8},{8,4},{5,9},{9,5},{6,10},{10,6},{7,11},{11,7},{20,24},{24,20... | collective-permute-start | bytes 2064392 | tf_op jit(solution)/shard_map/ppermute | solution.py:65
  41.0 15.9 %collective-permute-start.15 = (f32[4,104,128]{2,1,0:T(8,128)S(1)}, f32[4,104,128]{2,1,0:T(8,128)S(1)}, u32[]{:S(2)}, u32[]{:S(2)}) collective-permute-start(f32[4,104,128]{2,1,0:T(8,128)S(1)} %get-tuple-element.35.refs_4_), channel_id=1, source_target_pairs={{0,2},{1,3},{2,0},{3,1},{4,6},{5,7},{6,4},{7,5},{8,10},{9,11},{10,... | collective-permute-start | bytes 638984 | tf_op jit(solution)/shard_map/ppermute | solution.py:70
  47.2 9.8 %collective-permute-start.16 = (f32[4,104,128]{2,1,0:T(8,128)S(1)}, f32[4,104,128]{2,1,0:T(8,128)S(1)}, u32[]{:S(2)}, u32[]{:S(2)}) collective-permute-start(f32[4,104,128]{2,1,0:T(8,128)S(1)} %get-tuple-element.35.refs_4_), channel_id=1, source_target_pairs={{0,3},{1,0},{2,1},{3,2},{4,7},{5,4},{6,5},{7,6},{8,11},{9,8},{10,9... | collective-permute-start | bytes 638984 | tf_op jit(solution)/shard_map/ppermute | solution.py:70
  48.1 13.4 %collective-permute-start.14 = (f32[4,104,128]{2,1,0:T(8,128)S(1)}, f32[4,104,128]{2,1,0:T(8,128)S(1)}, u32[]{:S(2)}, u32[]{:S(2)}) collective-permute-start(f32[4,104,128]{2,1,0:T(8,128)S(1)} %get-tuple-element.35.refs_4_), channel_id=1, source_target_pairs={{0,1},{1,2},{2,3},{3,0},{4,5},{5,6},{6,7},{7,4},{8,9},{9,10},{10,1... | collective-permute-start | bytes 638984 | tf_op jit(solution)/shard_map/ppermute | solution.py:70
  61.5 26.2 %copy-start.2 = (f32[4,128,256]{2,1,0:T(8,128)S(1)}, f32[4,128,256]{2,1,0:T(8,128)}, u32[]{:S(2)}) copy-start(f32[4,128,256]{2,1,0:T(8,128)} %constant.15.clone.refs_4_) | copy-start | bytes 1572868
  61.5 32.6 %copy-start.6 = (f32[224,32]{1,0:T(8,128)S(1)}, f32[224,32]{1,0:T(8,128)}, u32[]{:S(2)}) copy-start(f32[224,32]{1,0:T(8,128)} %constant.16.clone.refs_8_) | copy-start | bytes 86020
  77.9 16.2 %copy-start.3 = (bf16[256,1024]{1,0:T(8,128)(2,1)S(1)}, bf16[256,1024]{1,0:T(8,128)(2,1)}, u32[]{:S(2)}) copy-start(bf16[256,1024]{1,0:T(8,128)(2,1)} %constant.17.clone.refs_9_) | copy-start | bytes 1572868
  78.0 16.2 %copy-start.4 = (bf16[16,32,192]{2,1,0:T(8,128)(2,1)S(1)}, bf16[16,32,192]{2,1,0:T(8,128)(2,1)}, u32[]{:S(2)}) copy-start(bf16[16,32,192]{2,1,0:T(8,128)(2,1)} %constant.18.clone.refs_10_) | copy-start | bytes 589828
  78.0 6.8 %collective-permute-start.10 = (f32[32,128]{1,0:T(8,128)S(1)}, f32[32,128]{1,0:T(8,128)S(1)}, u32[]{:S(2)}, u32[]{:S(2)}) collective-permute-start(f32[32,128]{1,0:T(8,128)S(1)} %get-tuple-element.31.refs_0_), channel_id=1, source_target_pairs={{0,3},{1,0},{2,1},{3,2},{4,7},{5,4},{6,5},{7,6},{8,11},{9,8},{10,9... | collective-permute-start | bytes 49160 | tf_op jit(solution)/shard_map/ppermute | solution.py:70
  78.0 7.3 %collective-permute-start.8 = (f32[32,128]{1,0:T(8,128)S(1)}, f32[32,128]{1,0:T(8,128)S(1)}, u32[]{:S(2)}, u32[]{:S(2)}) collective-permute-start(f32[32,128]{1,0:T(8,128)S(1)} %get-tuple-element.31.refs_0_), channel_id=1, source_target_pairs={{0,1},{1,2},{2,3},{3,0},{4,5},{5,6},{6,7},{7,4},{8,9},{9,10},{10,1... | collective-permute-start | bytes 49160 | tf_op jit(solution)/shard_map/ppermute | solution.py:70
  83.1 4.6 %collective-permute-start.9 = (f32[32,128]{1,0:T(8,128)S(1)}, f32[32,128]{1,0:T(8,128)S(1)}, u32[]{:S(2)}, u32[]{:S(2)}) collective-permute-start(f32[32,128]{1,0:T(8,128)S(1)} %get-tuple-element.31.refs_0_), channel_id=1, source_target_pairs={{0,2},{1,3},{2,0},{3,1},{4,6},{5,7},{6,4},{7,5},{8,10},{9,11},{10,... | collective-permute-start | bytes 49160 | tf_op jit(solution)/shard_map/ppermute | solution.py:70
  88.7 4.2 %collective-permute-start.11 = (f32[16,256]{1,0:T(8,128)S(1)}, f32[16,256]{1,0:T(8,128)S(1)}, u32[]{:S(2)}, u32[]{:S(2)}) collective-permute-start(f32[16,256]{1,0:T(8,128)S(1)} %get-tuple-element.34.refs_0_), channel_id=1, source_target_pairs={{0,4},{4,8},{8,12},{12,0},{1,5},{5,9},{9,13},{13,1},{2,6},{6,10},{... | collective-permute-start | bytes 49160 | tf_op jit(solution)/shard_map/ppermute | solution.py:70
  88.7 4.3 %collective-permute-start.12 = (f32[16,256]{1,0:T(8,128)S(1)}, f32[16,256]{1,0:T(8,128)S(1)}, u32[]{:S(2)}, u32[]{:S(2)}) collective-permute-start(f32[16,256]{1,0:T(8,128)S(1)} %get-tuple-element.34.refs_0_), channel_id=1, source_target_pairs={{0,8},{4,12},{8,0},{12,4},{1,9},{5,13},{9,1},{13,5},{2,10},{6,14},... | collective-permute-start | bytes 49160 | tf_op jit(solution)/shard_map/ppermute | solution.py:70
  91.3 2.8 %collective-permute-start.13 = (f32[16,256]{1,0:T(8,128)S(1)}, f32[16,256]{1,0:T(8,128)S(1)}, u32[]{:S(2)}, u32[]{:S(2)}) collective-permute-start(f32[16,256]{1,0:T(8,128)S(1)} %get-tuple-element.34.refs_0_), channel_id=1, source_target_pairs={{0,12},{4,0},{8,4},{12,8},{1,13},{5,1},{9,5},{13,9},{2,14},{6,2},{... | collective-permute-start | bytes 49160 | tf_op jit(solution)/shard_map/ppermute | solution.py:70
  104.5 3.7 %collective-permute-start.17 = (f32[32,512]{1,0:T(8,128)S(1)}, f32[32,512]{1,0:T(8,128)S(1)}, u32[]{:S(2)}, u32[]{:S(2)}) collective-permute-start(f32[32,512]{1,0:T(8,128)S(1)} %get-tuple-element.37), channel_id=1, source_target_pairs={{0,4},{4,8},{8,12},{12,0},{1,5},{5,9},{9,13},{13,1},{2,6},{6,10},{... | collective-permute-start | bytes 196616 | tf_op jit(solution)/shard_map/ppermute | solution.py:70
  104.9 4.7 %collective-permute-start.18 = (f32[32,512]{1,0:T(8,128)S(1)}, f32[32,512]{1,0:T(8,128)S(1)}, u32[]{:S(2)}, u32[]{:S(2)}) collective-permute-start(f32[32,512]{1,0:T(8,128)S(1)} %get-tuple-element.38), channel_id=1, source_target_pairs={{0,8},{4,12},{8,0},{12,4},{1,9},{5,13},{9,1},{13,5},{2,10},{6,14},... | collective-permute-start | bytes 196616 | tf_op jit(solution)/shard_map/ppermute | solution.py:70
  106.7 3.0 %collective-permute-start.19 = (f32[32,512]{1,0:T(8,128)S(1)}, f32[32,512]{1,0:T(8,128)S(1)}, u32[]{:S(2)}, u32[]{:S(2)}) collective-permute-start(f32[32,512]{1,0:T(8,128)S(1)} %get-tuple-element.39), channel_id=1, source_target_pairs={{0,12},{4,0},{8,4},{12,8},{1,13},{5,1},{9,5},{13,9},{2,14},{6,2},{... | collective-permute-start | bytes 196616 | tf_op jit(solution)/shard_map/ppermute | solution.py:70
where the time goes:
time: 111 us; the launch traced here: 110 us
  Pallas kernels  46.7 us (42%)
  starting transfers between devices  35.5 us (32%)
  waiting for transfers between devices  22 us (20%)
  local copies, waits for them, and re-layouts  4.54 us (4%)
    pallas_call x5, Pallas kernels, call(): pl.pallas_call(kernel, out_shape=outs, in_specs=[spaces[space]() for _, s...  46.7 us
    ppermute x12, starting transfers between devices, cyclic(): lax.ppermute(values, axis, [(i, (i + by) % count) for i in range(count)])  21.1 us
    ppermute x12, waiting for transfers between devices, cyclic(): lax.ppermute(values, axis, [(i, (i + by) % count) for i in range(count)])  19.5 us
    ppermute x8, starting transfers between devices, swap(): return lax.ppermute(values, axis, pairs)  14.4 us
    unnamed x24, local copies, waits for them, and re-layouts  4.35 us
    ppermute x8, waiting for transfers between devices, swap(): return lax.ppermute(values, axis, pairs)  2.52 us
  transfers between devices with their start and end apart: 20, of which 11 were waited for; matrix products, arithmetic and copies ran while one was open for 0% of the time, Pallas kernels for 0%

commit v1 on v0

--- a/solution.py
+++ b/solution.py
@@ -31,14 +31,19 @@
     return pl.BlockSpec(memory_space=pltpu.SMEM)
 
 
+def hbm():
+    return pl.BlockSpec(memory_space=pltpu.HBM)
+
+
 def call(kernel, ins, outs, scratch=(), limit=16):
-    spaces = {"h": vmem, "v": vmem, "s": smem}
+    spaces = {"h": hbm, "c": vmem, "v": vmem, "s": smem}
+    memories = {"h": pltpu.HBM, "v": pltpu.VMEM}
 
     def out_spec(out):
         return vmem() if not isinstance(out, jax.ShapeDtypeStruct) else pl.BlockSpec(memory_space=pl.ANY)
 
     held = [
-        pltpu.with_memory_space_constraint(array, pltpu.VMEM) if space == "v" else array
+        pltpu.with_memory_space_constraint(array, memories[space]) if space in memories else array
         for array, space in ins
     ]
     return pl.pallas_call(
@@ -77,8 +82,19 @@
 
 
 def pack_kernel(
-    fields, materials, shifts, weights, masks, send_a, send_b, send_c, send_d, source_pack, rows, *, geo
+    far_fields, far_map, shifts, weights, far_masks,
+    fields, materials, send_a, send_b, send_c, send_d, source_pack,
+    rows, masks, arrived, *, geo,
 ):
+    copies = [
+        pltpu.make_async_copy(far_fields, fields, arrived.at[0]),
+        pltpu.make_async_copy(far_map, materials, arrived.at[1]),
+        pltpu.make_async_copy(far_masks, masks, arrived.at[2]),
+    ]
+    for copy in copies:
+        copy.start()
+    for copy in copies:
+        copy.wait()
     depth, cells_x, lanes, halo, slot = geo
     even_x = lax.axis_index("gx") % 2 == 0
     even_y = lax.axis_index("gy") % 2 == 0
@@ -396,11 +412,16 @@
 
     row_shape = shape(halo, 7, depth, lanes)
     edge_shape = shape(7, depth, lanes)
-    to_a, to_b, to_c, to_d, my_pack = call(
+    near_fields, near_map, to_a, to_b, to_c, to_d, my_pack = call(
         functools.partial(pack_kernel, geo=geo),
         [(flat_fields, "h"), (flat_map, "h"), (source_shift.T, "s"), (source_weight, "s"), (source_mask, "h")],
-        [row_shape, row_shape, edge_shape, edge_shape, shape(local, orders_p + 8, wide)],
-        [pltpu.VMEM((cells_x, 7, depth, lanes), F32)],
+        [shape(*flat_fields.shape), shape(*flat_map.shape, dtype=jnp.int32)]
+        + [row_shape, row_shape, edge_shape, edge_shape, shape(local, orders_p + 8, wide)],
+        [
+            pltpu.VMEM((cells_x, 7, depth, lanes), F32),
+            pltpu.VMEM(source_mask.shape, jnp.int32),
+            pltpu.SemaphoreType.DMA((3,)),
+        ],
     )
     got_c = swap(to_c, "gy", 0)
     got_d = swap(to_d, "gy", 1)
@@ -421,7 +442,7 @@
     send_shape = shape(halo + 1, 6, depth, lanes)
     own, keep, curl, phase, to_a, to_b = call(
         functools.partial(first_kernel, geo=geo, total_x=total_x, total_y=total_y, count=count),
-        [(flat_fields, "h"), (flat_map, "h"), (got_a, "v"), (got_b, "v"), (got_c, "v"), (got_d, "v"),
+        [(near_fields, "v"), (near_map, "v"), (got_a, "v"), (got_b, "v"), (got_c, "v"), (got_d, "v"),
          (edge_a, "v"), (edge_b, "v"), (tables, "s"), (moments, "s")],
         [shape(6, cells_x, depth, 2 * lanes), coef_shape, coef_shape, phase_shape, send_shape, send_shape],
         [state, gate],
@@ -460,7 +481,7 @@
     part, final = call(
         functools.partial(along_y_kernel, count=tiles_y),
         [(piece, "v") for piece in pieces]
-        + [(jnp.asarray(table_y.reshape(tiles_y, lanes, 2 * wide)), "h"), (final, "v")],
+        + [(jnp.asarray(table_y.reshape(tiles_y, lanes, 2 * wide)), "c"), (final, "v")],
         [shape(2 * cells_x, 2 * wide), jax.ShapeDtypeStruct(final.shape, F32)],
         [pltpu.SemaphoreType.DMA],
     )
@@ -480,7 +501,7 @@
         ),
         [(piece, "v") for piece in parts]
         + [(pack, "v") for pack in packs]
-        + [(jnp.asarray(table_x), "h"), (jnp.asarray(g_matrix), "h"), (jnp.asarray(row_table), "h"),
+        + [(jnp.asarray(table_x), "c"), (jnp.asarray(g_matrix), "c"), (jnp.asarray(row_table), "c"),
            (shifts, "s"), (weights, "s")],
         [shape(strip, pixels) for _ in range(tiles_x)],
         [

time: 111 us -> 109 us (0.982)
  local copies, waits for them, and re-layouts: 4.54 us -> 1.58 us
  Pallas kernels: 46.7 us -> 47.9 us
    unnamed x24 -> x18, local copies, waits for them, and re-layouts: 4.35 us -> 1.39 us
    pallas_call x5, Pallas kernels: 46.7 us -> 47.9 us  [call(): pl.pallas_call(kernel, out_shape=outs, in_specs=[spaces[space]() for _, s...]
where the time goes in v1:
time: 109 us
  Pallas kernels  47.9 us (44%)
  starting transfers between devices  35.5 us (33%)
  waiting for transfers between devices  22 us (20%)
  local copies, waits for them, and re-layouts  1.58 us (1%)
    pallas_call x5, Pallas kernels, call(): pl.pallas_call(kernel, out_shape=outs, in_specs=[spaces[space]() for _, s...  47.9 us
    ppermute x12, starting transfers between devices, cyclic(): lax.ppermute(values, axis, [(i, (i + by) % count) for i in range(count)])  21.1 us
    ppermute x12, waiting for transfers between devices, cyclic(): lax.ppermute(values, axis, [(i, (i + by) % count) for i in range(count)])  19.5 us
    ppermute x8, starting transfers between devices, swap(): return lax.ppermute(values, axis, pairs)  14.4 us
    ppermute x8, waiting for transfers between devices, swap(): return lax.ppermute(values, axis, pairs)  2.52 us
  transfers between devices with their start and end apart: 20, of which 11 were waited for; matrix products, arithmetic and copies ran while one was open for 0% of the time, Pallas kernels for 0%

profile of v1, /device:TPU:0, one launch (start us, length us, event | category | flops | bytes accessed | tf_op | source)
XLA Modules:
  0.0 108.6 jit_solution(11675465039285286634)
XLA Ops:
  0.7 0.7 copy-done.5
  1.4 0.7 copy-done.6
  2.0 2.4 %shard_map.131 = (f32[6,256,128]{2,1,0:T(8,128)S(1)}, s32[256,128]{1,0:T(8,128)S(1)}, f32[6,7,32,128]{3,2,1,0:T(8,128)S(1)}, f32[6,7,32,128]{3,2,1,0:T(8,128)S(1...) custom-call(f32[6,256,128]{2,1,0:T(8,128)} %bitcast.17, s32[256,128]{1,0:T(8,128)} %bitcast.18, ...), custom_call_target="tpu_custom_call" | custom-call | tf_op jit(solution)/shard_map/pallas_call | solution.py:49
  4.5 0.5 collective-permute-start
  5.0 0.7 collective-permute-start.1
  5.7 2.7 %collective-permute-start.2 = (f32[7,32,128]{2,1,0:T(8,128)S(1)}, f32[7,32,128]{2,1,0:T(8,128)S(1)}, u32[]{:S(2)}, u32[]{:S(2)}) collective-permute-start(f32[7,32,128]{2,1,0:T(8,128)S(1)} %get-tuple-element.27), channel_id=1, source_target_pairs={{0,1},{1,0},{2,3},{3,2},{4,5},{5,4},{6,7},{7,6},{8,9},{9,8},{10,11... | collective-permute-start | bytes 344072 | tf_op jit(solution)/shard_map/ppermute | solution.py:70
  8.4 0.7 collective-permute-start.3
  9.0 2.1 %collective-permute-done.2.got_c = f32[7,32,128]{2,1,0:T(8,128)S(1)} collective-permute-done((f32[7,32,128]{2,1,0:T(8,128)S(1)}, f32[7,32,128]{2,1,0:T(8,128)S(1)}, u32[]{:S(2)}, u32[]{:S(2)}) %collective-permute-start.2) | collective-permute-done | bytes 114720 | tf_op jit(solution)/shard_map/ppermute | solution.py:70
  11.2 2.2 %collective-permute-start.4 = (f32[2,7,32,128]{3,2,1,0:T(8,128)S(1)}, f32[2,7,32,128]{3,2,1,0:T(8,128)S(1)}, u32[]{:S(2)}, u32[]{:S(2)}) collective-permute-start(f32[2,7,32,128]{3,2,1,0:T(8,128)S(1)} %pad_maximum_fusion), channel_id=1, source_target_pairs={{0,4},{4,0},{8,12},{12,8},{1,5},{5,1},{9,13},{13,9},{2,6},{6,2},{1... | collective-permute-start | bytes 688136 | tf_op jit(solution)/shard_map/ppermute | solution.py:70
  13.4 0.7 collective-permute-start.5
  14.5 17.8 %shard_map.132 = (f32[6,8,32,256]{3,2,1,0:T(8,128)S(1)}, f32[20,32,256]{2,1,0:T(8,128)S(1)}, f32[20,32,256]{2,1,0:T(8,128)S(1)}, f32[32,128]{1,0:T(8,128)S(1)}, ...) custom-call(f32[6,256,128]{2,1,0:T(8,128)S(1)} %get-tuple-element.23.fields, ...), custom_call_target="tpu_custom_call" | custom-call | tf_op jit(solution)/shard_map/pallas_call | solution.py:49
  32.3 6.3 %collective-permute-start.6 = (f32[7,6,32,128]{3,2,1,0:T(8,128)S(1)}, f32[7,6,32,128]{3,2,1,0:T(8,128)S(1)}, u32[]{:S(2)}, u32[]{:S(2)}) collective-permute-start(f32[7,6,32,128]{3,2,1,0:T(8,128)S(1)} %get-tuple-element.33), channel_id=1, source_target_pairs={{0,4},{4,0},{8,12},{12,8},{1,5},{5,1},{9,13},{13,9},{2,6},{6,2},{1... | collective-permute-start | bytes 2064392 | tf_op jit(solution)/shard_map/ppermute | solution.py:70
  38.6 0.7 collective-permute-start.7
  39.3 6.1 %collective-permute-start.15 = (f32[4,104,128]{2,1,0:T(8,128)S(1)}, f32[4,104,128]{2,1,0:T(8,128)S(1)}, u32[]{:S(2)}, u32[]{:S(2)}) collective-permute-start(f32[4,104,128]{2,1,0:T(8,128)S(1)} %get-tuple-element.39.refs_4_), channel_id=1, source_target_pairs={{0,2},{1,3},{2,0},{3,1},{4,6},{5,7},{6,4},{7,5},{8,10},{9,11},{10,... | collective-permute-start | bytes 638984 | tf_op jit(solution)/shard_map/ppermute | solution.py:75
  45.4 0.9 collective-permute-start.16
  46.3 1.1 %collective-permute-start.14 = (f32[4,104,128]{2,1,0:T(8,128)S(1)}, f32[4,104,128]{2,1,0:T(8,128)S(1)}, u32[]{:S(2)}, u32[]{:S(2)}) collective-permute-start(f32[4,104,128]{2,1,0:T(8,128)S(1)} %get-tuple-element.39.refs_4_), channel_id=1, source_target_pairs={{0,1},{1,2},{2,3},{3,0},{4,5},{5,6},{6,7},{7,4},{8,9},{9,10},{10,1... | collective-permute-start | bytes 638984 | tf_op jit(solution)/shard_map/ppermute | solution.py:75
  47.5 7.7 %collective-permute-done.15.refs_6_ = f32[4,104,128]{2,1,0:T(8,128)S(1)} collective-permute-done((f32[4,104,128]{2,1,0:T(8,128)S(1)}, f32[4,104,128]{2,1,0:T(8,128)S(1)}, u32[]{:S(2)}, u32[]{:S(2)}) %collective-permute-start.15) | collective-permute-done | bytes 213024 | tf_op jit(solution)/shard_map/ppermute | solution.py:75
  55.2 4.6 %collective-permute-done.14.refs_5_ = f32[4,104,128]{2,1,0:T(8,128)S(1)} collective-permute-done((f32[4,104,128]{2,1,0:T(8,128)S(1)}, f32[4,104,128]{2,1,0:T(8,128)S(1)}, u32[]{:S(2)}, u32[]{:S(2)}) %collective-permute-start.14) | collective-permute-done | bytes 213024 | tf_op jit(solution)/shard_map/ppermute | solution.py:75
  59.8 16.4 %shard_map.133 = (f32[6,256,128]{2,1,0:T(8,128)S(1)}, f32[32,128]{1,0:T(8,128)S(1)}) custom-call(f32[6,8,32,256]{3,2,1,0:T(8,128)S(1)} %get-tuple-element.29.own, f32[20,32,256]{2,1,0:T(8,128)S(1)} %get-tuple-element.30.keep, f32[20,32,256]{2,1,0:T(8,128)S(1)} %get-tuple-element.31.curl, f32[32,128]{1,0:T(8,128)S(1)} %get-tuple-element.32.phase_in, ...), custom_call_target="tpu_custom_call" | custom-call | tf_op jit(solution)/shard_map/pallas_call | solution.py:49
  76.3 5.1 %collective-permute-start.8 = (f32[32,128]{1,0:T(8,128)S(1)}, f32[32,128]{1,0:T(8,128)S(1)}, u32[]{:S(2)}, u32[]{:S(2)}) collective-permute-start(f32[32,128]{1,0:T(8,128)S(1)} %get-tuple-element.35.refs_0_), channel_id=1, source_target_pairs={{0,1},{1,2},{2,3},{3,0},{4,5},{5,6},{6,7},{7,4},{8,9},{9,10},{10,1... | collective-permute-start | bytes 49160 | tf_op jit(solution)/shard_map/ppermute | solution.py:75
  81.4 1.4 %collective-permute-start.9 = (f32[32,128]{1,0:T(8,128)S(1)}, f32[32,128]{1,0:T(8,128)S(1)}, u32[]{:S(2)}, u32[]{:S(2)}) collective-permute-start(f32[32,128]{1,0:T(8,128)S(1)} %get-tuple-element.35.refs_0_), channel_id=1, source_target_pairs={{0,2},{1,3},{2,0},{3,1},{4,6},{5,7},{6,4},{7,5},{8,10},{9,11},{10,... | collective-permute-start | bytes 49160 | tf_op jit(solution)/shard_map/ppermute | solution.py:75
  83.1 0.6 collective-permute-done.8.refs_1_
  83.7 2.4 %collective-permute-done.9.refs_2_ = f32[32,128]{1,0:T(8,128)S(1)} collective-permute-done((f32[32,128]{1,0:T(8,128)S(1)}, f32[32,128]{1,0:T(8,128)S(1)}, u32[]{:S(2)}, u32[]{:S(2)}) %collective-permute-start.9) | collective-permute-done | bytes 16416 | tf_op jit(solution)/shard_map/ppermute | solution.py:75
  86.0 0.9 shard_map.134
  87.0 2.6 %collective-permute-start.12 = (f32[16,256]{1,0:T(8,128)S(1)}, f32[16,256]{1,0:T(8,128)S(1)}, u32[]{:S(2)}, u32[]{:S(2)}) collective-permute-start(f32[16,256]{1,0:T(8,128)S(1)} %get-tuple-element.38.refs_0_), channel_id=1, source_target_pairs={{0,8},{4,12},{8,0},{12,4},{1,9},{5,13},{9,1},{13,5},{2,10},{6,14},... | collective-permute-start | bytes 49160 | tf_op jit(solution)/shard_map/ppermute | solution.py:75
  89.6 1.4 %collective-permute-start.13 = (f32[16,256]{1,0:T(8,128)S(1)}, f32[16,256]{1,0:T(8,128)S(1)}, u32[]{:S(2)}, u32[]{:S(2)}) collective-permute-start(f32[16,256]{1,0:T(8,128)S(1)} %get-tuple-element.38.refs_0_), channel_id=1, source_target_pairs={{0,12},{4,0},{8,4},{12,8},{1,13},{5,1},{9,5},{13,9},{2,14},{6,2},{... | collective-permute-start | bytes 49160 | tf_op jit(solution)/shard_map/ppermute | solution.py:75
  91.3 1.1 %collective-permute-done.13.refs_3_ = f32[16,256]{1,0:T(8,128)S(1)} collective-permute-done((f32[16,256]{1,0:T(8,128)S(1)}, f32[16,256]{1,0:T(8,128)S(1)}, u32[]{:S(2)}, u32[]{:S(2)}) %collective-permute-start.13) | collective-permute-done | bytes 16416 | tf_op jit(solution)/shard_map/ppermute | solution.py:75
  92.4 10.4 %shard_map.135 = (f32[32,512]{1,0:T(8,128)S(1)}, f32[32,512]{1,0:T(8,128)S(1)}, f32[32,512]{1,0:T(8,128)S(1)}, f32[32,512]{1,0:T(8,128)S(1)}) custom-call(f32[16,256]{1,0:T(8,128)S(1)} %get-tuple-element.38.refs_0_, f32[16,256]{1,0:T(8,128)S(1)} %collective-permute-done.11.refs_1_, f32[16,256]{1,0:T(8,128)S(1)} %collective-permute-done.12.refs_2_, ...), custom_call_target="tpu_custom_call" | custom-call | tf_op jit(solution)/shard_map/pallas_call | solution.py:49
  103.2 1.7 %collective-permute-start.18 = (f32[32,512]{1,0:T(8,128)S(1)}, f32[32,512]{1,0:T(8,128)S(1)}, u32[]{:S(2)}, u32[]{:S(2)}) collective-permute-start(f32[32,512]{1,0:T(8,128)S(1)} %get-tuple-element.42), channel_id=1, source_target_pairs={{0,8},{4,12},{8,0},{12,4},{1,9},{5,13},{9,1},{13,5},{2,10},{6,14},... | collective-permute-start | bytes 196616 | tf_op jit(solution)/shard_map/ppermute | solution.py:75
  105.2 1.3 %collective-permute-done.17 = f32[32,512]{1,0:T(8,128)S(1)} collective-permute-done((f32[32,512]{1,0:T(8,128)S(1)}, f32[32,512]{1,0:T(8,128)S(1)}, u32[]{:S(2)}, u32[]{:S(2)}) %collective-permute-start.17) | collective-permute-done | bytes 65568 | tf_op jit(solution)/shard_map/ppermute | solution.py:75
  106.5 1.4 %collective-permute-done.18 = f32[32,512]{1,0:T(8,128)S(1)} collective-permute-done((f32[32,512]{1,0:T(8,128)S(1)}, f32[32,512]{1,0:T(8,128)S(1)}, u32[]{:S(2)}, u32[]{:S(2)}) %collective-permute-start.18) | collective-permute-done | bytes 65568 | tf_op jit(solution)/shard_map/ppermute | solution.py:75
  107.9 0.6 add_add_fusion
  (42 shorter events, 2.0 us)
Async XLA Ops:
  0.6 13.9 %copy-start.4 = (f32[12,2]{1,0:T(8,128)S(1)}, f32[12,2]{1,0:T(8,128)}, u32[]{:S(2)}) copy-start(f32[12,2]{1,0:T(8,128)} %constant.14.clone.moments) | copy-start | bytes 292
  0.6 13.4 %copy-start.8 = (f32[4]{0:T(128)S(1)}, f32[4]{0:T(128)}, u32[]{:S(2)}) copy-start(f32[4]{0:T(128)} %param.14) | copy-start | bytes 52
  0.7 13.4 %copy-start.7 = (f32[4]{0:T(128)S(1)}, f32[4]{0:T(128)}, u32[]{:S(2)}) copy-start(f32[4]{0:T(128)} %param.15) | copy-start | bytes 52
  0.7 0.7 copy-start.5
  1.4 0.7 copy-start.6
  4.5 10.0 %collective-permute-start = (f32[6,7,32,128]{3,2,1,0:T(8,128)S(1)}, f32[6,7,32,128]{3,2,1,0:T(8,128)S(1)}, u32[]{:S(2)}, u32[]{:S(2)}) collective-permute-start(f32[6,7,32,128]{3,2,1,0:T(8,128)S(1)} %get-tuple-element.25), channel_id=1, source_target_pairs={{0,4},{4,0},{8,12},{12,8},{1,5},{5,1},{9,13},{13,9},{2,6},{6,2},{1... | collective-permute-start | bytes 2064392 | tf_op jit(solution)/shard_map/ppermute | solution.py:70
  5.0 9.5 %collective-permute-start.1 = (f32[6,7,32,128]{3,2,1,0:T(8,128)S(1)}, f32[6,7,32,128]{3,2,1,0:T(8,128)S(1)}, u32[]{:S(2)}, u32[]{:S(2)}) collective-permute-start(f32[6,7,32,128]{3,2,1,0:T(8,128)S(1)} %get-tuple-element.26), channel_id=1, source_target_pairs={{4,8},{8,4},{5,9},{9,5},{6,10},{10,6},{7,11},{11,7},{20,24},{24,20... | collective-permute-start | bytes 2064392 | tf_op jit(solution)/shard_map/ppermute | solution.py:70
  5.7 5.4 %collective-permute-start.2 = (f32[7,32,128]{2,1,0:T(8,128)S(1)}, f32[7,32,128]{2,1,0:T(8,128)S(1)}, u32[]{:S(2)}, u32[]{:S(2)}) collective-permute-start(f32[7,32,128]{2,1,0:T(8,128)S(1)} %get-tuple-element.27), channel_id=1, source_target_pairs={{0,1},{1,0},{2,3},{3,2},{4,5},{5,4},{6,7},{7,6},{8,9},{9,8},{10,11... | collective-permute-start | bytes 344072 | tf_op jit(solution)/shard_map/ppermute | solution.py:70
  8.4 2.8 %collective-permute-start.3 = (f32[7,32,128]{2,1,0:T(8,128)S(1)}, f32[7,32,128]{2,1,0:T(8,128)S(1)}, u32[]{:S(2)}, u32[]{:S(2)}) collective-permute-start(f32[7,32,128]{2,1,0:T(8,128)S(1)} %get-tuple-element.28), channel_id=1, source_target_pairs={{1,2},{2,1},{5,6},{6,5},{9,10},{10,9},{13,14},{14,13},{17,18},{18,... | collective-permute-start | bytes 344072 | tf_op jit(solution)/shard_map/ppermute | solution.py:70
  11.2 3.3 %collective-permute-start.4 = (f32[2,7,32,128]{3,2,1,0:T(8,128)S(1)}, f32[2,7,32,128]{3,2,1,0:T(8,128)S(1)}, u32[]{:S(2)}, u32[]{:S(2)}) collective-permute-start(f32[2,7,32,128]{3,2,1,0:T(8,128)S(1)} %pad_maximum_fusion), channel_id=1, source_target_pairs={{0,4},{4,0},{8,12},{12,8},{1,5},{5,1},{9,13},{13,9},{2,6},{6,2},{1... | collective-permute-start | bytes 688136 | tf_op jit(solution)/shard_map/ppermute | solution.py:70
  13.4 1.1 %collective-permute-start.5 = (f32[2,7,32,128]{3,2,1,0:T(8,128)S(1)}, f32[2,7,32,128]{3,2,1,0:T(8,128)S(1)}, u32[]{:S(2)}, u32[]{:S(2)}) collective-permute-start(f32[2,7,32,128]{3,2,1,0:T(8,128)S(1)} %pad_maximum_fusion), channel_id=1, source_target_pairs={{4,8},{8,4},{5,9},{9,5},{6,10},{10,6},{7,11},{11,7},{20,24},{24,20... | collective-permute-start | bytes 688136 | tf_op jit(solution)/shard_map/ppermute | solution.py:70
  32.3 27.5 %collective-permute-start.6 = (f32[7,6,32,128]{3,2,1,0:T(8,128)S(1)}, f32[7,6,32,128]{3,2,1,0:T(8,128)S(1)}, u32[]{:S(2)}, u32[]{:S(2)}) collective-permute-start(f32[7,6,32,128]{3,2,1,0:T(8,128)S(1)} %get-tuple-element.33), channel_id=1, source_target_pairs={{0,4},{4,0},{8,12},{12,8},{1,5},{5,1},{9,13},{13,9},{2,6},{6,2},{1... | collective-permute-start | bytes 2064392 | tf_op jit(solution)/shard_map/ppermute | solution.py:70
  38.6 21.2 %collective-permute-start.7 = (f32[7,6,32,128]{3,2,1,0:T(8,128)S(1)}, f32[7,6,32,128]{3,2,1,0:T(8,128)S(1)}, u32[]{:S(2)}, u32[]{:S(2)}) collective-permute-start(f32[7,6,32,128]{3,2,1,0:T(8,128)S(1)} %get-tuple-element.34), channel_id=1, source_target_pairs={{4,8},{8,4},{5,9},{9,5},{6,10},{10,6},{7,11},{11,7},{20,24},{24,20... | collective-permute-start | bytes 2064392 | tf_op jit(solution)/shard_map/ppermute | solution.py:70
  39.3 15.9 %collective-permute-start.15 = (f32[4,104,128]{2,1,0:T(8,128)S(1)}, f32[4,104,128]{2,1,0:T(8,128)S(1)}, u32[]{:S(2)}, u32[]{:S(2)}) collective-permute-start(f32[4,104,128]{2,1,0:T(8,128)S(1)} %get-tuple-element.39.refs_4_), channel_id=1, source_target_pairs={{0,2},{1,3},{2,0},{3,1},{4,6},{5,7},{6,4},{7,5},{8,10},{9,11},{10,... | collective-permute-start | bytes 638984 | tf_op jit(solution)/shard_map/ppermute | solution.py:75
  45.4 9.8 %collective-permute-start.16 = (f32[4,104,128]{2,1,0:T(8,128)S(1)}, f32[4,104,128]{2,1,0:T(8,128)S(1)}, u32[]{:S(2)}, u32[]{:S(2)}) collective-permute-start(f32[4,104,128]{2,1,0:T(8,128)S(1)} %get-tuple-element.39.refs_4_), channel_id=1, source_target_pairs={{0,3},{1,0},{2,1},{3,2},{4,7},{5,4},{6,5},{7,6},{8,11},{9,8},{10,9... | collective-permute-start | bytes 638984 | tf_op jit(solution)/shard_map/ppermute | solution.py:75
  46.3 13.4 %collective-permute-start.14 = (f32[4,104,128]{2,1,0:T(8,128)S(1)}, f32[4,104,128]{2,1,0:T(8,128)S(1)}, u32[]{:S(2)}, u32[]{:S(2)}) collective-permute-start(f32[4,104,128]{2,1,0:T(8,128)S(1)} %get-tuple-element.39.refs_4_), channel_id=1, source_target_pairs={{0,1},{1,2},{2,3},{3,0},{4,5},{5,6},{6,7},{7,4},{8,9},{9,10},{10,1... | collective-permute-start | bytes 638984 | tf_op jit(solution)/shard_map/ppermute | solution.py:75
  59.8 26.2 %copy-start = (f32[4,128,256]{2,1,0:T(8,128)S(1)}, f32[4,128,256]{2,1,0:T(8,128)}, u32[]{:S(2)}) copy-start(f32[4,128,256]{2,1,0:T(8,128)} %constant.15.clone.refs_4_) | copy-start | bytes 1572868
  59.8 32.6 %copy-start.3 = (f32[224,32]{1,0:T(8,128)S(1)}, f32[224,32]{1,0:T(8,128)}, u32[]{:S(2)}) copy-start(f32[224,32]{1,0:T(8,128)} %constant.16.clone.refs_8_) | copy-start | bytes 86020
  76.2 16.2 %copy-start.1 = (bf16[256,1024]{1,0:T(8,128)(2,1)S(1)}, bf16[256,1024]{1,0:T(8,128)(2,1)}, u32[]{:S(2)}) copy-start(bf16[256,1024]{1,0:T(8,128)(2,1)} %constant.17.clone.refs_9_) | copy-start | bytes 1572868
  76.2 16.2 %copy-start.2 = (bf16[16,32,192]{2,1,0:T(8,128)(2,1)S(1)}, bf16[16,32,192]{2,1,0:T(8,128)(2,1)}, u32[]{:S(2)}) copy-start(bf16[16,32,192]{2,1,0:T(8,128)(2,1)} %constant.18.clone.refs_10_) | copy-start | bytes 589828
  76.3 6.8 %collective-permute-start.10 = (f32[32,128]{1,0:T(8,128)S(1)}, f32[32,128]{1,0:T(8,128)S(1)}, u32[]{:S(2)}, u32[]{:S(2)}) collective-permute-start(f32[32,128]{1,0:T(8,128)S(1)} %get-tuple-element.35.refs_0_), channel_id=1, source_target_pairs={{0,3},{1,0},{2,1},{3,2},{4,7},{5,4},{6,5},{7,6},{8,11},{9,8},{10,9... | collective-permute-start | bytes 49160 | tf_op jit(solution)/shard_map/ppermute | solution.py:75
  76.3 7.3 %collective-permute-start.8 = (f32[32,128]{1,0:T(8,128)S(1)}, f32[32,128]{1,0:T(8,128)S(1)}, u32[]{:S(2)}, u32[]{:S(2)}) collective-permute-start(f32[32,128]{1,0:T(8,128)S(1)} %get-tuple-element.35.refs_0_), channel_id=1, source_target_pairs={{0,1},{1,2},{2,3},{3,0},{4,5},{5,6},{6,7},{7,4},{8,9},{9,10},{10,1... | collective-permute-start | bytes 49160 | tf_op jit(solution)/shard_map/ppermute | solution.py:75
  81.4 4.6 %collective-permute-start.9 = (f32[32,128]{1,0:T(8,128)S(1)}, f32[32,128]{1,0:T(8,128)S(1)}, u32[]{:S(2)}, u32[]{:S(2)}) collective-permute-start(f32[32,128]{1,0:T(8,128)S(1)} %get-tuple-element.35.refs_0_), channel_id=1, source_target_pairs={{0,2},{1,3},{2,0},{3,1},{4,6},{5,7},{6,4},{7,5},{8,10},{9,11},{10,... | collective-permute-start | bytes 49160 | tf_op jit(solution)/shard_map/ppermute | solution.py:75
  87.0 4.2 %collective-permute-start.11 = (f32[16,256]{1,0:T(8,128)S(1)}, f32[16,256]{1,0:T(8,128)S(1)}, u32[]{:S(2)}, u32[]{:S(2)}) collective-permute-start(f32[16,256]{1,0:T(8,128)S(1)} %get-tuple-element.38.refs_0_), channel_id=1, source_target_pairs={{0,4},{4,8},{8,12},{12,0},{1,5},{5,9},{9,13},{13,1},{2,6},{6,10},{... | collective-permute-start | bytes 49160 | tf_op jit(solution)/shard_map/ppermute | solution.py:75
  87.0 4.3 %collective-permute-start.12 = (f32[16,256]{1,0:T(8,128)S(1)}, f32[16,256]{1,0:T(8,128)S(1)}, u32[]{:S(2)}, u32[]{:S(2)}) collective-permute-start(f32[16,256]{1,0:T(8,128)S(1)} %get-tuple-element.38.refs_0_), channel_id=1, source_target_pairs={{0,8},{4,12},{8,0},{12,4},{1,9},{5,13},{9,1},{13,5},{2,10},{6,14},... | collective-permute-start | bytes 49160 | tf_op jit(solution)/shard_map/ppermute | solution.py:75
  89.6 2.8 %collective-permute-start.13 = (f32[16,256]{1,0:T(8,128)S(1)}, f32[16,256]{1,0:T(8,128)S(1)}, u32[]{:S(2)}, u32[]{:S(2)}) collective-permute-start(f32[16,256]{1,0:T(8,128)S(1)} %get-tuple-element.38.refs_0_), channel_id=1, source_target_pairs={{0,12},{4,0},{8,4},{12,8},{1,13},{5,1},{9,5},{13,9},{2,14},{6,2},{... | collective-permute-start | bytes 49160 | tf_op jit(solution)/shard_map/ppermute | solution.py:75
  102.8 3.7 %collective-permute-start.17 = (f32[32,512]{1,0:T(8,128)S(1)}, f32[32,512]{1,0:T(8,128)S(1)}, u32[]{:S(2)}, u32[]{:S(2)}) collective-permute-start(f32[32,512]{1,0:T(8,128)S(1)} %get-tuple-element.41), channel_id=1, source_target_pairs={{0,4},{4,8},{8,12},{12,0},{1,5},{5,9},{9,13},{13,1},{2,6},{6,10},{... | collective-permute-start | bytes 196616 | tf_op jit(solution)/shard_map/ppermute | solution.py:75
  103.2 4.7 %collective-permute-start.18 = (f32[32,512]{1,0:T(8,128)S(1)}, f32[32,512]{1,0:T(8,128)S(1)}, u32[]{:S(2)}, u32[]{:S(2)}) collective-permute-start(f32[32,512]{1,0:T(8,128)S(1)} %get-tuple-element.42), channel_id=1, source_target_pairs={{0,8},{4,12},{8,0},{12,4},{1,9},{5,13},{9,1},{13,5},{2,10},{6,14},... | collective-permute-start | bytes 196616 | tf_op jit(solution)/shard_map/ppermute | solution.py:75
  105.0 3.0 %collective-permute-start.19 = (f32[32,512]{1,0:T(8,128)S(1)}, f32[32,512]{1,0:T(8,128)S(1)}, u32[]{:S(2)}, u32[]{:S(2)}) collective-permute-start(f32[32,512]{1,0:T(8,128)S(1)} %get-tuple-element.43), channel_id=1, source_target_pairs={{0,12},{4,0},{8,4},{12,8},{1,13},{5,1},{9,5},{13,9},{2,14},{6,2},{... | collective-permute-start | bytes 196616 | tf_op jit(solution)/shard_map/ppermute | solution.py:75

commit v2 on v1

v2 whole, which is shorter than its diff:
```python
import functools
import math

import jax
import jax.numpy as jnp
import numpy as np
from jax import lax
from jax.experimental import pallas as pl
from jax.experimental.pallas import tpu as pltpu
from jax.sharding import PartitionSpec as P

STEPS = 12
ROUNDS = 2
M = 512
REACH = 8

COURANT = 0.55
ANGULAR = 0.7
PRECISE = lax.Precision.HIGHEST


F32 = jnp.float32
BF16 = jnp.bfloat16


def vmem():
    return pl.BlockSpec(memory_space=pltpu.VMEM)


def smem():
    return pl.BlockSpec(memory_space=pltpu.SMEM)


def hbm():
    return pl.BlockSpec(memory_space=pltpu.HBM)


def call(kernel, ins, outs, scratch=(), limit=16):
    spaces = {"h": hbm, "c": vmem, "v": vmem, "s": smem}
    memories = {"h": pltpu.HBM, "v": pltpu.VMEM}

    def out_spec(out):
        return vmem() if not isinstance(out, jax.ShapeDtypeStruct) else pl.BlockSpec(memory_space=pl.ANY)

    held = [
        pltpu.with_memory_space_constraint(array, memories[space]) if space in memories else array
        for array, space in ins
    ]
    return pl.pallas_call(
        kernel,
        out_shape=outs,
        in_specs=[spaces[space]() for _, space in ins],
        out_specs=[out_spec(out) for out in outs],
        scratch_shapes=list(scratch),
        compiler_params=pltpu.CompilerParams(vmem_limit_bytes=limit << 20),
    )(*held)


def shape(*dims, dtype=F32):
    return pltpu.VMEM(dims, dtype)


def swap(values, axis, first):
    count = lax.axis_size(axis)
    pairs = []
    for low in range(first, count - 1, 2):
        pairs += [(low, low + 1), (low + 1, low)]
    if not pairs:
        return jnp.zeros_like(values)
    return lax.ppermute(values, axis, pairs)


def cyclic(values, axis, by):
    count = lax.axis_size(axis)
    return lax.ppermute(values, axis, [(i, (i + by) % count) for i in range(count)])


def waves(order_ids, cell_ids, period):
    wrapped = (order_ids[:, None] * cell_ids[None, :]) % period
    angles = 2.0 * math.pi / period * wrapped
    return np.cos(angles), np.sin(angles)


class Geo:
    def __init__(self, depth, cells_x, cells_y, total_x, total_y, count):
        self.depth, self.cells_x, self.cells_y = depth, cells_x, cells_y
        self.total_x, self.total_y, self.count = total_x, total_y, count
        self.wide = 128
        self.per = self.wide // depth
        self.own = cells_x // self.per
        self.groups = 3 * self.own
        self.pad = 16
        self.slack = 8
        self.first = self.slack + self.pad
        self.rows = cells_y + 2 * self.first
        self.half = self.wide // 2
        self.reach = 8
        assert self.per * depth == self.wide and self.own == 2 and cells_x == 2 * self.per
        assert self.per + self.per // 2 == count and STEPS <= self.pad and STEPS - count <= self.reach


PLANES = 6
SCALE = 1.0 / COURANT


def halves_of(planes):
    return (planes + 1) // 2


def pack_rows(get, put, planes, upper, lane, half):
    for plane in range(planes):
        put(plane, get(plane, 1 if upper else 0))
    kept = (lane >= half) if upper else (lane < half)
    group = 0 if upper else 1
    for at in range(halves_of(planes)):
        value = get(2 * at, group)
        if 2 * at + 1 < planes:
            value = jnp.where(kept, value, pltpu.roll(get(2 * at + 1, group), half, 1))
        put(planes + at, value)


def unpack_rows(get, put, planes, inner, outer, kept, half):
    for plane in range(planes):
        put(plane, inner, get(plane))
        value = get(planes + plane // 2)
        if plane % 2:
            value = pltpu.roll(value, half, 1)
        put(plane, outer, jnp.where(kept, value, 0.0))


def pack_kernel(
    far_fields, far_map, shifts, weights, far_masks,
    tile, send_a, send_b, send_c, send_d, source_pack,
    fields, materials, masks, arrived, *, geo,
):
    copies = [
        pltpu.make_async_copy(far_fields, fields, arrived.at[0]),
        pltpu.make_async_copy(far_map, materials, arrived.at[1]),
        pltpu.make_async_copy(far_masks, masks, arrived.at[2]),
    ]
    for copy in copies:
        copy.start()
    for copy in copies:
        copy.wait()
    even_x = lax.axis_index("gx") % 2 == 0
    even_y = lax.axis_index("gy") % 2 == 0
    pad, last = geo.pad, geo.cells_y - geo.pad
    for plane in range(PLANES + 1):
        for group in range(geo.own):
            parts = []
            for x in range(group * geo.per, (group + 1) * geo.per):
                here = pl.ds(x, geo.depth, stride=geo.cells_x)
                parts.append(fields[plane, here, :] if plane < PLANES else materials[here, :].astype(F32))
            values = jnp.concatenate(parts, 0).T
            if 3 <= plane < PLANES:
                values = values * SCALE
            tile[plane, group] = values
            low, high = values[0:pad], values[last:]
            send_c[plane, group] = jnp.where(even_y, high, low)
            send_d[plane, group] = jnp.where(even_y, low, high)
    lane = lax.broadcasted_iota(jnp.int32, (geo.cells_y, geo.wide), 1)

    def fill(send, upper):
        def put(at, value):
            send[at] = value

        pack_rows(lambda plane, group: tile[plane, group], put, PLANES + 1, upper, lane, geo.half)

    @pl.when(even_x)
    def _():
        fill(send_a, True)
        fill(send_b, False)

    @pl.when(jnp.logical_not(even_x))
    def _():
        fill(send_a, False)
        fill(send_b, True)

    orders_p, orders_q = masks.shape[1:]
    source_pack[...] = jnp.zeros(source_pack.shape, F32)
    for source in range(masks.shape[0]):
        source_pack[source, 0:orders_p, 0:orders_q] = masks[source].astype(F32)
        for at, fact in enumerate((shifts[0, source], shifts[1, source], weights[source])):
            source_pack[source, orders_p : orders_p + 1, at : at + 1] = jnp.full((1, 1), fact).astype(F32)


def edge_kernel(got_c, got_d, send_a, send_b, *, geo):
    even_x = lax.axis_index("gx") % 2 == 0
    even_y = lax.axis_index("gy") % 2 == 0
    lane = lax.broadcasted_iota(jnp.int32, (geo.pad, geo.wide), 1)

    def fill(send, upper):
        for side in range(2):

            def get(plane, group, side=side):
                c_value, d_value = got_c[plane, group], got_d[plane, group]
                if side:
                    return jnp.where(even_y, c_value, d_value)
                return jnp.where(even_y, d_value, c_value)

            def put(at, value, side=side):
                send[at, side * geo.pad : (side + 1) * geo.pad, :] = value

            pack_rows(get, put, PLANES + 1, upper, lane, geo.half)

    @pl.when(even_x)
    def _():
        fill(send_a, True)
        fill(send_b, False)

    @pl.when(jnp.logical_not(even_x))
    def _():
        fill(send_a, False)
        fill(send_b, True)


def run_steps(state, keep, curl, phase, moments, first_step, geo):
    ex, ey, ez, hx, hy, hz = state
    wide, depth, groups = geo.wide, geo.depth, geo.groups
    first = geo.first
    chunk = 16
    beyond = geo.pad if first_step == 0 else geo.reach
    starts = range(first - beyond, first + geo.cells_y + beyond, chunk)
    lane = lax.broadcasted_iota(jnp.int32, (chunk, wide), 1)
    level = lane % depth
    at_top, at_bottom = level == depth - 1, level == 0
    not_first, not_last = lane >= depth, lane < wide - depth
    low_x = lax.axis_index("gx") == 0
    low_y = lax.axis_index("gy") == 0

    def next_z(values):
        return jnp.where(at_top, 0.0, pltpu.roll(values, wide - 1, 1))

    def last_z(values):
        return jnp.where(at_bottom, 0.0, pltpu.roll(values, 1, 1))

    def magnetic(g, carry):
        after = jnp.minimum(g + 1, groups - 1)
        for start in starts:
            here, ahead = pl.ds(start, chunk), pl.ds(start + 1, chunk)
            x, y, z = ex[g, here, :], ey[g, here, :], ez[g, here, :]
            y_x = pltpu.roll(jnp.where(not_first, y, ey[after, here, :]), wide - depth, 1)
            z_x = pltpu.roll(jnp.where(not_first, z, ez[after, here, :]), wide - depth, 1)
            hx[g, here, :] = hx[g, here, :] - ((ez[g, ahead, :] - z) - (next_z(y) - y))
            hy[g, here, :] = hy[g, here, :] - ((next_z(x) - x) - (z_x - z))
            hz[g, here, :] = hz[g, here, :] - ((y_x - y) - (ex[g, ahead, :] - x))
        return carry

    def electric(g, carry):
        before = jnp.maximum(g - 1, 0)
        for start in starts:
            here, behind = pl.ds(start, chunk), pl.ds(start - 1, chunk)
            x, y, z = hx[g, here, :], hy[g, here, :], hz[g, here, :]
            y_x = pltpu.roll(jnp.where(not_last, y, hy[before, here, :]), depth, 1)
            z_x = pltpu.roll(jnp.where(not_last, z, hz[before, here, :]), depth, 1)
            row = pl.ds(start - first + geo.pad, chunk)
            kept, turned = keep[g, row, :], curl[g, row, :]
            ex[g, here, :] = kept * ex[g, here, :] + turned * ((z - hz[g, behind, :]) - (y - last_z(y)))
            ey[g, here, :] = kept * ey[g, here, :] + turned * ((x - last_z(x)) - (z - z_x))
            ez[g, here, :] = kept * ez[g, here, :] + turned * ((y - y_x) - (x - hx[g, behind, :]))
        return carry

    near = geo.own * geo.per

    def step(index, carry):
        left = geo.count - 1 - index
        low = (near - left - 1) // geo.per
        high = (near + geo.cells_x - 1 + left) // geo.per + 1
        lax.fori_loop(low, high, magnetic, 0)

        @pl.when(low_y)
        def _():
            for field in (hx, hz):
                for g in range(groups):
                    field[g, first - 1 : first, :] = jnp.zeros((1, wide), F32)

        @pl.when(low_x)
        def _():
            for field in (hy, hz):
                for start in starts:
                    here = pl.ds(start, chunk)
                    field[geo.own - 1, here, :] = jnp.where(not_last, field[geo.own - 1, here, :], 0.0)

        lax.fori_loop(low, high, electric, 0)
        at = first_step + index
        cosine, sine = moments[at, 0], moments[at, 1]
        middle = depth // 2
        for start in range(0, geo.cells_y, chunk):
            here = pl.ds(first + start, chunk)
            seen = ex[geo.own, here, :]
            for spot, (field, g) in enumerate(((ex, 1), (ey, 0), (ey, 1)), 1):
                moved = pltpu.roll(field[geo.own + g, here, :], spot, 1)
                seen = jnp.where(level == middle + spot, moved, seen)
            there = pl.ds(start, chunk)
            phase[0, there, :] = phase[0, there, :] + seen * cosine
            phase[1, there, :] = phase[1, there, :] - seen * sine
        return carry

    lax.fori_loop(0, geo.count, step, 0)


def sides(geo):
    odd_x = lax.axis_index("gx") % 2 == 1
    below = (geo.own - 1, geo.own - 2)
    above = (2 * geo.own, 2 * geo.own + 1)
    return [
        (jnp.where(odd_x, below[0], above[0]), jnp.where(odd_x, below[1], above[1]), odd_x),
        (jnp.where(odd_x, above[0], below[0]), jnp.where(odd_x, above[1], below[1]), jnp.logical_not(odd_x)),
    ]


def clear(state, geo, beyond):
    low, high = geo.first - beyond, geo.first + geo.cells_y + beyond
    for field in state:
        for g in range(geo.groups):
            field[g, 0:low, :] = jnp.zeros((low, geo.wide), F32)
            field[g, high : geo.rows, :] = jnp.zeros((geo.rows - high, geo.wide), F32)


def half_lanes(rows, geo, lower):
    lane = lax.broadcasted_iota(jnp.int32, (rows, geo.wide), 1)
    return (lane >= geo.half) == lower


def first_kernel(
    tile, got_a, got_b, got_c, got_d, edge_a, edge_b, tables, moments,
    own, keep, curl, phase, send_a, send_b,
    ex, ey, ez, hx, hy, hz, kinds, *, geo,
):
    state = (ex, ey, ez, hx, hy, hz)
    planes = (*state, kinds)
    even_y = lax.axis_index("gy") % 2 == 0
    pad, first, cells_y = geo.pad, geo.first, geo.cells_y
    main = pl.ds(first, cells_y)
    spans = (pl.ds(first - pad, pad), pl.ds(first + cells_y, pad))
    clear(state, geo, pad)
    for at, plane in enumerate(planes):
        for group in range(geo.own):
            g = geo.own + group
            plane[g, main, :] = tile[at, group]
            c_value, d_value = got_c[at, group], got_d[at, group]
            plane[g, spans[0], :] = jnp.where(even_y, d_value, c_value)
            plane[g, spans[1], :] = jnp.where(even_y, c_value, d_value)
    for got, edge, (inner, outer, lower) in zip((got_a, got_b), (edge_a, edge_b), sides(geo)):

        def put_main(at, g, value):
            planes[at][g, main, :] = value

        unpack_rows(
            lambda at, got=got: got[at], put_main, PLANES + 1, inner, outer, half_lanes(cells_y, geo, lower), geo.half
        )
        for side in range(2):

            def put_side(at, g, value, side=side):
                planes[at][g, spans[side], :] = value

            unpack_rows(
                lambda at, edge=edge, side=side: edge[at, side * pad : (side + 1) * pad, :],
                put_side, PLANES + 1, inner, outer, half_lanes(pad, geo, lower), geo.half,
            )

    chunk = 16
    lane = lax.broadcasted_iota(jnp.int32, (chunk, geo.wide), 1)
    row = lax.broadcasted_iota(jnp.int32, (chunk, geo.wide), 0)
    base_x = (lax.axis_index("gx") - 1) * geo.cells_x
    base_y = lax.axis_index("gy") * cells_y - pad

    def coefs(g, carry):
        place_x = base_x + g * geo.per + lane // geo.depth
        inside_x = (place_x >= 0) & (place_x < geo.total_x)
        for start in range(0, cells_y + 2 * pad, chunk):
            place_y = base_y + start + row
            inside = inside_x & (place_y >= 0) & (place_y < geo.total_y)
            kind = kinds[g, pl.ds(first - pad + start, chunk), :]
            kept = jnp.zeros(kind.shape, F32)
            turned = jnp.zeros(kind.shape, F32)
            for material in range(tables.shape[1]):
                match = kind == float(material)
                kept = jnp.where(match, tables[0, material], kept)
                turned = jnp.where(match, tables[1, material], turned)
            there = pl.ds(start, chunk)
            keep[g, there, :] = jnp.where(inside, kept, 0.0)
            curl[g, there, :] = jnp.where(inside, turned, 0.0)
        return carry

    lax.fori_loop(0, geo.groups, coefs, 0)
    phase[...] = jnp.zeros(phase.shape, F32)
    run_steps(state, keep, curl, phase, moments, 0, geo)

    more = pl.ds(first - geo.reach, cells_y + 2 * geo.reach)
    lane = lax.broadcasted_iota(jnp.int32, (cells_y + 2 * geo.reach, geo.wide), 1)
    for at, field in enumerate(state):
        for group in range(geo.own):
            own[at, group] = field[geo.own + group, more, :]

    def fill(send, upper):
        def put(at, value):
            send[at] = value

        pack_rows(lambda at, group: own[at, group], put, PLANES, upper, lane, geo.half)

    even_x = lax.axis_index("gx") % 2 == 0

    @pl.when(even_x)
    def _():
        fill(send_a, True)
        fill(send_b, False)

    @pl.when(jnp.logical_not(even_x))
    def _():
        fill(send_a, False)
        fill(send_b, True)


def second_kernel(
    own, keep, curl, phase_in, got_a, got_b, moments,
    final, phase,
    ex, ey, ez, hx, hy, hz, seen, *, geo,
):
    state = (ex, ey, ez, hx, hy, hz)
    first, cells_y = geo.first, geo.cells_y
    rows = cells_y + 2 * geo.reach
    more = pl.ds(first - geo.reach, rows)
    clear(state, geo, geo.reach)
    for at, field in enumerate(state):
        for group in range(geo.own):
            field[geo.own + group, more, :] = own[at, group]
    for got, (inner, outer, lower) in zip((got_a, got_b), sides(geo)):

        def put(at, g, value):
            state[at][g, more, :] = value

        unpack_rows(lambda at, got=got: got[at], put, PLANES, inner, outer, half_lanes(rows, geo, lower), geo.half)
    seen[...] = phase_in[...]
    run_steps(state, keep, curl, seen, moments, geo.count, geo)
    middle = geo.depth // 2
    for part in range(2):
        turned = seen[part].T
        for within in range(geo.per):
            for comp in range(2):
                for group in range(geo.own):
                    source = within * geo.depth + middle + comp * geo.own + group
                    target = (part * 2 + comp) * geo.cells_x + group * geo.per + within
                    phase[target : target + 1, :] = turned[source : source + 1, :]
    for at, field in enumerate(state):
        for group in range(geo.own):
            values = field[geo.own + group, pl.ds(first, cells_y), :].T
            if at >= 3:
                values = values * COURANT
            for within in range(geo.per):
                here = pl.ds(group * geo.per + within, geo.depth, stride=geo.cells_x)
                final[at, here, :] = values[within * geo.depth : (within + 1) * geo.depth]


def along_y_kernel(*refs, count):
    pieces, (table, fields, part, kept, done) = refs[:count], refs[count:]
    keeping = pltpu.make_async_copy(fields, kept, done)
    keeping.start()
    me = lax.axis_index("gy")
    total = None
    for back, piece in enumerate(pieces):
        origin = (me - back + count) % count
        term = jnp.dot(piece[...], table[origin], precision=PRECISE, preferred_element_type=F32)
        total = term if total is None else total + term
    rows, width = total.shape[0] // 2, total.shape[1] // 2
    re_cos, re_sin = total[:rows, :width], total[:rows, width:]
    im_cos, im_sin = total[rows:, :width], total[rows:, width:]
    part[:, 0:width] = re_cos + im_sin
    part[:, width : 2 * width] = im_cos - re_sin
    keeping.wait()


def image_kernel(*refs, tiles_x, tiles_y, cells_x, scaling, sources_all):
    parts, refs = refs[:tiles_x], refs[tiles_x:]
    packs, refs = refs[:tiles_y], refs[tiles_y:]
    table_x, g_matrix, row_table, shifts, weights = refs[:5]
    strips, refs = refs[5 : 5 + tiles_x], refs[5 + tiles_x :]
    gathered, orders, columns, rows, total = refs
    me_x = lax.axis_index("gx")
    me_y = lax.axis_index("gy")
    width = orders.shape[2]
    reach = orders.shape[1]
    for back, part in enumerate(parts):
        origin = pl.multiple_of((me_x - back + tiles_x) % tiles_x * cells_x, cells_x)
        for comp in range(2):
            gathered[comp, pl.ds(origin, cells_x), :] = part[comp * cells_x : (comp + 1) * cells_x, :]
    for comp in range(2):
        re, im = gathered[comp, :, 0:width], gathered[comp, :, width : 2 * width]
        dot = functools.partial(jnp.dot, precision=PRECISE, preferred_element_type=F32)
        cos_x, sin_x = table_x[0:reach, :], table_x[reach : 2 * reach, :]
        order_re = dot(cos_x, re) + dot(sin_x, im)
        order_im = dot(cos_x, im) - dot(sin_x, re)
        orders[2 * comp] = (order_re * scaling).astype(BF16).astype(F32)
        orders[2 * comp + 1] = (order_im * scaling).astype(BF16).astype(F32)
    strip = row_table.shape[1]
    for ahead in range(tiles_x):
        owner = (me_x + ahead) % tiles_x * tiles_y + me_y
        rows[strip * ahead : strip * (ahead + 1), :] = row_table[owner]
    pixels = g_matrix.shape[1] // 2
    orders_p = rows.shape[1] // 2
    local = packs[0].shape[0]
    total[...] = jnp.zeros(total.shape, F32)
    for at, pack in enumerate(packs):

        def source(index, carry, at=at, pack=pack):
            number = at * local + index
            down = shifts[number, 0] + REACH
            across = width - (shifts[number, 1] + REACH)
            passed = pack[index, 0:orders_p, :]
            masked = []
            for plane in range(4):
                window = orders[plane, pl.ds(down, orders_p), :]
                masked.append((pltpu.roll(window, across, 1) * passed).astype(BF16))
            halves = jnp.concatenate(
                (jnp.concatenate(masked[:2], 1), jnp.concatenate(masked[2:], 1)), 0
            )
            spread = jnp.dot(halves, g_matrix[...], preferred_element_type=F32).astype(BF16)
            for comp in range(2):
                part = spread[comp * orders_p : (comp + 1) * orders_p]
                real, imag = part[:, :pixels], part[:, pixels:]
                low = 2 * comp * pixels
                columns[0:orders_p, low : low + pixels] = real
                columns[0:orders_p, low + pixels : low + 2 * pixels] = imag
                columns[orders_p : 2 * orders_p, low : low + pixels] = -imag
                columns[orders_p : 2 * orders_p, low + pixels : low + 2 * pixels] = real
            bright = None
            for block in range(4):
                value = jnp.dot(
                    rows[...],
                    columns[:, block * pixels : (block + 1) * pixels],
                    preferred_element_type=F32,
                )
                bright = value * value if bright is None else bright + value * value
            total[...] = total[...] + (weights[number] / sources_all) * bright
            return carry

        lax.fori_loop(0, local, source, 0)
    for ahead in range(tiles_x):
        strips[ahead][...] = total[strip * ahead : strip * (ahead + 1), :]


def body(
    fields, material_map, material_eps, material_loss, source_shift, source_mask, source_weight
):
    tiles_x = lax.axis_size("gx")
    tiles_y = lax.axis_size("gy")
    _, depth, cells_x, lanes = fields.shape
    total_x, total_y = cells_x * tiles_x, lanes * tiles_y
    count = STEPS // ROUNDS
    geo = Geo(depth, cells_x, lanes, total_x, total_y, count)
    flat_fields = fields.reshape(6, depth * cells_x, lanes)
    flat_map = material_map.reshape(depth * cells_x, lanes)
    local, orders_p, orders_q = source_mask.shape
    wide = 128

    keep_table = (1.0 - material_loss) / (1.0 + material_loss)
    curl_table = COURANT * (COURANT / (material_eps * (1.0 + material_loss)))
    tables = jnp.stack((keep_table, curl_table))
    angle = np.float32(ANGULAR) * np.arange(1, STEPS + 1, dtype=np.float32)
    moments = jnp.asarray(np.stack((np.cos(angle), np.sin(angle)), 1).astype(np.float32))

    sent = PLANES + 1 + halves_of(PLANES + 1)
    row_shape = shape(sent, lanes, wide)
    side_shape = shape(PLANES + 1, geo.own, geo.pad, wide)
    edge_shape = shape(sent, 2 * geo.pad, wide)
    tile, to_a, to_b, to_c, to_d, my_pack = call(
        functools.partial(pack_kernel, geo=geo),
        [(flat_fields, "h"), (flat_map, "h"), (source_shift.T, "s"), (source_weight, "s"), (source_mask, "h")],
        [shape(PLANES + 1, geo.own, lanes, wide), row_shape, row_shape, side_shape, side_shape]
        + [shape(local, orders_p + 8, wide)],
        [
            pltpu.VMEM(flat_fields.shape, F32),
            pltpu.VMEM(flat_map.shape, jnp.int32),
            pltpu.VMEM(source_mask.shape, jnp.int32),
            pltpu.SemaphoreType.DMA((3,)),
        ],
    )
    got_c = swap(to_c, "gy", 0)
    got_d = swap(to_d, "gy", 1)
    got_a = swap(to_a, "gx", 0)
    got_b = swap(to_b, "gx", 1)
    to_a, to_b = call(functools.partial(edge_kernel, geo=geo), [(got_c, "v"), (got_d, "v")], [edge_shape, edge_shape])
    edge_a = swap(to_a, "gx", 0)
    edge_b = swap(to_b, "gx", 1)
    packs = [my_pack]
    for by in range(1, tiles_y):
        packs.append(cyclic(my_pack, "gy", by))

    state = [pltpu.VMEM((geo.groups, geo.rows, wide), F32) for _ in range(PLANES)]
    coef_shape = shape(geo.groups, lanes + 2 * geo.pad, wide)
    seen_shape = shape(2, lanes, wide)
    longer = lanes + 2 * geo.reach
    send_shape = shape(PLANES + halves_of(PLANES), longer, wide)
    own, keep, curl, seen, to_a, to_b = call(
        functools.partial(first_kernel, geo=geo),
        [(tile, "v"), (got_a, "v"), (got_b, "v"), (got_c, "v"), (got_d, "v"), (edge_a, "v"), (edge_b, "v"),
         (tables, "s"), (moments, "s")],
        [shape(PLANES, geo.own, longer, wide), coef_shape, coef_shape, seen_shape, send_shape, send_shape],
        [*state, pltpu.VMEM((geo.groups, geo.rows, wide), F32)],
    )
    got_a = swap(to_a, "gx", 0)
    got_b = swap(to_b, "gx", 1)
    final, phase = call(
        functools.partial(second_kernel, geo=geo),
        [(own, "v"), (keep, "v"), (curl, "v"), (seen, "v"), (got_a, "v"), (got_b, "v"), (moments, "s")],
        [shape(PLANES, depth * cells_x, lanes), shape(4 * cells_x, lanes)],
        [*state, pltpu.VMEM((2, lanes, wide), F32)],
    )

    reach = orders_p + 2 * REACH
    ids_p = np.arange(-REACH, orders_p + REACH) % orders_p - orders_p // 2
    ids_q = np.arange(-REACH, orders_q + REACH) % orders_q - orders_q // 2
    cos_y, sin_y = waves(ids_q, np.arange(total_y), total_y)
    table_y = np.zeros((total_y, 2 * wide), np.float32)
    table_y[:, : len(ids_q)] = cos_y.T
    table_y[:, wide : wide + len(ids_q)] = sin_y.T
    cos_x, sin_x = waves(ids_p, np.arange(total_x), total_x)
    table_x = np.concatenate((cos_x, sin_x), 0).astype(np.float32)
    pixels = M
    cos_u, sin_u = waves(np.arange(orders_p) - orders_p // 2, np.arange(pixels), pixels)
    strip = pixels // (tiles_x * tiles_y)
    row_table = (np.concatenate((cos_u, sin_u), 0).T / math.sqrt(orders_p)).astype(np.float32)
    row_table = row_table.reshape(tiles_x * tiles_y, strip, 2 * orders_p).astype(jnp.bfloat16)
    cos_v, sin_v = waves(np.arange(orders_q) - orders_q // 2, np.arange(pixels), pixels)
    g_matrix = np.zeros((2 * wide, 2 * pixels), np.float32)
    g_matrix[:orders_q, :pixels] = cos_v / math.sqrt(orders_q)
    g_matrix[:orders_q, pixels:] = sin_v / math.sqrt(orders_q)
    g_matrix[wide : wide + orders_q, :pixels] = -sin_v / math.sqrt(orders_q)
    g_matrix[wide : wide + orders_q, pixels:] = cos_v / math.sqrt(orders_q)
    g_matrix = g_matrix.astype(jnp.bfloat16)

    pieces = [phase] + [cyclic(phase, "gy", by) for by in range(1, tiles_y)]
    part, final = call(
        functools.partial(along_y_kernel, count=tiles_y),
        [(piece, "v") for piece in pieces]
        + [(jnp.asarray(table_y.reshape(tiles_y, lanes, 2 * wide)), "c"), (final, "v")],
        [shape(2 * cells_x, 2 * wide), jax.ShapeDtypeStruct(final.shape, F32)],
        [pltpu.SemaphoreType.DMA],
    )
    parts = [part] + [cyclic(part, "gx", by) for by in range(1, tiles_x)]

    facts = jnp.concatenate([pack[:, orders_p, 0:3] for pack in packs], 0)
    shifts = facts[:, 0:2].astype(jnp.int32)
    weights = facts[:, 2]
    strips = call(
        functools.partial(
            image_kernel,
            tiles_x=tiles_x,
            tiles_y=tiles_y,
            cells_x=cells_x,
            scaling=1.0 / math.sqrt(total_x * total_y * STEPS),
            sources_all=local * tiles_x * tiles_y,
        ),
        [(piece, "v") for piece in parts]
        + [(pack, "v") for pack in packs]
        + [(jnp.asarray(table_x), "c"), (jnp.asarray(g_matrix), "c"), (jnp.asarray(row_table), "c"),
           (shifts, "s"), (weights, "s")],
        [shape(strip, pixels) for _ in range(tiles_x)],
        [
            pltpu.VMEM((2, total_x, 2 * wide), F32),
            pltpu.VMEM((4, reach, wide), F32),
            pltpu.VMEM((2 * orders_p, 4 * pixels), BF16),
            pltpu.VMEM((tiles_x * strip, 2 * orders_p), BF16),
            pltpu.VMEM((tiles_x * strip, pixels), F32),
        ],
    )
    image = strips[0]
    for by in range(1, tiles_x):
        image = image + cyclic(strips[by], "gx", by)
    return (final.reshape(fields.shape), image)


def solution(mesh):
    placed = (
        P("clips", None, "gx", "gy"),
        P("clips", "gx", "gy"),
        P(),
        P(),
        P(("gx", "gy"), None),
        P(("gx", "gy"), None, None),
        P(("gx", "gy")),
    )

    return jax.shard_map(
        body,
        mesh=mesh,
        in_specs=placed,
        out_specs=(P("clips", None, "gx", "gy"), P(("gx", "gy"), "clips")),
        check_vma=False,
    )
```

time: 109 us -> 96.9 us (0.89)
  Pallas kernels: 47.9 us -> 34.5 us
  starting transfers between devices: 35.5 us -> 38 us
    pallas_call x5 -> x6, Pallas kernels: 47.9 us -> 34.5 us  [call(): pl.pallas_call(kernel, out_shape=outs, in_specs=[spaces[space]() for _, s...]
    ppermute x12, starting transfers between devices: 21.1 us -> 23.9 us  [cyclic(): lax.ppermute(values, axis, [(i, (i + by) % count) for i in range(count)])]
  transfers between devices with their start and end apart: 20 -> 20, of which waited for: 11 -> 9; matrix products, arithmetic and copies ran while one was open for 0% -> 0% of each run, Pallas kernels for 0% -> 0%
where the time goes in v2:
time: 96.9 us; the launch traced here: 96.7 us
  starting transfers between devices  38 us (39%)
  Pallas kernels  34.5 us (36%)
  waiting for transfers between devices  21.8 us (22%)
    pallas_call x6, Pallas kernels, call(): pl.pallas_call(kernel, out_shape=outs, in_specs=[spaces[space]() for _, s...  34.5 us
    ppermute x12, starting transfers between devices, cyclic(): lax.ppermute(values, axis, [(i, (i + by) % count) for i in range(count)])  23.9 us
    ppermute x12, waiting for transfers between devices, cyclic(): lax.ppermute(values, axis, [(i, (i + by) % count) for i in range(count)])  19.4 us
    ppermute x8, starting transfers between devices, swap(): return lax.ppermute(values, axis, pairs)  14 us
    ppermute x8, waiting for transfers between devices, swap(): return lax.ppermute(values, axis, pairs)  2.45 us
  transfers between devices with their start and end apart: 20, of which 9 were waited for; matrix products, arithmetic and copies ran while one was open for 0% of the time, Pallas kernels for 0%

profile of v2, /device:TPU:0, one launch (start us, length us, event | category | flops | bytes accessed | tf_op | source)
XLA Modules:
  0.0 96.7 jit_solution(17485685723047671762)
XLA Ops:
  0.7 0.7 copy-done.5
  1.3 2.3 %shard_map.131 = (f32[7,2,128,128]{3,2,1,0:T(8,128)S(1)}, f32[11,128,128]{2,1,0:T(8,128)S(1)}, f32[11,128,128]{2,1,0:T(8,128)S(1)}, f32[7,2,16,128]{3,2,1,0:T(8,...) custom-call(f32[6,256,128]{2,1,0:T(8,128)} %bitcast.13, s32[256,128]{1,0:T(8,128)} %bitcast.14, ...), custom_call_target="tpu_custom_call" | custom-call | tf_op jit(solution)/shard_map/pallas_call | solution.py:49
  3.6 0.6 collective-permute-start
  4.2 0.7 collective-permute-start.1
  4.9 2.6 %collective-permute-start.2 = (f32[7,2,16,128]{3,2,1,0:T(8,128)S(1)}, f32[7,2,16,128]{3,2,1,0:T(8,128)S(1)}, u32[]{:S(2)}, u32[]{:S(2)}) collective-permute-start(f32[7,2,16,128]{3,2,1,0:T(8,128)S(1)} %get-tuple-element.27), channel_id=1, source_target_pairs={{0,1},{1,0},{2,3},{3,2},{4,5},{5,4},{6,7},{7,6},{8,9},{9,8},{10,11... | collective-permute-start | bytes 344072 | tf_op jit(solution)/shard_map/ppermute | solution.py:70
  7.5 0.7 collective-permute-start.3
  8.2 2.1 %collective-permute-done.2.got_c = f32[7,2,16,128]{3,2,1,0:T(8,128)S(1)} collective-permute-done((f32[7,2,16,128]{3,2,1,0:T(8,128)S(1)}, f32[7,2,16,128]{3,2,1,0:T(8,128)S(1)}, u32[]{:S(2)}, u32[]{:S(2)}) %collective-permute-start.2) | collective-permute-done | bytes 114720 | tf_op jit(solution)/shard_map/ppermute | solution.py:70
  10.4 2.2 %collective-permute-start.4 = (f32[11,32,128]{2,1,0:T(8,128)S(1)}, f32[11,32,128]{2,1,0:T(8,128)S(1)}, u32[]{:S(2)}, u32[]{:S(2)}) collective-permute-start(f32[11,32,128]{2,1,0:T(8,128)S(1)} %get-tuple-element.29), channel_id=1, source_target_pairs={{0,4},{4,0},{8,12},{12,8},{1,5},{5,1},{9,13},{13,9},{2,6},{6,2},{1... | collective-permute-start | bytes 540680 | tf_op jit(solution)/shard_map/ppermute | solution.py:70
  12.6 0.7 collective-permute-start.5
  13.7 10.9 %shard_map.133 = (f32[6,2,144,128]{3,2,1,0:T(8,128)S(1)}, f32[6,160,128]{2,1,0:T(8,128)S(1)}, f32[6,160,128]{2,1,0:T(8,128)S(1)}, f32[2,128,128]{2,1,0:T(8,128)S...) custom-call(f32[7,2,128,128]{3,2,1,0:T(8,128)S(1)} %get-tuple-element.24.tile, ...), custom_call_target="tpu_custom_call" | custom-call | tf_op jit(solution)/shard_map/pallas_call | solution.py:49
  24.6 5.9 %collective-permute-start.6 = (f32[9,144,128]{2,1,0:T(8,128)S(1)}, f32[9,144,128]{2,1,0:T(8,128)S(1)}, u32[]{:S(2)}, u32[]{:S(2)}) collective-permute-start(f32[9,144,128]{2,1,0:T(8,128)S(1)} %get-tuple-element.35), channel_id=1, source_target_pairs={{0,4},{4,0},{8,12},{12,8},{1,5},{5,1},{9,13},{13,9},{2,6},{6,2},{1... | collective-permute-start | bytes 1990664 | tf_op jit(solution)/shard_map/ppermute | solution.py:70
  30.5 0.7 collective-permute-start.7
  31.2 4.5 %collective-permute-start.14 = (f32[4,104,128]{2,1,0:T(8,128)S(1)}, f32[4,104,128]{2,1,0:T(8,128)S(1)}, u32[]{:S(2)}, u32[]{:S(2)}) collective-permute-start(f32[4,104,128]{2,1,0:T(8,128)S(1)} %get-tuple-element.41.refs_4_), channel_id=1, source_target_pairs={{0,1},{1,2},{2,3},{3,0},{4,5},{5,6},{6,7},{7,4},{8,9},{9,10},{10,1... | collective-permute-start | bytes 638984 | tf_op jit(solution)/shard_map/ppermute | solution.py:75
  35.7 1.5 %collective-permute-start.15 = (f32[4,104,128]{2,1,0:T(8,128)S(1)}, f32[4,104,128]{2,1,0:T(8,128)S(1)}, u32[]{:S(2)}, u32[]{:S(2)}) collective-permute-start(f32[4,104,128]{2,1,0:T(8,128)S(1)} %get-tuple-element.41.refs_4_), channel_id=1, source_target_pairs={{0,2},{1,3},{2,0},{3,1},{4,6},{5,7},{6,4},{7,5},{8,10},{9,11},{10,... | collective-permute-start | bytes 638984 | tf_op jit(solution)/shard_map/ppermute | solution.py:75
  37.2 2.8 %collective-permute-start.16 = (f32[4,104,128]{2,1,0:T(8,128)S(1)}, f32[4,104,128]{2,1,0:T(8,128)S(1)}, u32[]{:S(2)}, u32[]{:S(2)}) collective-permute-start(f32[4,104,128]{2,1,0:T(8,128)S(1)} %get-tuple-element.41.refs_4_), channel_id=1, source_target_pairs={{0,3},{1,0},{2,1},{3,2},{4,7},{5,4},{6,5},{7,6},{8,11},{9,8},{10,9... | collective-permute-start | bytes 638984 | tf_op jit(solution)/shard_map/ppermute | solution.py:75
  40.1 10.5 %collective-permute-done.15.refs_6_ = f32[4,104,128]{2,1,0:T(8,128)S(1)} collective-permute-done((f32[4,104,128]{2,1,0:T(8,128)S(1)}, f32[4,104,128]{2,1,0:T(8,128)S(1)}, u32[]{:S(2)}, u32[]{:S(2)}) %collective-permute-start.15) | collective-permute-done | bytes 213024 | tf_op jit(solution)/shard_map/ppermute | solution.py:75
  50.6 9.9 %shard_map.134 = (f32[6,256,128]{2,1,0:T(8,128)S(1)}, f32[32,128]{1,0:T(8,128)S(1)}) custom-call(f32[6,2,144,128]{3,2,1,0:T(8,128)S(1)} %get-tuple-element.31.own, f32[6,160,128]{2,1,0:T(8,128)S(1)} %get-tuple-element.32.keep, f32[6,160,128]{2,1,0:T(8,128)S(1)} %get-tuple-element.33.curl, f32[2,128,128]{2,1,0:T(8,128)S(1)} %get-tuple-element.34.phase_in, ...), custom_call_target="tpu_custom_call" | custom-call | tf_op jit(solution)/shard_map/pallas_call | solution.py:49
  60.6 7.3 %collective-permute-start.10 = (f32[32,128]{1,0:T(8,128)S(1)}, f32[32,128]{1,0:T(8,128)S(1)}, u32[]{:S(2)}, u32[]{:S(2)}) collective-permute-start(f32[32,128]{1,0:T(8,128)S(1)} %get-tuple-element.37.refs_0_), channel_id=1, source_target_pairs={{0,3},{1,0},{2,1},{3,2},{4,7},{5,4},{6,5},{7,6},{8,11},{9,8},{10,9... | collective-permute-start | bytes 49160 | tf_op jit(solution)/shard_map/ppermute | solution.py:75
  67.9 0.6 collective-permute-start.9
  68.5 0.8 collective-permute-done.10.refs_3_
  69.4 4.1 %collective-permute-done.8.refs_1_ = f32[32,128]{1,0:T(8,128)S(1)} collective-permute-done((f32[32,128]{1,0:T(8,128)S(1)}, f32[32,128]{1,0:T(8,128)S(1)}, u32[]{:S(2)}, u32[]{:S(2)}) %collective-permute-start.8) | collective-permute-done | bytes 16416 | tf_op jit(solution)/shard_map/ppermute | solution.py:75
  73.5 0.9 shard_map.135
  74.4 0.4 collective-permute-start.11
  74.8 2.8 %collective-permute-start.12 = (f32[16,256]{1,0:T(8,128)S(1)}, f32[16,256]{1,0:T(8,128)S(1)}, u32[]{:S(2)}, u32[]{:S(2)}) collective-permute-start(f32[16,256]{1,0:T(8,128)S(1)} %get-tuple-element.40.refs_0_), channel_id=1, source_target_pairs={{0,8},{4,12},{8,0},{12,4},{1,9},{5,13},{9,1},{13,5},{2,10},{6,14},... | collective-permute-start | bytes 49160 | tf_op jit(solution)/shard_map/ppermute | solution.py:75
  77.7 1.4 %collective-permute-start.13 = (f32[16,256]{1,0:T(8,128)S(1)}, f32[16,256]{1,0:T(8,128)S(1)}, u32[]{:S(2)}, u32[]{:S(2)}) collective-permute-start(f32[16,256]{1,0:T(8,128)S(1)} %get-tuple-element.40.refs_0_), channel_id=1, source_target_pairs={{0,12},{4,0},{8,4},{12,8},{1,13},{5,1},{9,5},{13,9},{2,14},{6,2},{... | collective-permute-start | bytes 49160 | tf_op jit(solution)/shard_map/ppermute | solution.py:75
  79.4 1.1 %collective-permute-done.13.refs_3_ = f32[16,256]{1,0:T(8,128)S(1)} collective-permute-done((f32[16,256]{1,0:T(8,128)S(1)}, f32[16,256]{1,0:T(8,128)S(1)}, u32[]{:S(2)}, u32[]{:S(2)}) %collective-permute-start.13) | collective-permute-done | bytes 16416 | tf_op jit(solution)/shard_map/ppermute | solution.py:75
  80.5 10.4 %shard_map.136 = (f32[32,512]{1,0:T(8,128)S(1)}, f32[32,512]{1,0:T(8,128)S(1)}, f32[32,512]{1,0:T(8,128)S(1)}, f32[32,512]{1,0:T(8,128)S(1)}) custom-call(f32[16,256]{1,0:T(8,128)S(1)} %get-tuple-element.40.refs_0_, f32[16,256]{1,0:T(8,128)S(1)} %collective-permute-done.11.refs_1_, f32[16,256]{1,0:T(8,128)S(1)} %collective-permute-done.12.refs_2_, ...), custom_call_target="tpu_custom_call" | custom-call | tf_op jit(solution)/shard_map/pallas_call | solution.py:49
  90.9 0.4 collective-permute-start.17
  91.3 1.7 %collective-permute-start.18 = (f32[32,512]{1,0:T(8,128)S(1)}, f32[32,512]{1,0:T(8,128)S(1)}, u32[]{:S(2)}, u32[]{:S(2)}) collective-permute-start(f32[32,512]{1,0:T(8,128)S(1)} %get-tuple-element.44), channel_id=1, source_target_pairs={{0,8},{4,12},{8,0},{12,4},{1,9},{5,13},{9,1},{13,5},{2,10},{6,14},... | collective-permute-start | bytes 196616 | tf_op jit(solution)/shard_map/ppermute | solution.py:75
  93.3 1.3 %collective-permute-done.17 = f32[32,512]{1,0:T(8,128)S(1)} collective-permute-done((f32[32,512]{1,0:T(8,128)S(1)}, f32[32,512]{1,0:T(8,128)S(1)}, u32[]{:S(2)}, u32[]{:S(2)}) %collective-permute-start.17) | collective-permute-done | bytes 65568 | tf_op jit(solution)/shard_map/ppermute | solution.py:75
  94.6 1.4 %collective-permute-done.18 = f32[32,512]{1,0:T(8,128)S(1)} collective-permute-done((f32[32,512]{1,0:T(8,128)S(1)}, f32[32,512]{1,0:T(8,128)S(1)}, u32[]{:S(2)}, u32[]{:S(2)}) %collective-permute-start.18) | collective-permute-done | bytes 65568 | tf_op jit(solution)/shard_map/ppermute | solution.py:75
  96.0 0.6 add_add_fusion
  (42 shorter events, 1.2 us)
Async XLA Ops:
  0.6 0.7 copy-start.5
  0.6 0.7 copy-start.6
  3.6 10.1 %collective-permute-start = (f32[11,128,128]{2,1,0:T(8,128)S(1)}, f32[11,128,128]{2,1,0:T(8,128)S(1)}, u32[]{:S(2)}, u32[]{:S(2)}) collective-permute-start(f32[11,128,128]{2,1,0:T(8,128)S(1)} %get-tuple-element.25), channel_id=1, source_target_pairs={{0,4},{4,0},{8,12},{12,8},{1,5},{5,1},{9,13},{13,9},{2,6},{6,2},{1... | collective-permute-start | bytes 2162696 | tf_op jit(solution)/shard_map/ppermute | solution.py:70
  4.2 9.5 %collective-permute-start.1 = (f32[11,128,128]{2,1,0:T(8,128)S(1)}, f32[11,128,128]{2,1,0:T(8,128)S(1)}, u32[]{:S(2)}, u32[]{:S(2)}) collective-permute-start(f32[11,128,128]{2,1,0:T(8,128)S(1)} %get-tuple-element.26), channel_id=1, source_target_pairs={{4,8},{8,4},{5,9},{9,5},{6,10},{10,6},{7,11},{11,7},{20,24},{24,20... | collective-permute-start | bytes 2162696 | tf_op jit(solution)/shard_map/ppermute | solution.py:70
  4.9 5.4 %collective-permute-start.2 = (f32[7,2,16,128]{3,2,1,0:T(8,128)S(1)}, f32[7,2,16,128]{3,2,1,0:T(8,128)S(1)}, u32[]{:S(2)}, u32[]{:S(2)}) collective-permute-start(f32[7,2,16,128]{3,2,1,0:T(8,128)S(1)} %get-tuple-element.27), channel_id=1, source_target_pairs={{0,1},{1,0},{2,3},{3,2},{4,5},{5,4},{6,7},{7,6},{8,9},{9,8},{10,11... | collective-permute-start | bytes 344072 | tf_op jit(solution)/shard_map/ppermute | solution.py:70
  7.5 2.8 %collective-permute-start.3 = (f32[7,2,16,128]{3,2,1,0:T(8,128)S(1)}, f32[7,2,16,128]{3,2,1,0:T(8,128)S(1)}, u32[]{:S(2)}, u32[]{:S(2)}) collective-permute-start(f32[7,2,16,128]{3,2,1,0:T(8,128)S(1)} %get-tuple-element.28), channel_id=1, source_target_pairs={{1,2},{2,1},{5,6},{6,5},{9,10},{10,9},{13,14},{14,13},{17,18},{18,... | collective-permute-start | bytes 344072 | tf_op jit(solution)/shard_map/ppermute | solution.py:70
  10.3 3.0 %copy-start.7 = (f32[4]{0:T(128)S(1)}, f32[4]{0:T(128)}, u32[]{:S(2)}) copy-start(f32[4]{0:T(128)} %param.15) | copy-start | bytes 52
  10.3 3.0 %copy-start.8 = (f32[4]{0:T(128)S(1)}, f32[4]{0:T(128)}, u32[]{:S(2)}) copy-start(f32[4]{0:T(128)} %param.14) | copy-start | bytes 52
  10.4 3.3 %copy-start.4 = (f32[12,2]{1,0:T(8,128)S(1)}, f32[12,2]{1,0:T(8,128)}, u32[]{:S(2)}) copy-start(f32[12,2]{1,0:T(8,128)} %constant.14.clone.moments) | copy-start | bytes 292
  10.4 3.2 %collective-permute-start.4 = (f32[11,32,128]{2,1,0:T(8,128)S(1)}, f32[11,32,128]{2,1,0:T(8,128)S(1)}, u32[]{:S(2)}, u32[]{:S(2)}) collective-permute-start(f32[11,32,128]{2,1,0:T(8,128)S(1)} %get-tuple-element.29), channel_id=1, source_target_pairs={{0,4},{4,0},{8,12},{12,8},{1,5},{5,1},{9,13},{13,9},{2,6},{6,2},{1... | collective-permute-start | bytes 540680 | tf_op jit(solution)/shard_map/ppermute | solution.py:70
  12.6 1.1 %collective-permute-start.5 = (f32[11,32,128]{2,1,0:T(8,128)S(1)}, f32[11,32,128]{2,1,0:T(8,128)S(1)}, u32[]{:S(2)}, u32[]{:S(2)}) collective-permute-start(f32[11,32,128]{2,1,0:T(8,128)S(1)} %get-tuple-element.30), channel_id=1, source_target_pairs={{4,8},{8,4},{5,9},{9,5},{6,10},{10,6},{7,11},{11,7},{20,24},{24,20... | collective-permute-start | bytes 540680 | tf_op jit(solution)/shard_map/ppermute | solution.py:70
  24.6 26.0 %collective-permute-start.6 = (f32[9,144,128]{2,1,0:T(8,128)S(1)}, f32[9,144,128]{2,1,0:T(8,128)S(1)}, u32[]{:S(2)}, u32[]{:S(2)}) collective-permute-start(f32[9,144,128]{2,1,0:T(8,128)S(1)} %get-tuple-element.35), channel_id=1, source_target_pairs={{0,4},{4,0},{8,12},{12,8},{1,5},{5,1},{9,13},{13,9},{2,6},{6,2},{1... | collective-permute-start | bytes 1990664 | tf_op jit(solution)/shard_map/ppermute | solution.py:70
  30.5 20.1 %collective-permute-start.7 = (f32[9,144,128]{2,1,0:T(8,128)S(1)}, f32[9,144,128]{2,1,0:T(8,128)S(1)}, u32[]{:S(2)}, u32[]{:S(2)}) collective-permute-start(f32[9,144,128]{2,1,0:T(8,128)S(1)} %get-tuple-element.36), channel_id=1, source_target_pairs={{4,8},{8,4},{5,9},{9,5},{6,10},{10,6},{7,11},{11,7},{20,24},{24,20... | collective-permute-start | bytes 1990664 | tf_op jit(solution)/shard_map/ppermute | solution.py:70
  31.2 8.9 %collective-permute-start.14 = (f32[4,104,128]{2,1,0:T(8,128)S(1)}, f32[4,104,128]{2,1,0:T(8,128)S(1)}, u32[]{:S(2)}, u32[]{:S(2)}) collective-permute-start(f32[4,104,128]{2,1,0:T(8,128)S(1)} %get-tuple-element.41.refs_4_), channel_id=1, source_target_pairs={{0,1},{1,2},{2,3},{3,0},{4,5},{5,6},{6,7},{7,4},{8,9},{9,10},{10,1... | collective-permute-start | bytes 638984 | tf_op jit(solution)/shard_map/ppermute | solution.py:75
  35.7 14.9 %collective-permute-start.15 = (f32[4,104,128]{2,1,0:T(8,128)S(1)}, f32[4,104,128]{2,1,0:T(8,128)S(1)}, u32[]{:S(2)}, u32[]{:S(2)}) collective-permute-start(f32[4,104,128]{2,1,0:T(8,128)S(1)} %get-tuple-element.41.refs_4_), channel_id=1, source_target_pairs={{0,2},{1,3},{2,0},{3,1},{4,6},{5,7},{6,4},{7,5},{8,10},{9,11},{10,... | collective-permute-start | bytes 638984 | tf_op jit(solution)/shard_map/ppermute | solution.py:75
  37.2 13.3 %collective-permute-start.16 = (f32[4,104,128]{2,1,0:T(8,128)S(1)}, f32[4,104,128]{2,1,0:T(8,128)S(1)}, u32[]{:S(2)}, u32[]{:S(2)}) collective-permute-start(f32[4,104,128]{2,1,0:T(8,128)S(1)} %get-tuple-element.41.refs_4_), channel_id=1, source_target_pairs={{0,3},{1,0},{2,1},{3,2},{4,7},{5,4},{6,5},{7,6},{8,11},{9,8},{10,9... | collective-permute-start | bytes 638984 | tf_op jit(solution)/shard_map/ppermute | solution.py:75
  50.6 22.8 %copy-start = (f32[4,128,256]{2,1,0:T(8,128)S(1)}, f32[4,128,256]{2,1,0:T(8,128)}, u32[]{:S(2)}) copy-start(f32[4,128,256]{2,1,0:T(8,128)} %constant.15.clone.refs_4_) | copy-start | bytes 1572868
  60.6 8.8 %collective-permute-start.10 = (f32[32,128]{1,0:T(8,128)S(1)}, f32[32,128]{1,0:T(8,128)S(1)}, u32[]{:S(2)}, u32[]{:S(2)}) collective-permute-start(f32[32,128]{1,0:T(8,128)S(1)} %get-tuple-element.37.refs_0_), channel_id=1, source_target_pairs={{0,3},{1,0},{2,1},{3,2},{4,7},{5,4},{6,5},{7,6},{8,11},{9,8},{10,9... | collective-permute-start | bytes 49160 | tf_op jit(solution)/shard_map/ppermute | solution.py:75
  67.9 5.5 %collective-permute-start.8 = (f32[32,128]{1,0:T(8,128)S(1)}, f32[32,128]{1,0:T(8,128)S(1)}, u32[]{:S(2)}, u32[]{:S(2)}) collective-permute-start(f32[32,128]{1,0:T(8,128)S(1)} %get-tuple-element.37.refs_0_), channel_id=1, source_target_pairs={{0,1},{1,2},{2,3},{3,0},{4,5},{5,6},{6,7},{7,4},{8,9},{9,10},{10,1... | collective-permute-start | bytes 49160 | tf_op jit(solution)/shard_map/ppermute | solution.py:75
  67.9 5.5 %collective-permute-start.9 = (f32[32,128]{1,0:T(8,128)S(1)}, f32[32,128]{1,0:T(8,128)S(1)}, u32[]{:S(2)}, u32[]{:S(2)}) collective-permute-start(f32[32,128]{1,0:T(8,128)S(1)} %get-tuple-element.37.refs_0_), channel_id=1, source_target_pairs={{0,2},{1,3},{2,0},{3,1},{4,6},{5,7},{6,4},{7,5},{8,10},{9,11},{10,... | collective-permute-start | bytes 49160 | tf_op jit(solution)/shard_map/ppermute | solution.py:75
  73.5 7.0 %copy-start.1 = (bf16[256,1024]{1,0:T(8,128)(2,1)S(1)}, bf16[256,1024]{1,0:T(8,128)(2,1)}, u32[]{:S(2)}) copy-start(bf16[256,1024]{1,0:T(8,128)(2,1)} %constant.17.clone.refs_9_) | copy-start | bytes 1572868
  73.5 7.0 %copy-start.2 = (bf16[16,32,192]{2,1,0:T(8,128)(2,1)S(1)}, bf16[16,32,192]{2,1,0:T(8,128)(2,1)}, u32[]{:S(2)}) copy-start(bf16[16,32,192]{2,1,0:T(8,128)(2,1)} %constant.18.clone.refs_10_) | copy-start | bytes 589828
  73.5 7.0 %copy-start.3 = (f32[224,32]{1,0:T(8,128)S(1)}, f32[224,32]{1,0:T(8,128)}, u32[]{:S(2)}) copy-start(f32[224,32]{1,0:T(8,128)} %constant.16.clone.refs_8_) | copy-start | bytes 86020
  74.4 4.8 %collective-permute-start.11 = (f32[16,256]{1,0:T(8,128)S(1)}, f32[16,256]{1,0:T(8,128)S(1)}, u32[]{:S(2)}, u32[]{:S(2)}) collective-permute-start(f32[16,256]{1,0:T(8,128)S(1)} %get-tuple-element.40.refs_0_), channel_id=1, source_target_pairs={{0,4},{4,8},{8,12},{12,0},{1,5},{5,9},{9,13},{13,1},{2,6},{6,10},{... | collective-permute-start | bytes 49160 | tf_op jit(solution)/shard_map/ppermute | solution.py:75
  74.8 4.6 %collective-permute-start.12 = (f32[16,256]{1,0:T(8,128)S(1)}, f32[16,256]{1,0:T(8,128)S(1)}, u32[]{:S(2)}, u32[]{:S(2)}) collective-permute-start(f32[16,256]{1,0:T(8,128)S(1)} %get-tuple-element.40.refs_0_), channel_id=1, source_target_pairs={{0,8},{4,12},{8,0},{12,4},{1,9},{5,13},{9,1},{13,5},{2,10},{6,14},... | collective-permute-start | bytes 49160 | tf_op jit(solution)/shard_map/ppermute | solution.py:75
  77.7 2.8 %collective-permute-start.13 = (f32[16,256]{1,0:T(8,128)S(1)}, f32[16,256]{1,0:T(8,128)S(1)}, u32[]{:S(2)}, u32[]{:S(2)}) collective-permute-start(f32[16,256]{1,0:T(8,128)S(1)} %get-tuple-element.40.refs_0_), channel_id=1, source_target_pairs={{0,12},{4,0},{8,4},{12,8},{1,13},{5,1},{9,5},{13,9},{2,14},{6,2},{... | collective-permute-start | bytes 49160 | tf_op jit(solution)/shard_map/ppermute | solution.py:75
  90.9 3.7 %collective-permute-start.17 = (f32[32,512]{1,0:T(8,128)S(1)}, f32[32,512]{1,0:T(8,128)S(1)}, u32[]{:S(2)}, u32[]{:S(2)}) collective-permute-start(f32[32,512]{1,0:T(8,128)S(1)} %get-tuple-element.43), channel_id=1, source_target_pairs={{0,4},{4,8},{8,12},{12,0},{1,5},{5,9},{9,13},{13,1},{2,6},{6,10},{... | collective-permute-start | bytes 196616 | tf_op jit(solution)/shard_map/ppermute | solution.py:75
  91.3 4.7 %collective-permute-start.18 = (f32[32,512]{1,0:T(8,128)S(1)}, f32[32,512]{1,0:T(8,128)S(1)}, u32[]{:S(2)}, u32[]{:S(2)}) collective-permute-start(f32[32,512]{1,0:T(8,128)S(1)} %get-tuple-element.44), channel_id=1, source_target_pairs={{0,8},{4,12},{8,0},{12,4},{1,9},{5,13},{9,1},{13,5},{2,10},{6,14},... | collective-permute-start | bytes 196616 | tf_op jit(solution)/shard_map/ppermute | solution.py:75
  93.0 3.0 %collective-permute-start.19 = (f32[32,512]{1,0:T(8,128)S(1)}, f32[32,512]{1,0:T(8,128)S(1)}, u32[]{:S(2)}, u32[]{:S(2)}) collective-permute-start(f32[32,512]{1,0:T(8,128)S(1)} %get-tuple-element.45), channel_id=1, source_target_pairs={{0,12},{4,0},{8,4},{12,8},{1,13},{5,1},{9,5},{13,9},{2,14},{6,2},{... | collective-permute-start | bytes 196616 | tf_op jit(solution)/shard_map/ppermute | solution.py:75

commit v3 on v2

--- a/solution.py
+++ b/solution.py
@@ -129,14 +129,13 @@
 
 
 def pack_kernel(
-    far_fields, far_map, shifts, weights, far_masks,
-    tile, send_a, send_b, send_c, send_d, source_pack,
-    fields, materials, masks, arrived, *, geo,
+    far_fields, far_map,
+    tile, send_a, send_b, send_c, send_d,
+    fields, materials, arrived, *, geo,
 ):
     copies = [
         pltpu.make_async_copy(far_fields, fields, arrived.at[0]),
         pltpu.make_async_copy(far_map, materials, arrived.at[1]),
-        pltpu.make_async_copy(far_masks, masks, arrived.at[2]),
     ]
     for copy in copies:
         copy.start()
@@ -176,12 +175,16 @@
         fill(send_a, False)
         fill(send_b, True)
 
+
+def source_kernel(masks, shifts, weights, source_pack, square):
     orders_p, orders_q = masks.shape[1:]
+    square[...] = jnp.zeros(square.shape, F32)
     source_pack[...] = jnp.zeros(source_pack.shape, F32)
     for source in range(masks.shape[0]):
-        source_pack[source, 0:orders_p, 0:orders_q] = masks[source].astype(F32)
+        square[0:orders_p, 0:orders_q] = masks[source].astype(F32)
+        source_pack[source, 0:orders_q, :] = square[...].T[0:orders_q, :]
         for at, fact in enumerate((shifts[0, source], shifts[1, source], weights[source])):
-            source_pack[source, orders_p : orders_p + 1, at : at + 1] = jnp.full((1, 1), fact).astype(F32)
+            source_pack[source, orders_q : orders_q + 1, at : at + 1] = jnp.full((1, 1), fact).astype(F32)
 
 
 def edge_kernel(got_c, got_d, send_a, send_b, *, geo):
@@ -475,68 +478,83 @@
     packs, refs = refs[:tiles_y], refs[tiles_y:]
     table_x, g_matrix, row_table, shifts, weights = refs[:5]
     strips, refs = refs[5 : 5 + tiles_x], refs[5 + tiles_x :]
-    gathered, orders, columns, rows, total = refs
+    gathered, orders, rows, turn, spread_a, spread_b, total = refs
     me_x = lax.axis_index("gx")
     me_y = lax.axis_index("gy")
-    width = orders.shape[2]
-    reach = orders.shape[1]
+    wide = orders.shape[2]
     for back, part in enumerate(parts):
         origin = pl.multiple_of((me_x - back + tiles_x) % tiles_x * cells_x, cells_x)
         for comp in range(2):
             gathered[comp, pl.ds(origin, cells_x), :] = part[comp * cells_x : (comp + 1) * cells_x, :]
     for comp in range(2):
-        re, im = gathered[comp, :, 0:width], gathered[comp, :, width : 2 * width]
+        re, im = gathered[comp, :, 0:wide], gathered[comp, :, wide : 2 * wide]
         dot = functools.partial(jnp.dot, precision=PRECISE, preferred_element_type=F32)
-        cos_x, sin_x = table_x[0:reach, :], table_x[reach : 2 * reach, :]
+        cos_x, sin_x = table_x[0:wide, :], table_x[wide : 2 * wide, :]
         order_re = dot(cos_x, re) + dot(sin_x, im)
         order_im = dot(cos_x, im) - dot(sin_x, re)
-        orders[2 * comp] = (order_re * scaling).astype(BF16).astype(F32)
-        orders[2 * comp + 1] = (order_im * scaling).astype(BF16).astype(F32)
-    strip = row_table.shape[1]
+        orders[2 * comp] = (order_re * scaling).astype(BF16).astype(F32).T
+        orders[2 * comp + 1] = (order_im * scaling).astype(BF16).astype(F32).T
+    strip = row_table.shape[2]
+    mine = tiles_x * strip
+    rows[...] = jnp.zeros(rows.shape, F32)
     for ahead in range(tiles_x):
         owner = (me_x + ahead) % tiles_x * tiles_y + me_y
-        rows[strip * ahead : strip * (ahead + 1), :] = row_table[owner]
-    pixels = g_matrix.shape[1] // 2
-    orders_p = rows.shape[1] // 2
+        for part in range(2):
+            rows[part, strip * ahead : strip * (ahead + 1), :] = row_table[part, owner]
+    cos_u, sin_u = rows[0].T, rows[1].T
+    turn[0:wide, 0:wide] = cos_u.astype(BF16)
+    turn[0:wide, wide : 2 * wide] = sin_u.astype(BF16)
+    turn[wide : 2 * wide, 0:wide] = (-sin_u).astype(BF16)
+    turn[wide : 2 * wide, wide : 2 * wide] = cos_u.astype(BF16)
+    pixels = g_matrix.shape[0] // 2
     local = packs[0].shape[0]
+    orders_q = packs[0].shape[1] - 8
+    count = local * tiles_y
+
+    def spread(number, pack, index, out):
+        down = shifts[number, 1] + REACH
+        across = wide - (shifts[number, 0] + REACH)
+        passed = pack[index, 0:orders_q, :]
+        masked = []
+        for plane in range(4):
+            window = orders[plane, pl.ds(down, orders_q), :]
+            value = pltpu.roll(window, across, 1) * passed
+            masked.append(jnp.concatenate((value, jnp.zeros((wide - orders_q, wide), F32)), 0).astype(BF16))
+        halves = jnp.concatenate(
+            (jnp.concatenate((masked[0], masked[2]), 1), jnp.concatenate((masked[1], masked[3]), 1)), 0
+        )
+        both = jnp.dot(g_matrix[...], halves, preferred_element_type=F32).astype(BF16)
+        for comp in range(2):
+            low = 2 * comp * wide
+            out[:, low : low + wide] = both[0:pixels, comp * wide : (comp + 1) * wide]
+            out[:, low + wide : low + 2 * wide] = both[pixels:, comp * wide : (comp + 1) * wide]
+
+    def expose(number, made):
+        bright = None
+        for comp in range(2):
+            low = 2 * comp * wide
+            value = jnp.dot(made[:, low : low + 2 * wide], turn[...], preferred_element_type=F32)
+            value = value * value
+            value = value[:, 0:wide] + value[:, wide : 2 * wide]
+            bright = value if bright is None else bright + value
+        total[...] = total[...] + (weights[number] / sources_all) * bright
+
     total[...] = jnp.zeros(total.shape, F32)
+    slots = (spread_a, spread_b)
+    spread(0, packs[0], 0, slots[0])
     for at, pack in enumerate(packs):
-
-        def source(index, carry, at=at, pack=pack):
+        following = packs[min(at + 1, tiles_y - 1)]
+        for index in range(local):
             number = at * local + index
-            down = shifts[number, 0] + REACH
-            across = width - (shifts[number, 1] + REACH)
-            passed = pack[index, 0:orders_p, :]
-            masked = []
-            for plane in range(4):
-                window = orders[plane, pl.ds(down, orders_p), :]
-                masked.append((pltpu.roll(window, across, 1) * passed).astype(BF16))
-            halves = jnp.concatenate(
-                (jnp.concatenate(masked[:2], 1), jnp.concatenate(masked[2:], 1)), 0
-            )
-            spread = jnp.dot(halves, g_matrix[...], preferred_element_type=F32).astype(BF16)
-            for comp in range(2):
-                part = spread[comp * orders_p : (comp + 1) * orders_p]
-                real, imag = part[:, :pixels], part[:, pixels:]
-                low = 2 * comp * pixels
-                columns[0:orders_p, low : low + pixels] = real
-                columns[0:orders_p, low + pixels : low + 2 * pixels] = imag
-                columns[orders_p : 2 * orders_p, low : low + pixels] = -imag
-                columns[orders_p : 2 * orders_p, low + pixels : low + 2 * pixels] = real
-            bright = None
-            for block in range(4):
-                value = jnp.dot(
-                    rows[...],
-                    columns[:, block * pixels : (block + 1) * pixels],
-                    preferred_element_type=F32,
-                )
-                bright = value * value if bright is None else bright + value * value
-            total[...] = total[...] + (weights[number] / sources_all) * bright
-            return carry
-
-        lax.fori_loop(0, local, source, 0)
-    for ahead in range(tiles_x):
-        strips[ahead][...] = total[strip * ahead : strip * (ahead + 1), :]
+            if number + 1 < count:
+                last = index + 1 == local
+                spread(number + 1, following if last else pack, 0 if last else index + 1, slots[(number + 1) % 2])
+            expose(number, slots[number % 2])
+    for block in range(pixels // wide):
+        turned = total[block * wide : (block + 1) * wide, :].T
+        for ahead in range(tiles_x):
+            strips[ahead][:, block * wide : (block + 1) * wide] = turned[strip * ahead : strip * (ahead + 1), :]
+    assert mine <= wide
 
 
 def body(
@@ -563,16 +581,14 @@
     row_shape = shape(sent, lanes, wide)
     side_shape = shape(PLANES + 1, geo.own, geo.pad, wide)
     edge_shape = shape(sent, 2 * geo.pad, wide)
-    tile, to_a, to_b, to_c, to_d, my_pack = call(
+    tile, to_a, to_b, to_c, to_d = call(
         functools.partial(pack_kernel, geo=geo),
-        [(flat_fields, "h"), (flat_map, "h"), (source_shift.T, "s"), (source_weight, "s"), (source_mask, "h")],
-        [shape(PLANES + 1, geo.own, lanes, wide), row_shape, row_shape, side_shape, side_shape]
-        + [shape(local, orders_p + 8, wide)],
+        [(flat_fields, "h"), (flat_map, "h")],
+        [shape(PLANES + 1, geo.own, lanes, wide), row_shape, row_shape, side_shape, side_shape],
         [
             pltpu.VMEM(flat_fields.shape, F32),
             pltpu.VMEM(flat_map.shape, jnp.int32),
-            pltpu.VMEM(source_mask.shape, jnp.int32),
-            pltpu.SemaphoreType.DMA((3,)),
+            pltpu.SemaphoreType.DMA((2,)),
         ],
     )
     got_c = swap(to_c, "gy", 0)
@@ -582,6 +598,12 @@
     to_a, to_b = call(functools.partial(edge_kernel, geo=geo), [(got_c, "v"), (got_d, "v")], [edge_shape, edge_shape])
     edge_a = swap(to_a, "gx", 0)
     edge_b = swap(to_b, "gx", 1)
+    (my_pack,) = call(
+        source_kernel,
+        [(source_mask, "c"), (source_shift.T, "s"), (source_weight, "s")],
+        [shape(local, orders_q + 8, wide)],
+        [pltpu.VMEM((wide, wide), F32)],
+    )
     packs = [my_pack]
     for by in range(1, tiles_y):
         packs.append(cyclic(my_pack, "gy", by))
@@ -607,9 +629,8 @@
         [*state, pltpu.VMEM((2, lanes, wide), F32)],
     )
 
-    reach = orders_p + 2 * REACH
-    ids_p = np.arange(-REACH, orders_p + REACH) % orders_p - orders_p // 2
-    ids_q = np.arange(-REACH, orders_q + REACH) % orders_q - orders_q // 2
+    ids_p = np.arange(-REACH, wide - REACH) % orders_p - orders_p // 2
+    ids_q = np.arange(-REACH, wide - REACH) % orders_q - orders_q // 2
     cos_y, sin_y = waves(ids_q, np.arange(total_y), total_y)
     table_y = np.zeros((total_y, 2 * wide), np.float32)
     table_y[:, : len(ids_q)] = cos_y.T
@@ -619,14 +640,15 @@
     pixels = M
     cos_u, sin_u = waves(np.arange(orders_p) - orders_p // 2, np.arange(pixels), pixels)
     strip = pixels // (tiles_x * tiles_y)
-    row_table = (np.concatenate((cos_u, sin_u), 0).T / math.sqrt(orders_p)).astype(np.float32)
-    row_table = row_table.reshape(tiles_x * tiles_y, strip, 2 * orders_p).astype(jnp.bfloat16)
+    row_table = np.zeros((2, tiles_x * tiles_y, strip, wide), np.float32)
+    row_table[0, :, :, :orders_p] = (cos_u.T / math.sqrt(orders_p)).reshape(-1, strip, orders_p)
+    row_table[1, :, :, :orders_p] = (sin_u.T / math.sqrt(orders_p)).reshape(-1, strip, orders_p)
     cos_v, sin_v = waves(np.arange(orders_q) - orders_q // 2, np.arange(pixels), pixels)
-    g_matrix = np.zeros((2 * wide, 2 * pixels), np.float32)
-    g_matrix[:orders_q, :pixels] = cos_v / math.sqrt(orders_q)
-    g_matrix[:orders_q, pixels:] = sin_v / math.sqrt(orders_q)
-    g_matrix[wide : wide + orders_q, :pixels] = -sin_v / math.sqrt(orders_q)
-    g_matrix[wide : wide + orders_q, pixels:] = cos_v / math.sqrt(orders_q)
+    g_matrix = np.zeros((2 * pixels, 2 * wide), np.float32)
+    g_matrix[:pixels, :orders_q] = cos_v.T / math.sqrt(orders_q)
+    g_matrix[pixels:, :orders_q] = sin_v.T / math.sqrt(orders_q)
+    g_matrix[:pixels, wide : wide + orders_q] = -sin_v.T / math.sqrt(orders_q)
+    g_matrix[pixels:, wide : wide + orders_q] = cos_v.T / math.sqrt(orders_q)
     g_matrix = g_matrix.astype(jnp.bfloat16)
 
     pieces = [phase] + [cyclic(phase, "gy", by) for by in range(1, tiles_y)]
@@ -639,7 +661,7 @@
     )
     parts = [part] + [cyclic(part, "gx", by) for by in range(1, tiles_x)]
 
-    facts = jnp.concatenate([pack[:, orders_p, 0:3] for pack in packs], 0)
+    facts = jnp.concatenate([pack[:, orders_q, 0:3] for pack in packs], 0)
     shifts = facts[:, 0:2].astype(jnp.int32)
     weights = facts[:, 2]
     strips = call(
@@ -658,10 +680,12 @@
         [shape(strip, pixels) for _ in range(tiles_x)],
         [
             pltpu.VMEM((2, total_x, 2 * wide), F32),
-            pltpu.VMEM((4, reach, wide), F32),
-            pltpu.VMEM((2 * orders_p, 4 * pixels), BF16),
-            pltpu.VMEM((tiles_x * strip, 2 * orders_p), BF16),
-            pltpu.VMEM((tiles_x * strip, pixels), F32),
+            pltpu.VMEM((4, wide, wide), F32),
+            pltpu.VMEM((2, wide, wide), F32),
+            pltpu.VMEM((2 * wide, 2 * wide), BF16),
+            pltpu.VMEM((pixels, 4 * wide), BF16),
+            pltpu.VMEM((pixels, 4 * wide), BF16),
+            pltpu.VMEM((pixels, wide), F32),
         ],
     )
     image = strips[0]

time: 96.9 us -> 92.3 us (0.953)
  Pallas kernels: 34.5 us -> 30.3 us
    pallas_call x6 -> x7, Pallas kernels: 34.5 us -> 30.3 us  [call(): pl.pallas_call(kernel, out_shape=outs, in_specs=[spaces[space]() for _, s...]
  transfers between devices with their start and end apart: 20 -> 20, of which waited for: 9 -> 9; matrix products, arithmetic and copies ran while one was open for 0% -> 0% of each run, Pallas kernels for 0% -> 1%
where the time goes in v3:
time: 92.3 us; the launch traced here: 92.1 us
  starting transfers between devices  38.1 us (41%)
  Pallas kernels  30.3 us (33%)
  waiting for transfers between devices  21.8 us (24%)
    pallas_call x7, Pallas kernels, call(): pl.pallas_call(kernel, out_shape=outs, in_specs=[spaces[space]() for _, s...  30.3 us
    ppermute x12, starting transfers between devices, cyclic(): lax.ppermute(values, axis, [(i, (i + by) % count) for i in range(count)])  23.9 us
    ppermute x12, waiting for transfers between devices, cyclic(): lax.ppermute(values, axis, [(i, (i + by) % count) for i in range(count)])  19.4 us
    ppermute x8, starting transfers between devices, swap(): return lax.ppermute(values, axis, pairs)  14.2 us
    ppermute x8, waiting for transfers between devices, swap(): return lax.ppermute(values, axis, pairs)  2.45 us
  transfers between devices with their start and end apart: 20, of which 9 were waited for; matrix products, arithmetic and copies ran while one was open for 0% of the time, Pallas kernels for 1%

profile of v3, /device:TPU:0, one launch (start us, length us, event | category | flops | bytes accessed | tf_op | source)
XLA Modules:
  0.0 92.1 jit_solution(17228944692303271359)
XLA Ops:
  0.6 1.6 %shard_map.131 = (f32[7,2,128,128]{3,2,1,0:T(8,128)S(1)}, f32[11,128,128]{2,1,0:T(8,128)S(1)}, f32[11,128,128]{2,1,0:T(8,128)S(1)}, f32[7,2,16,128]{3,2,1,0:T(8,128)S(1)}, f32[7,2,16,128]{3,2,1,0:T(8,128)S(1)}) custom-call(f32[6,256,128]{2,1,0:T(8,128)} %bitcast.13, s32[256,128]{1,0:T(8,128)} %bitcast.14), custom_call_target="tpu_custom_call" | custom-call | tf_op jit(solution)/shard_map/pallas_call | solution.py:49
  2.3 0.6 collective-permute-start
  2.8 0.7 collective-permute-start.1
  3.5 2.6 %collective-permute-start.2 = (f32[7,2,16,128]{3,2,1,0:T(8,128)S(1)}, f32[7,2,16,128]{3,2,1,0:T(8,128)S(1)}, u32[]{:S(2)}, u32[]{:S(2)}) collective-permute-start(f32[7,2,16,128]{3,2,1,0:T(8,128)S(1)} %get-tuple-element.26), channel_id=1, source_target_pairs={{0,1},{1,0},{2,3},{3,2},{4,5},{5,4},{6,7},{7,6},{8,9},{9,8},{10,11... | collective-permute-start | bytes 344072 | tf_op jit(solution)/shard_map/ppermute | solution.py:70
  6.2 0.7 collective-permute-start.3
  6.8 2.1 %collective-permute-done.2.got_c = f32[7,2,16,128]{3,2,1,0:T(8,128)S(1)} collective-permute-done((f32[7,2,16,128]{3,2,1,0:T(8,128)S(1)}, f32[7,2,16,128]{3,2,1,0:T(8,128)S(1)}, u32[]{:S(2)}, u32[]{:S(2)}) %collective-permute-start.2) | collective-permute-done | bytes 114720 | tf_op jit(solution)/shard_map/ppermute | solution.py:70
  9.1 2.2 %collective-permute-start.4 = (f32[11,32,128]{2,1,0:T(8,128)S(1)}, f32[11,32,128]{2,1,0:T(8,128)S(1)}, u32[]{:S(2)}, u32[]{:S(2)}) collective-permute-start(f32[11,32,128]{2,1,0:T(8,128)S(1)} %get-tuple-element.28), channel_id=1, source_target_pairs={{0,4},{4,0},{8,12},{12,8},{1,5},{5,1},{9,13},{13,9},{2,6},{6,2},{1... | collective-permute-start | bytes 540680 | tf_op jit(solution)/shard_map/ppermute | solution.py:70
  11.3 0.7 collective-permute-start.5
  12.0 0.3 collective-permute-done.4.edge_a
  12.4 10.9 %shard_map.133 = (f32[6,2,144,128]{3,2,1,0:T(8,128)S(1)}, f32[6,160,128]{2,1,0:T(8,128)S(1)}, f32[6,160,128]{2,1,0:T(8,128)S(1)}, f32[2,128,128]{2,1,0:T(8,128)S...) custom-call(f32[7,2,128,128]{3,2,1,0:T(8,128)S(1)} %get-tuple-element.23.tile, ...), custom_call_target="tpu_custom_call" | custom-call | tf_op jit(solution)/shard_map/pallas_call | solution.py:49
  23.2 5.9 %collective-permute-start.6 = (f32[9,144,128]{2,1,0:T(8,128)S(1)}, f32[9,144,128]{2,1,0:T(8,128)S(1)}, u32[]{:S(2)}, u32[]{:S(2)}) collective-permute-start(f32[9,144,128]{2,1,0:T(8,128)S(1)} %get-tuple-element.34), channel_id=1, source_target_pairs={{0,4},{4,0},{8,12},{12,8},{1,5},{5,1},{9,13},{13,9},{2,6},{6,2},{1... | collective-permute-start | bytes 1990664 | tf_op jit(solution)/shard_map/ppermute | solution.py:70
  29.2 0.8 collective-permute-start.7
  30.0 0.7 shard_map.136.refs_4_
  30.7 4.5 %collective-permute-start.14 = (f32[4,104,128]{2,1,0:T(8,128)S(1)}, f32[4,104,128]{2,1,0:T(8,128)S(1)}, u32[]{:S(2)}, u32[]{:S(2)}) collective-permute-start(f32[4,104,128]{2,1,0:T(8,128)S(1)} %shard_map.136.refs_4_), channel_id=1, source_target_pairs={{0,1},{1,2},{2,3},{3,0},{4,5},{5,6},{6,7},{7,4},{8,9},{9,10},{10,1... | collective-permute-start | bytes 638984 | tf_op jit(solution)/shard_map/ppermute | solution.py:75
  35.2 1.5 %collective-permute-start.15 = (f32[4,104,128]{2,1,0:T(8,128)S(1)}, f32[4,104,128]{2,1,0:T(8,128)S(1)}, u32[]{:S(2)}, u32[]{:S(2)}) collective-permute-start(f32[4,104,128]{2,1,0:T(8,128)S(1)} %shard_map.136.refs_4_), channel_id=1, source_target_pairs={{0,2},{1,3},{2,0},{3,1},{4,6},{5,7},{6,4},{7,5},{8,10},{9,11},{10,... | collective-permute-start | bytes 638984 | tf_op jit(solution)/shard_map/ppermute | solution.py:75
  36.7 2.8 %collective-permute-start.16 = (f32[4,104,128]{2,1,0:T(8,128)S(1)}, f32[4,104,128]{2,1,0:T(8,128)S(1)}, u32[]{:S(2)}, u32[]{:S(2)}) collective-permute-start(f32[4,104,128]{2,1,0:T(8,128)S(1)} %shard_map.136.refs_4_), channel_id=1, source_target_pairs={{0,3},{1,0},{2,1},{3,2},{4,7},{5,4},{6,5},{7,6},{8,11},{9,8},{10,9... | collective-permute-start | bytes 638984 | tf_op jit(solution)/shard_map/ppermute | solution.py:75
  39.6 10.5 %collective-permute-done.15.refs_6_ = f32[4,104,128]{2,1,0:T(8,128)S(1)} collective-permute-done((f32[4,104,128]{2,1,0:T(8,128)S(1)}, f32[4,104,128]{2,1,0:T(8,128)S(1)}, u32[]{:S(2)}, u32[]{:S(2)}) %collective-permute-start.15) | collective-permute-done | bytes 213024 | tf_op jit(solution)/shard_map/ppermute | solution.py:75
  50.1 9.9 %shard_map.134 = (f32[6,256,128]{2,1,0:T(8,128)S(1)}, f32[32,128]{1,0:T(8,128)S(1)}) custom-call(f32[6,2,144,128]{3,2,1,0:T(8,128)S(1)} %get-tuple-element.30.own, f32[6,160,128]{2,1,0:T(8,128)S(1)} %get-tuple-element.31.keep, f32[6,160,128]{2,1,0:T(8,128)S(1)} %get-tuple-element.32.curl, f32[2,128,128]{2,1,0:T(8,128)S(1)} %get-tuple-element.33.phase_in, ...), custom_call_target="tpu_custom_call" | custom-call | tf_op jit(solution)/shard_map/pallas_call | solution.py:49
  60.1 7.4 %collective-permute-start.10 = (f32[32,128]{1,0:T(8,128)S(1)}, f32[32,128]{1,0:T(8,128)S(1)}, u32[]{:S(2)}, u32[]{:S(2)}) collective-permute-start(f32[32,128]{1,0:T(8,128)S(1)} %get-tuple-element.36.refs_0_), channel_id=1, source_target_pairs={{0,3},{1,0},{2,1},{3,2},{4,7},{5,4},{6,5},{7,6},{8,11},{9,8},{10,9... | collective-permute-start | bytes 49160 | tf_op jit(solution)/shard_map/ppermute | solution.py:75
  67.5 0.6 collective-permute-start.9
  68.2 0.8 collective-permute-done.10.refs_3_
  69.0 4.1 %collective-permute-done.8.refs_1_ = f32[32,128]{1,0:T(8,128)S(1)} collective-permute-done((f32[32,128]{1,0:T(8,128)S(1)}, f32[32,128]{1,0:T(8,128)S(1)}, u32[]{:S(2)}, u32[]{:S(2)}) %collective-permute-start.8) | collective-permute-done | bytes 16416 | tf_op jit(solution)/shard_map/ppermute | solution.py:75
  73.1 0.9 shard_map.135
  74.3 2.9 %collective-permute-start.12 = (f32[16,256]{1,0:T(8,128)S(1)}, f32[16,256]{1,0:T(8,128)S(1)}, u32[]{:S(2)}, u32[]{:S(2)}) collective-permute-start(f32[16,256]{1,0:T(8,128)S(1)} %get-tuple-element.39.refs_0_), channel_id=1, source_target_pairs={{0,8},{4,12},{8,0},{12,4},{1,9},{5,13},{9,1},{13,5},{2,10},{6,14},... | collective-permute-start | bytes 49160 | tf_op jit(solution)/shard_map/ppermute | solution.py:75
  77.2 1.4 %collective-permute-start.13 = (f32[16,256]{1,0:T(8,128)S(1)}, f32[16,256]{1,0:T(8,128)S(1)}, u32[]{:S(2)}, u32[]{:S(2)}) collective-permute-start(f32[16,256]{1,0:T(8,128)S(1)} %get-tuple-element.39.refs_0_), channel_id=1, source_target_pairs={{0,12},{4,0},{8,4},{12,8},{1,13},{5,1},{9,5},{13,9},{2,14},{6,2},{... | collective-permute-start | bytes 49160 | tf_op jit(solution)/shard_map/ppermute | solution.py:75
  78.9 1.1 %collective-permute-done.13.refs_3_ = f32[16,256]{1,0:T(8,128)S(1)} collective-permute-done((f32[16,256]{1,0:T(8,128)S(1)}, f32[16,256]{1,0:T(8,128)S(1)}, u32[]{:S(2)}, u32[]{:S(2)}) %collective-permute-start.13) | collective-permute-done | bytes 16416 | tf_op jit(solution)/shard_map/ppermute | solution.py:75
  80.0 6.2 %shard_map.137 = (f32[32,512]{1,0:T(8,128)S(1)}, f32[32,512]{1,0:T(8,128)S(1)}, f32[32,512]{1,0:T(8,128)S(1)}, f32[32,512]{1,0:T(8,128)S(1)}) custom-call(f32[16,256]{1,0:T(8,128)S(1)} %get-tuple-element.39.refs_0_, f32[16,256]{1,0:T(8,128)S(1)} %collective-permute-done.11.refs_1_, f32[16,256]{1,0:T(8,128)S(1)} %collective-permute-done.12.refs_2_, ...), custom_call_target="tpu_custom_call" | custom-call | tf_op jit(solution)/shard_map/pallas_call | solution.py:49
  86.3 0.4 collective-permute-start.17
  86.7 1.8 %collective-permute-start.18 = (f32[32,512]{1,0:T(8,128)S(1)}, f32[32,512]{1,0:T(8,128)S(1)}, u32[]{:S(2)}, u32[]{:S(2)}) collective-permute-start(f32[32,512]{1,0:T(8,128)S(1)} %get-tuple-element.42), channel_id=1, source_target_pairs={{0,8},{4,12},{8,0},{12,4},{1,9},{5,13},{9,1},{13,5},{2,10},{6,14},... | collective-permute-start | bytes 196616 | tf_op jit(solution)/shard_map/ppermute | solution.py:75
  88.7 1.3 %collective-permute-done.17 = f32[32,512]{1,0:T(8,128)S(1)} collective-permute-done((f32[32,512]{1,0:T(8,128)S(1)}, f32[32,512]{1,0:T(8,128)S(1)}, u32[]{:S(2)}, u32[]{:S(2)}) %collective-permute-start.17) | collective-permute-done | bytes 65568 | tf_op jit(solution)/shard_map/ppermute | solution.py:75
  90.0 1.4 %collective-permute-done.18 = f32[32,512]{1,0:T(8,128)S(1)} collective-permute-done((f32[32,512]{1,0:T(8,128)S(1)}, f32[32,512]{1,0:T(8,128)S(1)}, u32[]{:S(2)}, u32[]{:S(2)}) %collective-permute-start.18) | collective-permute-done | bytes 65568 | tf_op jit(solution)/shard_map/ppermute | solution.py:75
  91.4 0.6 add_add_fusion
  (45 shorter events, 1.1 us)
Async XLA Ops:
  2.3 10.1 %collective-permute-start = (f32[11,128,128]{2,1,0:T(8,128)S(1)}, f32[11,128,128]{2,1,0:T(8,128)S(1)}, u32[]{:S(2)}, u32[]{:S(2)}) collective-permute-start(f32[11,128,128]{2,1,0:T(8,128)S(1)} %get-tuple-element.24), channel_id=1, source_target_pairs={{0,4},{4,0},{8,12},{12,8},{1,5},{5,1},{9,13},{13,9},{2,6},{6,2},{1... | collective-permute-start | bytes 2162696 | tf_op jit(solution)/shard_map/ppermute | solution.py:70
  2.8 9.5 %collective-permute-start.1 = (f32[11,128,128]{2,1,0:T(8,128)S(1)}, f32[11,128,128]{2,1,0:T(8,128)S(1)}, u32[]{:S(2)}, u32[]{:S(2)}) collective-permute-start(f32[11,128,128]{2,1,0:T(8,128)S(1)} %get-tuple-element.25), channel_id=1, source_target_pairs={{4,8},{8,4},{5,9},{9,5},{6,10},{10,6},{7,11},{11,7},{20,24},{24,20... | collective-permute-start | bytes 2162696 | tf_op jit(solution)/shard_map/ppermute | solution.py:70
  3.5 5.4 %collective-permute-start.2 = (f32[7,2,16,128]{3,2,1,0:T(8,128)S(1)}, f32[7,2,16,128]{3,2,1,0:T(8,128)S(1)}, u32[]{:S(2)}, u32[]{:S(2)}) collective-permute-start(f32[7,2,16,128]{3,2,1,0:T(8,128)S(1)} %get-tuple-element.26), channel_id=1, source_target_pairs={{0,1},{1,0},{2,3},{3,2},{4,5},{5,4},{6,7},{7,6},{8,9},{9,8},{10,11... | collective-permute-start | bytes 344072 | tf_op jit(solution)/shard_map/ppermute | solution.py:70
  6.2 2.8 %collective-permute-start.3 = (f32[7,2,16,128]{3,2,1,0:T(8,128)S(1)}, f32[7,2,16,128]{3,2,1,0:T(8,128)S(1)}, u32[]{:S(2)}, u32[]{:S(2)}) collective-permute-start(f32[7,2,16,128]{3,2,1,0:T(8,128)S(1)} %get-tuple-element.27), channel_id=1, source_target_pairs={{1,2},{2,1},{5,6},{6,5},{9,10},{10,9},{13,14},{14,13},{17,18},{18,... | collective-permute-start | bytes 344072 | tf_op jit(solution)/shard_map/ppermute | solution.py:70
  8.9 3.0 %copy-start.8 = (f32[4]{0:T(128)S(1)}, f32[4]{0:T(128)}, u32[]{:S(2)}) copy-start(f32[4]{0:T(128)} %param.15) | copy-start | bytes 52
  8.9 3.0 %copy-start.9 = (f32[4]{0:T(128)S(1)}, f32[4]{0:T(128)}, u32[]{:S(2)}) copy-start(f32[4]{0:T(128)} %param.14) | copy-start | bytes 52
  9.1 3.3 %copy-start.5 = (f32[12,2]{1,0:T(8,128)S(1)}, f32[12,2]{1,0:T(8,128)}, u32[]{:S(2)}) copy-start(f32[12,2]{1,0:T(8,128)} %constant.14.clone.moments) | copy-start | bytes 292
  9.1 3.2 %collective-permute-start.4 = (f32[11,32,128]{2,1,0:T(8,128)S(1)}, f32[11,32,128]{2,1,0:T(8,128)S(1)}, u32[]{:S(2)}, u32[]{:S(2)}) collective-permute-start(f32[11,32,128]{2,1,0:T(8,128)S(1)} %get-tuple-element.28), channel_id=1, source_target_pairs={{0,4},{4,0},{8,12},{12,8},{1,5},{5,1},{9,13},{13,9},{2,6},{6,2},{1... | collective-permute-start | bytes 540680 | tf_op jit(solution)/shard_map/ppermute | solution.py:70
  11.3 1.1 %collective-permute-start.5 = (f32[11,32,128]{2,1,0:T(8,128)S(1)}, f32[11,32,128]{2,1,0:T(8,128)S(1)}, u32[]{:S(2)}, u32[]{:S(2)}) collective-permute-start(f32[11,32,128]{2,1,0:T(8,128)S(1)} %get-tuple-element.29), channel_id=1, source_target_pairs={{4,8},{8,4},{5,9},{9,5},{6,10},{10,6},{7,11},{11,7},{20,24},{24,20... | collective-permute-start | bytes 540680 | tf_op jit(solution)/shard_map/ppermute | solution.py:70
  12.3 17.6 %copy-start.3 = (s32[4,96,96]{2,1,0:T(8,128)S(1)}, s32[4,96,96]{2,1,0:T(8,128)}, u32[]{:S(2)}) copy-start(s32[4,96,96]{2,1,0:T(8,128)} %masks.1) | copy-start | bytes 442372
  23.2 26.9 %collective-permute-start.6 = (f32[9,144,128]{2,1,0:T(8,128)S(1)}, f32[9,144,128]{2,1,0:T(8,128)S(1)}, u32[]{:S(2)}, u32[]{:S(2)}) collective-permute-start(f32[9,144,128]{2,1,0:T(8,128)S(1)} %get-tuple-element.34), channel_id=1, source_target_pairs={{0,4},{4,0},{8,12},{12,8},{1,5},{5,1},{9,13},{13,9},{2,6},{6,2},{1... | collective-permute-start | bytes 1990664 | tf_op jit(solution)/shard_map/ppermute | solution.py:70
  29.1 0.8 copy-start.6
  29.2 0.9 copy-start.7
  29.2 21.0 %collective-permute-start.7 = (f32[9,144,128]{2,1,0:T(8,128)S(1)}, f32[9,144,128]{2,1,0:T(8,128)S(1)}, u32[]{:S(2)}, u32[]{:S(2)}) collective-permute-start(f32[9,144,128]{2,1,0:T(8,128)S(1)} %get-tuple-element.35), channel_id=1, source_target_pairs={{4,8},{8,4},{5,9},{9,5},{6,10},{10,6},{7,11},{11,7},{20,24},{24,20... | collective-permute-start | bytes 1990664 | tf_op jit(solution)/shard_map/ppermute | solution.py:70
  30.7 8.9 %collective-permute-start.14 = (f32[4,104,128]{2,1,0:T(8,128)S(1)}, f32[4,104,128]{2,1,0:T(8,128)S(1)}, u32[]{:S(2)}, u32[]{:S(2)}) collective-permute-start(f32[4,104,128]{2,1,0:T(8,128)S(1)} %shard_map.136.refs_4_), channel_id=1, source_target_pairs={{0,1},{1,2},{2,3},{3,0},{4,5},{5,6},{6,7},{7,4},{8,9},{9,10},{10,1... | collective-permute-start | bytes 638984 | tf_op jit(solution)/shard_map/ppermute | solution.py:75
  35.2 14.9 %collective-permute-start.15 = (f32[4,104,128]{2,1,0:T(8,128)S(1)}, f32[4,104,128]{2,1,0:T(8,128)S(1)}, u32[]{:S(2)}, u32[]{:S(2)}) collective-permute-start(f32[4,104,128]{2,1,0:T(8,128)S(1)} %shard_map.136.refs_4_), channel_id=1, source_target_pairs={{0,2},{1,3},{2,0},{3,1},{4,6},{5,7},{6,4},{7,5},{8,10},{9,11},{10,... | collective-permute-start | bytes 638984 | tf_op jit(solution)/shard_map/ppermute | solution.py:75
  36.7 13.3 %collective-permute-start.16 = (f32[4,104,128]{2,1,0:T(8,128)S(1)}, f32[4,104,128]{2,1,0:T(8,128)S(1)}, u32[]{:S(2)}, u32[]{:S(2)}) collective-permute-start(f32[4,104,128]{2,1,0:T(8,128)S(1)} %shard_map.136.refs_4_), channel_id=1, source_target_pairs={{0,3},{1,0},{2,1},{3,2},{4,7},{5,4},{6,5},{7,6},{8,11},{9,8},{10,9... | collective-permute-start | bytes 638984 | tf_op jit(solution)/shard_map/ppermute | solution.py:75
  50.1 23.0 %copy-start.2 = (f32[4,128,256]{2,1,0:T(8,128)S(1)}, f32[4,128,256]{2,1,0:T(8,128)}, u32[]{:S(2)}) copy-start(f32[4,128,256]{2,1,0:T(8,128)} %constant.15.clone.refs_4_) | copy-start | bytes 1572868
  60.1 8.9 %collective-permute-start.10 = (f32[32,128]{1,0:T(8,128)S(1)}, f32[32,128]{1,0:T(8,128)S(1)}, u32[]{:S(2)}, u32[]{:S(2)}) collective-permute-start(f32[32,128]{1,0:T(8,128)S(1)} %get-tuple-element.36.refs_0_), channel_id=1, source_target_pairs={{0,3},{1,0},{2,1},{3,2},{4,7},{5,4},{6,5},{7,6},{8,11},{9,8},{10,9... | collective-permute-start | bytes 49160 | tf_op jit(solution)/shard_map/ppermute | solution.py:75
  67.5 5.5 %collective-permute-start.8 = (f32[32,128]{1,0:T(8,128)S(1)}, f32[32,128]{1,0:T(8,128)S(1)}, u32[]{:S(2)}, u32[]{:S(2)}) collective-permute-start(f32[32,128]{1,0:T(8,128)S(1)} %get-tuple-element.36.refs_0_), channel_id=1, source_target_pairs={{0,1},{1,2},{2,3},{3,0},{4,5},{5,6},{6,7},{7,4},{8,9},{9,10},{10,1... | collective-permute-start | bytes 49160 | tf_op jit(solution)/shard_map/ppermute | solution.py:75
  67.5 5.5 %collective-permute-start.9 = (f32[32,128]{1,0:T(8,128)S(1)}, f32[32,128]{1,0:T(8,128)S(1)}, u32[]{:S(2)}, u32[]{:S(2)}) collective-permute-start(f32[32,128]{1,0:T(8,128)S(1)} %get-tuple-element.36.refs_0_), channel_id=1, source_target_pairs={{0,2},{1,3},{2,0},{3,1},{4,6},{5,7},{6,4},{7,5},{8,10},{9,11},{10,... | collective-permute-start | bytes 49160 | tf_op jit(solution)/shard_map/ppermute | solution.py:75
  73.1 6.9 %copy-start = (bf16[1024,256]{1,0:T(8,128)(2,1)S(1)}, bf16[1024,256]{1,0:T(8,128)(2,1)}, u32[]{:S(2)}) copy-start(bf16[1024,256]{1,0:T(8,128)(2,1)} %constant.17.clone.refs_9_) | copy-start | bytes 1572868
  73.1 6.9 %copy-start.1 = (f32[2,16,32,128]{3,2,1,0:T(8,128)S(1)}, f32[2,16,32,128]{3,2,1,0:T(8,128)}, u32[]{:S(2)}) copy-start(f32[2,16,32,128]{3,2,1,0:T(8,128)} %constant.18.clone.refs_10_) | copy-start | bytes 1572868
  73.1 6.9 %copy-start.4 = (f32[256,32]{1,0:T(8,128)S(1)}, f32[256,32]{1,0:T(8,128)}, u32[]{:S(2)}) copy-start(f32[256,32]{1,0:T(8,128)} %constant.16.clone.refs_8_) | copy-start | bytes 98308
  74.0 4.7 %collective-permute-start.11 = (f32[16,256]{1,0:T(8,128)S(1)}, f32[16,256]{1,0:T(8,128)S(1)}, u32[]{:S(2)}, u32[]{:S(2)}) collective-permute-start(f32[16,256]{1,0:T(8,128)S(1)} %get-tuple-element.39.refs_0_), channel_id=1, source_target_pairs={{0,4},{4,8},{8,12},{12,0},{1,5},{5,9},{9,13},{13,1},{2,6},{6,10},{... | collective-permute-start | bytes 49160 | tf_op jit(solution)/shard_map/ppermute | solution.py:75
  74.3 4.6 %collective-permute-start.12 = (f32[16,256]{1,0:T(8,128)S(1)}, f32[16,256]{1,0:T(8,128)S(1)}, u32[]{:S(2)}, u32[]{:S(2)}) collective-permute-start(f32[16,256]{1,0:T(8,128)S(1)} %get-tuple-element.39.refs_0_), channel_id=1, source_target_pairs={{0,8},{4,12},{8,0},{12,4},{1,9},{5,13},{9,1},{13,5},{2,10},{6,14},... | collective-permute-start | bytes 49160 | tf_op jit(solution)/shard_map/ppermute | solution.py:75
  77.2 2.8 %collective-permute-start.13 = (f32[16,256]{1,0:T(8,128)S(1)}, f32[16,256]{1,0:T(8,128)S(1)}, u32[]{:S(2)}, u32[]{:S(2)}) collective-permute-start(f32[16,256]{1,0:T(8,128)S(1)} %get-tuple-element.39.refs_0_), channel_id=1, source_target_pairs={{0,12},{4,0},{8,4},{12,8},{1,13},{5,1},{9,5},{13,9},{2,14},{6,2},{... | collective-permute-start | bytes 49160 | tf_op jit(solution)/shard_map/ppermute | solution.py:75
  86.3 3.8 %collective-permute-start.17 = (f32[32,512]{1,0:T(8,128)S(1)}, f32[32,512]{1,0:T(8,128)S(1)}, u32[]{:S(2)}, u32[]{:S(2)}) collective-permute-start(f32[32,512]{1,0:T(8,128)S(1)} %get-tuple-element.41), channel_id=1, source_target_pairs={{0,4},{4,8},{8,12},{12,0},{1,5},{5,9},{9,13},{13,1},{2,6},{6,10},{... | collective-permute-start | bytes 196616 | tf_op jit(solution)/shard_map/ppermute | solution.py:75
  86.7 4.7 %collective-permute-start.18 = (f32[32,512]{1,0:T(8,128)S(1)}, f32[32,512]{1,0:T(8,128)S(1)}, u32[]{:S(2)}, u32[]{:S(2)}) collective-permute-start(f32[32,512]{1,0:T(8,128)S(1)} %get-tuple-element.42), channel_id=1, source_target_pairs={{0,8},{4,12},{8,0},{12,4},{1,9},{5,13},{9,1},{13,5},{2,10},{6,14},... | collective-permute-start | bytes 196616 | tf_op jit(solution)/shard_map/ppermute | solution.py:75
  88.5 3.0 %collective-permute-start.19 = (f32[32,512]{1,0:T(8,128)S(1)}, f32[32,512]{1,0:T(8,128)S(1)}, u32[]{:S(2)}, u32[]{:S(2)}) collective-permute-start(f32[32,512]{1,0:T(8,128)S(1)} %get-tuple-element.43), channel_id=1, source_target_pairs={{0,12},{4,0},{8,4},{12,8},{1,13},{5,1},{9,5},{13,9},{2,14},{6,2},{... | collective-permute-start | bytes 196616 | tf_op jit(solution)/shard_map/ppermute | solution.py:75

commit v4 on v3

--- a/solution.py
+++ b/solution.py
@@ -10,7 +10,6 @@
 from jax.sharding import PartitionSpec as P
 
 STEPS = 12
-ROUNDS = 2
 M = 512
 REACH = 8
 
@@ -82,9 +81,9 @@
 
 
 class Geo:
-    def __init__(self, depth, cells_x, cells_y, total_x, total_y, count):
+    def __init__(self, depth, cells_x, cells_y, total_x, total_y):
         self.depth, self.cells_x, self.cells_y = depth, cells_x, cells_y
-        self.total_x, self.total_y, self.count = total_x, total_y, count
+        self.total_x, self.total_y = total_x, total_y
         self.wide = 128
         self.per = self.wide // depth
         self.own = cells_x // self.per
@@ -93,44 +92,25 @@
         self.slack = 8
         self.first = self.slack + self.pad
         self.rows = cells_y + 2 * self.first
-        self.half = self.wide // 2
         self.reach = 8
+        self.counts = (min(cells_x, STEPS), max(STEPS - cells_x, 0))
         assert self.per * depth == self.wide and self.own == 2 and cells_x == 2 * self.per
-        assert self.per + self.per // 2 == count and STEPS <= self.pad and STEPS - count <= self.reach
+        assert self.counts[1] <= min(self.per, self.reach) and STEPS <= self.pad
+
+    def plane(self):
+        return pltpu.VMEM(((self.groups + 4) * self.rows, self.wide), F32)
+
+    def at(self, group, row, count):
+        return pl.ds(pl.multiple_of((group + 2) * self.rows, 8) + row, count)
 
 
 PLANES = 6
 SCALE = 1.0 / COURANT
 
 
-def halves_of(planes):
-    return (planes + 1) // 2
-
-
-def pack_rows(get, put, planes, upper, lane, half):
-    for plane in range(planes):
-        put(plane, get(plane, 1 if upper else 0))
-    kept = (lane >= half) if upper else (lane < half)
-    group = 0 if upper else 1
-    for at in range(halves_of(planes)):
-        value = get(2 * at, group)
-        if 2 * at + 1 < planes:
-            value = jnp.where(kept, value, pltpu.roll(get(2 * at + 1, group), half, 1))
-        put(planes + at, value)
-
-
-def unpack_rows(get, put, planes, inner, outer, kept, half):
-    for plane in range(planes):
-        put(plane, inner, get(plane))
-        value = get(planes + plane // 2)
-        if plane % 2:
-            value = pltpu.roll(value, half, 1)
-        put(plane, outer, jnp.where(kept, value, 0.0))
-
-
 def pack_kernel(
     far_fields, far_map,
-    tile, send_a, send_b, send_c, send_d,
+    tile, send_c, send_d,
     fields, materials, arrived, *, geo,
 ):
     copies = [
@@ -141,7 +121,6 @@
         copy.start()
     for copy in copies:
         copy.wait()
-    even_x = lax.axis_index("gx") % 2 == 0
     even_y = lax.axis_index("gy") % 2 == 0
     pad, last = geo.pad, geo.cells_y - geo.pad
     for plane in range(PLANES + 1):
@@ -157,23 +136,6 @@
             low, high = values[0:pad], values[last:]
             send_c[plane, group] = jnp.where(even_y, high, low)
             send_d[plane, group] = jnp.where(even_y, low, high)
-    lane = lax.broadcasted_iota(jnp.int32, (geo.cells_y, geo.wide), 1)
-
-    def fill(send, upper):
-        def put(at, value):
-            send[at] = value
-
-        pack_rows(lambda plane, group: tile[plane, group], put, PLANES + 1, upper, lane, geo.half)
-
-    @pl.when(even_x)
-    def _():
-        fill(send_a, True)
-        fill(send_b, False)
-
-    @pl.when(jnp.logical_not(even_x))
-    def _():
-        fill(send_a, False)
-        fill(send_b, True)
 
 
 def source_kernel(masks, shifts, weights, source_pack, square):
@@ -187,49 +149,28 @@
             source_pack[source, orders_q : orders_q + 1, at : at + 1] = jnp.full((1, 1), fact).astype(F32)
 
 
-def edge_kernel(got_c, got_d, send_a, send_b, *, geo):
-    even_x = lax.axis_index("gx") % 2 == 0
+def edge_kernel(got_c, got_d, edges, *, geo):
     even_y = lax.axis_index("gy") % 2 == 0
-    lane = lax.broadcasted_iota(jnp.int32, (geo.pad, geo.wide), 1)
-
-    def fill(send, upper):
-        for side in range(2):
-
-            def get(plane, group, side=side):
-                c_value, d_value = got_c[plane, group], got_d[plane, group]
-                if side:
-                    return jnp.where(even_y, c_value, d_value)
-                return jnp.where(even_y, d_value, c_value)
-
-            def put(at, value, side=side):
-                send[at, side * geo.pad : (side + 1) * geo.pad, :] = value
-
-            pack_rows(get, put, PLANES + 1, upper, lane, geo.half)
-
-    @pl.when(even_x)
-    def _():
-        fill(send_a, True)
-        fill(send_b, False)
-
-    @pl.when(jnp.logical_not(even_x))
-    def _():
-        fill(send_a, False)
-        fill(send_b, True)
-
-
-def run_steps(state, keep, curl, phase, moments, first_step, geo):
-    ex, ey, ez, hx, hy, hz = state
-    wide, depth, groups = geo.wide, geo.depth, geo.groups
+    for plane in range(PLANES + 1):
+        for group in range(geo.own):
+            c_value, d_value = got_c[plane, group], got_d[plane, group]
+            edges[plane, group, 0 : geo.pad] = jnp.where(even_y, d_value, c_value)
+            edges[plane, group, geo.pad : 2 * geo.pad] = jnp.where(even_y, c_value, d_value)
+
+
+def run_steps(state, keep, curl, phase, moments, first_step, count, beyond, geo):
+    ex, ey, _, _, hy, hz = state
+    wide, depth, rows = geo.wide, geo.depth, geo.rows
     first = geo.first
     chunk = 16
-    beyond = geo.pad if first_step == 0 else geo.reach
     starts = range(first - beyond, first + geo.cells_y + beyond, chunk)
     lane = lax.broadcasted_iota(jnp.int32, (chunk, wide), 1)
+    row = lax.broadcasted_iota(jnp.int32, (chunk, wide), 0)
     level = lane % depth
     at_top, at_bottom = level == depth - 1, level == 0
     not_first, not_last = lane >= depth, lane < wide - depth
     low_x = lax.axis_index("gx") == 0
-    low_y = lax.axis_index("gy") == 0
+    open_y = jnp.where(lax.axis_index("gy") == 0, 0.0, 1.0)
 
     def next_z(values):
         return jnp.where(at_top, 0.0, pltpu.roll(values, wide - 1, 1))
@@ -237,92 +178,80 @@
     def last_z(values):
         return jnp.where(at_bottom, 0.0, pltpu.roll(values, 1, 1))
 
+    def gated(values, start):
+        if start <= first - 1 < start + chunk:
+            return values * jnp.where(row == first - 1 - start, open_y, 1.0)
+        return values
+
     def magnetic(g, carry):
-        after = jnp.minimum(g + 1, groups - 1)
+        base = pl.multiple_of((g + 2) * rows, 8)
+        ex, ey, ez, hx, hy, hz = [field.at[pl.ds(base, 2 * rows), :] for field in state]
         for start in starts:
             here, ahead = pl.ds(start, chunk), pl.ds(start + 1, chunk)
-            x, y, z = ex[g, here, :], ey[g, here, :], ez[g, here, :]
-            y_x = pltpu.roll(jnp.where(not_first, y, ey[after, here, :]), wide - depth, 1)
-            z_x = pltpu.roll(jnp.where(not_first, z, ez[after, here, :]), wide - depth, 1)
-            hx[g, here, :] = hx[g, here, :] - ((ez[g, ahead, :] - z) - (next_z(y) - y))
-            hy[g, here, :] = hy[g, here, :] - ((next_z(x) - x) - (z_x - z))
-            hz[g, here, :] = hz[g, here, :] - ((y_x - y) - (ex[g, ahead, :] - x))
+            over = pl.ds(rows + start, chunk)
+            x, y, z = ex[here, :], ey[here, :], ez[here, :]
+            y_x = pltpu.roll(jnp.where(not_first, y, ey[over, :]), wide - depth, 1)
+            z_x = pltpu.roll(jnp.where(not_first, z, ez[over, :]), wide - depth, 1)
+            hx[here, :] = gated(hx[here, :] - ((ez[ahead, :] - z) - (next_z(y) - y)), start)
+            hy[here, :] = hy[here, :] - ((next_z(x) - x) - (z_x - z))
+            hz[here, :] = gated(hz[here, :] - ((y_x - y) - (ex[ahead, :] - x)), start)
         return carry
 
     def electric(g, carry):
-        before = jnp.maximum(g - 1, 0)
+        base = pl.multiple_of((g + 1) * rows, 8)
+        ex, ey, ez, hx, hy, hz = [field.at[pl.ds(base, 2 * rows), :] for field in state]
+        kept_all, turned_all = keep.at[g], curl.at[g]
         for start in starts:
-            here, behind = pl.ds(start, chunk), pl.ds(start - 1, chunk)
-            x, y, z = hx[g, here, :], hy[g, here, :], hz[g, here, :]
-            y_x = pltpu.roll(jnp.where(not_last, y, hy[before, here, :]), depth, 1)
-            z_x = pltpu.roll(jnp.where(not_last, z, hz[before, here, :]), depth, 1)
-            row = pl.ds(start - first + geo.pad, chunk)
-            kept, turned = keep[g, row, :], curl[g, row, :]
-            ex[g, here, :] = kept * ex[g, here, :] + turned * ((z - hz[g, behind, :]) - (y - last_z(y)))
-            ey[g, here, :] = kept * ey[g, here, :] + turned * ((x - last_z(x)) - (z - z_x))
-            ez[g, here, :] = kept * ez[g, here, :] + turned * ((y - y_x) - (x - hx[g, behind, :]))
+            here, behind = pl.ds(rows + start, chunk), pl.ds(rows + start - 1, chunk)
+            under = pl.ds(start, chunk)
+            x, y, z = hx[here, :], hy[here, :], hz[here, :]
+            y_x = pltpu.roll(jnp.where(not_last, y, hy[under, :]), depth, 1)
+            z_x = pltpu.roll(jnp.where(not_last, z, hz[under, :]), depth, 1)
+            spot = pl.ds(start - first + geo.pad, chunk)
+            kept, turned = kept_all[spot, :], turned_all[spot, :]
+            ex[here, :] = kept * ex[here, :] + turned * ((z - hz[behind, :]) - (y - last_z(y)))
+            ey[here, :] = kept * ey[here, :] + turned * ((x - last_z(x)) - (z - z_x))
+            ez[here, :] = kept * ez[here, :] + turned * ((y - y_x) - (x - hx[behind, :]))
         return carry
 
     near = geo.own * geo.per
 
     def step(index, carry):
-        left = geo.count - 1 - index
+        left = count - 1 - index
         low = (near - left - 1) // geo.per
-        high = (near + geo.cells_x - 1 + left) // geo.per + 1
-        lax.fori_loop(low, high, magnetic, 0)
-
-        @pl.when(low_y)
-        def _():
-            for field in (hx, hz):
-                for g in range(groups):
-                    field[g, first - 1 : first, :] = jnp.zeros((1, wide), F32)
+        high = (near + geo.cells_x - 1 + left) // geo.per
+        lax.fori_loop(low, high + 1, magnetic, 0)
 
         @pl.when(low_x)
         def _():
             for field in (hy, hz):
-                for start in starts:
-                    here = pl.ds(start, chunk)
-                    field[geo.own - 1, here, :] = jnp.where(not_last, field[geo.own - 1, here, :], 0.0)
-
-        lax.fori_loop(low, high, electric, 0)
+                field[geo.at(geo.own - 1, 0, rows), :] = jnp.zeros((rows, wide), F32)
+
+        lax.fori_loop(low, high + 1, electric, 0)
         at = first_step + index
         cosine, sine = moments[at, 0], moments[at, 1]
         middle = depth // 2
         for start in range(0, geo.cells_y, chunk):
-            here = pl.ds(first + start, chunk)
-            seen = ex[geo.own, here, :]
+            seen = ex[geo.at(geo.own, first + start, chunk), :]
             for spot, (field, g) in enumerate(((ex, 1), (ey, 0), (ey, 1)), 1):
-                moved = pltpu.roll(field[geo.own + g, here, :], spot, 1)
+                moved = pltpu.roll(field[geo.at(geo.own + g, first + start, chunk), :], spot, 1)
                 seen = jnp.where(level == middle + spot, moved, seen)
             there = pl.ds(start, chunk)
             phase[0, there, :] = phase[0, there, :] + seen * cosine
             phase[1, there, :] = phase[1, there, :] - seen * sine
         return carry
 
-    lax.fori_loop(0, geo.count, step, 0)
-
-
-def sides(geo):
-    odd_x = lax.axis_index("gx") % 2 == 1
-    below = (geo.own - 1, geo.own - 2)
-    above = (2 * geo.own, 2 * geo.own + 1)
-    return [
-        (jnp.where(odd_x, below[0], above[0]), jnp.where(odd_x, below[1], above[1]), odd_x),
-        (jnp.where(odd_x, above[0], below[0]), jnp.where(odd_x, above[1], below[1]), jnp.logical_not(odd_x)),
-    ]
+    lax.fori_loop(0, count, step, 0)
 
 
 def clear(state, geo, beyond):
     low, high = geo.first - beyond, geo.first + geo.cells_y + beyond
     for field in state:
+        for g in (-2, -1, geo.groups, geo.groups + 1):
+            field[geo.at(g, 0, geo.rows), :] = jnp.zeros((geo.rows, geo.wide), F32)
         for g in range(geo.groups):
-            field[g, 0:low, :] = jnp.zeros((low, geo.wide), F32)
-            field[g, high : geo.rows, :] = jnp.zeros((geo.rows - high, geo.wide), F32)
-
-
-def half_lanes(rows, geo, lower):
-    lane = lax.broadcasted_iota(jnp.int32, (rows, geo.wide), 1)
-    return (lane >= geo.half) == lower
+            field[geo.at(g, 0, low), :] = jnp.zeros((low, geo.wide), F32)
+            field[geo.at(g, high, geo.rows - high), :] = jnp.zeros((geo.rows - high, geo.wide), F32)
 
 
 def first_kernel(
@@ -333,34 +262,22 @@
     state = (ex, ey, ez, hx, hy, hz)
     planes = (*state, kinds)
     even_y = lax.axis_index("gy") % 2 == 0
+    odd_x = lax.axis_index("gx") % 2 == 1
     pad, first, cells_y = geo.pad, geo.first, geo.cells_y
-    main = pl.ds(first, cells_y)
-    spans = (pl.ds(first - pad, pad), pl.ds(first + cells_y, pad))
     clear(state, geo, pad)
+    base_a = jnp.where(odd_x, 0, 2 * geo.own)
+    base_b = jnp.where(odd_x, 2 * geo.own, 0)
     for at, plane in enumerate(planes):
         for group in range(geo.own):
             g = geo.own + group
-            plane[g, main, :] = tile[at, group]
+            plane[geo.at(g, first, cells_y), :] = tile[at, group]
             c_value, d_value = got_c[at, group], got_d[at, group]
-            plane[g, spans[0], :] = jnp.where(even_y, d_value, c_value)
-            plane[g, spans[1], :] = jnp.where(even_y, c_value, d_value)
-    for got, edge, (inner, outer, lower) in zip((got_a, got_b), (edge_a, edge_b), sides(geo)):
-
-        def put_main(at, g, value):
-            planes[at][g, main, :] = value
-
-        unpack_rows(
-            lambda at, got=got: got[at], put_main, PLANES + 1, inner, outer, half_lanes(cells_y, geo, lower), geo.half
-        )
-        for side in range(2):
-
-            def put_side(at, g, value, side=side):
-                planes[at][g, spans[side], :] = value
-
-            unpack_rows(
-                lambda at, edge=edge, side=side: edge[at, side * pad : (side + 1) * pad, :],
-                put_side, PLANES + 1, inner, outer, half_lanes(pad, geo, lower), geo.half,
-            )
+            plane[geo.at(g, first - pad, pad), :] = jnp.where(even_y, d_value, c_value)
+            plane[geo.at(g, first + cells_y, pad), :] = jnp.where(even_y, c_value, d_value)
+            for got, edge, base in ((got_a, edge_a, base_a), (got_b, edge_b, base_b)):
+                plane[geo.at(base + group, first, cells_y), :] = got[at, group]
+                plane[geo.at(base + group, first - pad, pad), :] = edge[at, group, 0:pad]
+                plane[geo.at(base + group, first + cells_y, pad), :] = edge[at, group, pad : 2 * pad]
 
     chunk = 16
     lane = lax.broadcasted_iota(jnp.int32, (chunk, geo.wide), 1)
@@ -374,7 +291,7 @@
         for start in range(0, cells_y + 2 * pad, chunk):
             place_y = base_y + start + row
             inside = inside_x & (place_y >= 0) & (place_y < geo.total_y)
-            kind = kinds[g, pl.ds(first - pad + start, chunk), :]
+            kind = kinds[geo.at(g, first - pad + start, chunk), :]
             kept = jnp.zeros(kind.shape, F32)
             turned = jnp.zeros(kind.shape, F32)
             for material in range(tables.shape[1]):
@@ -388,31 +305,16 @@
 
     lax.fori_loop(0, geo.groups, coefs, 0)
     phase[...] = jnp.zeros(phase.shape, F32)
-    run_steps(state, keep, curl, phase, moments, 0, geo)
-
-    more = pl.ds(first - geo.reach, cells_y + 2 * geo.reach)
-    lane = lax.broadcasted_iota(jnp.int32, (cells_y + 2 * geo.reach, geo.wide), 1)
+    run_steps(state, keep, curl, phase, moments, 0, geo.counts[0], pad, geo)
+
+    rows = cells_y + 2 * geo.reach
+    near_a = jnp.where(odd_x, 0, geo.own - 1)
+    near_b = jnp.where(odd_x, geo.own - 1, 0)
     for at, field in enumerate(state):
         for group in range(geo.own):
-            own[at, group] = field[geo.own + group, more, :]
-
-    def fill(send, upper):
-        def put(at, value):
-            send[at] = value
-
-        pack_rows(lambda at, group: own[at, group], put, PLANES, upper, lane, geo.half)
-
-    even_x = lax.axis_index("gx") % 2 == 0
-
-    @pl.when(even_x)
-    def _():
-        fill(send_a, True)
-        fill(send_b, False)
-
-    @pl.when(jnp.logical_not(even_x))
-    def _():
-        fill(send_a, False)
-        fill(send_b, True)
+            own[at, group] = field[geo.at(geo.own + group, first - geo.reach, rows), :]
+        send_a[at] = field[geo.at(geo.own + near_a, first - geo.reach, rows), :]
+        send_b[at] = field[geo.at(geo.own + near_b, first - geo.reach, rows), :]
 
 
 def second_kernel(
@@ -421,21 +323,22 @@
     ex, ey, ez, hx, hy, hz, seen, *, geo,
 ):
     state = (ex, ey, ez, hx, hy, hz)
-    first, cells_y = geo.first, geo.cells_y
-    rows = cells_y + 2 * geo.reach
-    more = pl.ds(first - geo.reach, rows)
-    clear(state, geo, geo.reach)
+    first, cells_y, reach = geo.first, geo.cells_y, geo.reach
+    rows = cells_y + 2 * reach
+    odd_x = lax.axis_index("gx") % 2 == 1
+    clear(state, geo, reach)
+    below, above = geo.own - 1, 2 * geo.own
+    base_a = jnp.where(odd_x, below, above)
+    base_b = jnp.where(odd_x, above, below)
     for at, field in enumerate(state):
+        for g in (below - 1, above + 1):
+            field[geo.at(g, first - reach, rows), :] = jnp.zeros((rows, geo.wide), F32)
         for group in range(geo.own):
-            field[geo.own + group, more, :] = own[at, group]
-    for got, (inner, outer, lower) in zip((got_a, got_b), sides(geo)):
-
-        def put(at, g, value):
-            state[at][g, more, :] = value
-
-        unpack_rows(lambda at, got=got: got[at], put, PLANES, inner, outer, half_lanes(rows, geo, lower), geo.half)
+            field[geo.at(geo.own + group, first - reach, rows), :] = own[at, group]
+        field[geo.at(base_a, first - reach, rows), :] = got_a[at]
+        field[geo.at(base_b, first - reach, rows), :] = got_b[at]
     seen[...] = phase_in[...]
-    run_steps(state, keep, curl, seen, moments, geo.count, geo)
+    run_steps(state, keep, curl, seen, moments, geo.counts[0], geo.counts[1], reach, geo)
     middle = geo.depth // 2
     for part in range(2):
         turned = seen[part].T
@@ -447,7 +350,7 @@
                     phase[target : target + 1, :] = turned[source : source + 1, :]
     for at, field in enumerate(state):
         for group in range(geo.own):
-            values = field[geo.own + group, pl.ds(first, cells_y), :].T
+            values = field[geo.at(geo.own + group, first, cells_y), :].T
             if at >= 3:
                 values = values * COURANT
             for within in range(geo.per):
@@ -564,8 +467,7 @@
     tiles_y = lax.axis_size("gy")
     _, depth, cells_x, lanes = fields.shape
     total_x, total_y = cells_x * tiles_x, lanes * tiles_y
-    count = STEPS // ROUNDS
-    geo = Geo(depth, cells_x, lanes, total_x, total_y, count)
+    geo = Geo(depth, cells_x, lanes, total_x, total_y)
     flat_fields = fields.reshape(6, depth * cells_x, lanes)
     flat_map = material_map.reshape(depth * cells_x, lanes)
     local, orders_p, orders_q = source_mask.shape
@@ -577,14 +479,11 @@
     angle = np.float32(ANGULAR) * np.arange(1, STEPS + 1, dtype=np.float32)
     moments = jnp.asarray(np.stack((np.cos(angle), np.sin(angle)), 1).astype(np.float32))
 
-    sent = PLANES + 1 + halves_of(PLANES + 1)
-    row_shape = shape(sent, lanes, wide)
     side_shape = shape(PLANES + 1, geo.own, geo.pad, wide)
-    edge_shape = shape(sent, 2 * geo.pad, wide)
-    tile, to_a, to_b, to_c, to_d = call(
+    tile, to_c, to_d = call(
         functools.partial(pack_kernel, geo=geo),
         [(flat_fields, "h"), (flat_map, "h")],
-        [shape(PLANES + 1, geo.own, lanes, wide), row_shape, row_shape, side_shape, side_shape],
+        [shape(PLANES + 1, geo.own, lanes, wide), side_shape, side_shape],
         [
             pltpu.VMEM(flat_fields.shape, F32),
             pltpu.VMEM(flat_map.shape, jnp.int32),
@@ -593,11 +492,30 @@
     )
     got_c = swap(to_c, "gy", 0)
     got_d = swap(to_d, "gy", 1)
+    got_a = swap(tile, "gx", 0)
+    got_b = swap(tile, "gx", 1)
+    (edges,) = call(
+        functools.partial(edge_kernel, geo=geo),
+        [(got_c, "v"), (got_d, "v")],
+        [shape(PLANES + 1, geo.own, 2 * geo.pad, wide)],
+    )
+    edge_a = swap(edges, "gx", 0)
+    edge_b = swap(edges, "gx", 1)
+
+    state = [geo.plane() for _ in range(PLANES)]
+    coef_shape = shape(geo.groups, lanes + 2 * geo.pad, wide)
+    seen_shape = shape(2, lanes, wide)
+    longer = lanes + 2 * geo.reach
+    send_shape = shape(PLANES, longer, wide)
+    own, keep, curl, seen, to_a, to_b = call(
+        functools.partial(first_kernel, geo=geo),
+        [(tile, "v"), (got_a, "v"), (got_b, "v"), (got_c, "v"), (got_d, "v"), (edge_a, "v"), (edge_b, "v"),
+         (tables, "s"), (moments, "s")],
+        [shape(PLANES, geo.own, longer, wide), coef_shape, coef_shape, seen_shape, send_shape, send_shape],
+        [*state, geo.plane()],
+    )
     got_a = swap(to_a, "gx", 0)
     got_b = swap(to_b, "gx", 1)
-    to_a, to_b = call(functools.partial(edge_kernel, geo=geo), [(got_c, "v"), (got_d, "v")], [edge_shape, edge_shape])
-    edge_a = swap(to_a, "gx", 0)
-    edge_b = swap(to_b, "gx", 1)
     (my_pack,) = call(
         source_kernel,
         [(source_mask, "c"), (source_shift.T, "s"), (source_weight, "s")],
@@ -607,21 +525,6 @@
     packs = [my_pack]
     for by in range(1, tiles_y):
         packs.append(cyclic(my_pack, "gy", by))
-
-    state = [pltpu.VMEM((geo.groups, geo.rows, wide), F32) for _ in range(PLANES)]
-    coef_shape = shape(geo.groups, lanes + 2 * geo.pad, wide)
-    seen_shape = shape(2, lanes, wide)
-    longer = lanes + 2 * geo.reach
-    send_shape = shape(PLANES + halves_of(PLANES), longer, wide)
-    own, keep, curl, seen, to_a, to_b = call(
-        functools.partial(first_kernel, geo=geo),
-        [(tile, "v"), (got_a, "v"), (got_b, "v"), (got_c, "v"), (got_d, "v"), (edge_a, "v"), (edge_b, "v"),
-         (tables, "s"), (moments, "s")],
-        [shape(PLANES, geo.own, longer, wide), coef_shape, coef_shape, seen_shape, send_shape, send_shape],
-        [*state, pltpu.VMEM((geo.groups, geo.rows, wide), F32)],
-    )
-    got_a = swap(to_a, "gx", 0)
-    got_b = swap(to_b, "gx", 1)
     final, phase = call(
         functools.partial(second_kernel, geo=geo),
         [(own, "v"), (keep, "v"), (curl, "v"), (seen, "v"), (got_a, "v"), (got_b, "v"), (moments, "s")],

time: 92.3 us -> 93 us (level)
  waiting for transfers between devices: 21.8 us -> 23.2 us
    ppermute x12, starting transfers between devices: 23.9 us -> 20.4 us  [cyclic(): lax.ppermute(values, axis, [(i, (i + by) % count) for i in range(count)])]
    ppermute x8, starting transfers between devices: 14.2 us -> 16.9 us  [swap(): return lax.ppermute(values, axis, pairs)]
    ppermute x12, waiting for transfers between devices: 19.4 us -> 20.8 us  [cyclic(): lax.ppermute(values, axis, [(i, (i + by) % count) for i in range(count)])]
  transfers between devices with their start and end apart: 20 -> 20, of which waited for: 9 -> 10; matrix products, arithmetic and copies ran while one was open for 0% -> 0% of each run, Pallas kernels for 1% -> 1%
where the time goes in v4:
time: 93 us; the launch traced here: 92.7 us
  starting transfers between devices  37.4 us (40%)
  Pallas kernels  30.4 us (33%)
  waiting for transfers between devices  23.2 us (25%)
    pallas_call x7, Pallas kernels, call(): pl.pallas_call(kernel, out_shape=outs, in_specs=[spaces[space]() for _, s...  30.4 us
    ppermute x12, waiting for transfers between devices, cyclic(): lax.ppermute(values, axis, [(i, (i + by) % count) for i in range(count)])  20.8 us
    ppermute x12, starting transfers between devices, cyclic(): lax.ppermute(values, axis, [(i, (i + by) % count) for i in range(count)])  20.4 us
    ppermute x8, starting transfers between devices, swap(): return lax.ppermute(values, axis, pairs)  16.9 us
    ppermute x8, waiting for transfers between devices, swap(): return lax.ppermute(values, axis, pairs)  2.37 us
  transfers between devices with their start and end apart: 20, of which 10 were waited for; matrix products, arithmetic and copies ran while one was open for 0% of the time, Pallas kernels for 1%

profile of v4, /device:TPU:0, one launch (start us, length us, event | category | flops | bytes accessed | tf_op | source)
XLA Modules:
  0.0 92.7 jit_solution(5881134288808072951)
XLA Ops:
  0.6 1.5 %shard_map.131 = (f32[7,2,128,128]{3,2,1,0:T(8,128)S(1)}, f32[7,2,16,128]{3,2,1,0:T(8,128)S(1)}, f32[7,2,16,128]{3,2,1,0:T(8,128)S(1)}) custom-call(f32[6,256,128]{2,1,0:T(8,128)} %bitcast.13, s32[256,128]{1,0:T(8,128)} %bitcast.14), custom_call_target="tpu_custom_call" | custom-call | tf_op jit(solution)/shard_map/pallas_call | solution.py:48
  2.1 0.6 collective-permute-start
  2.7 0.7 collective-permute-start.1
  3.4 2.6 %collective-permute-start.2 = (f32[7,2,16,128]{3,2,1,0:T(8,128)S(1)}, f32[7,2,16,128]{3,2,1,0:T(8,128)S(1)}, u32[]{:S(2)}, u32[]{:S(2)}) collective-permute-start(f32[7,2,16,128]{3,2,1,0:T(8,128)S(1)} %get-tuple-element.20), channel_id=1, source_target_pairs={{0,1},{1,0},{2,3},{3,2},{4,5},{5,4},{6,7},{7,6},{8,9},{9,8},{10,11... | collective-permute-start | bytes 344072 | tf_op jit(solution)/shard_map/ppermute | solution.py:69
  6.0 0.8 collective-permute-start.3
  6.8 2.0 %collective-permute-done.2.got_c = f32[7,2,16,128]{3,2,1,0:T(8,128)S(1)} collective-permute-done((f32[7,2,16,128]{3,2,1,0:T(8,128)S(1)}, f32[7,2,16,128]{3,2,1,0:T(8,128)S(1)}, u32[]{:S(2)}, u32[]{:S(2)}) %collective-permute-start.2) | collective-permute-done | bytes 114720 | tf_op jit(solution)/shard_map/ppermute | solution.py:69
  8.8 2.2 %collective-permute-start.4 = (f32[7,2,32,128]{3,2,1,0:T(8,128)S(1)}, f32[7,2,32,128]{3,2,1,0:T(8,128)S(1)}, u32[]{:S(2)}, u32[]{:S(2)}) collective-permute-start(f32[7,2,32,128]{3,2,1,0:T(8,128)S(1)} %shard_map.132), channel_id=1, source_target_pairs={{0,4},{4,0},{8,12},{12,8},{1,5},{5,1},{9,13},{13,9},{2,6},{6,2},{1... | collective-permute-start | bytes 688136 | tf_op jit(solution)/shard_map/ppermute | solution.py:69
  11.0 0.7 collective-permute-start.5
  12.2 14.6 %shard_map.133 = (f32[6,2,144,128]{3,2,1,0:T(8,128)S(1)}, f32[6,160,128]{2,1,0:T(8,128)S(1)}, f32[6,160,128]{2,1,0:T(8,128)S(1)}, f32[2,128,128]{2,1,0:T(8,128)S...) custom-call(f32[7,2,128,128]{3,2,1,0:T(8,128)S(1)} %get-tuple-element.19.tile, ...), custom_call_target="tpu_custom_call" | custom-call | tf_op jit(solution)/shard_map/pallas_call | solution.py:48
  26.8 8.6 %collective-permute-start.6 = (f32[6,144,128]{2,1,0:T(8,128)S(1)}, f32[6,144,128]{2,1,0:T(8,128)S(1)}, u32[]{:S(2)}, u32[]{:S(2)}) collective-permute-start(f32[6,144,128]{2,1,0:T(8,128)S(1)} %get-tuple-element.26), channel_id=1, source_target_pairs={{0,4},{4,0},{8,12},{12,8},{1,5},{5,1},{9,13},{13,9},{2,6},{6,2},{1... | collective-permute-start | bytes 1327112 | tf_op jit(solution)/shard_map/ppermute | solution.py:69
  35.3 0.8 collective-permute-start.7
  36.2 0.7 shard_map.136.refs_4_
  36.9 2.4 %collective-permute-start.14 = (f32[4,104,128]{2,1,0:T(8,128)S(1)}, f32[4,104,128]{2,1,0:T(8,128)S(1)}, u32[]{:S(2)}, u32[]{:S(2)}) collective-permute-start(f32[4,104,128]{2,1,0:T(8,128)S(1)} %shard_map.136.refs_4_), channel_id=1, source_target_pairs={{0,1},{1,2},{2,3},{3,0},{4,5},{5,6},{6,7},{7,4},{8,9},{9,10},{10,1... | collective-permute-start | bytes 638984 | tf_op jit(solution)/shard_map/ppermute | solution.py:74
  39.3 2.4 %collective-permute-start.15 = (f32[4,104,128]{2,1,0:T(8,128)S(1)}, f32[4,104,128]{2,1,0:T(8,128)S(1)}, u32[]{:S(2)}, u32[]{:S(2)}) collective-permute-start(f32[4,104,128]{2,1,0:T(8,128)S(1)} %shard_map.136.refs_4_), channel_id=1, source_target_pairs={{0,2},{1,3},{2,0},{3,1},{4,6},{5,7},{6,4},{7,5},{8,10},{9,11},{10,... | collective-permute-start | bytes 638984 | tf_op jit(solution)/shard_map/ppermute | solution.py:74
  41.7 2.0 %collective-permute-start.16 = (f32[4,104,128]{2,1,0:T(8,128)S(1)}, f32[4,104,128]{2,1,0:T(8,128)S(1)}, u32[]{:S(2)}, u32[]{:S(2)}) collective-permute-start(f32[4,104,128]{2,1,0:T(8,128)S(1)} %shard_map.136.refs_4_), channel_id=1, source_target_pairs={{0,3},{1,0},{2,1},{3,2},{4,7},{5,4},{6,5},{7,6},{8,11},{9,8},{10,9... | collective-permute-start | bytes 638984 | tf_op jit(solution)/shard_map/ppermute | solution.py:74
  43.7 2.1 %collective-permute-done.14.refs_5_ = f32[4,104,128]{2,1,0:T(8,128)S(1)} collective-permute-done((f32[4,104,128]{2,1,0:T(8,128)S(1)}, f32[4,104,128]{2,1,0:T(8,128)S(1)}, u32[]{:S(2)}, u32[]{:S(2)}) %collective-permute-start.14) | collective-permute-done | bytes 213024 | tf_op jit(solution)/shard_map/ppermute | solution.py:74
  45.8 10.5 %collective-permute-done.15.refs_6_ = f32[4,104,128]{2,1,0:T(8,128)S(1)} collective-permute-done((f32[4,104,128]{2,1,0:T(8,128)S(1)}, f32[4,104,128]{2,1,0:T(8,128)S(1)}, u32[]{:S(2)}, u32[]{:S(2)}) %collective-permute-start.15) | collective-permute-done | bytes 213024 | tf_op jit(solution)/shard_map/ppermute | solution.py:74
  56.3 6.4 %shard_map.134 = (f32[6,256,128]{2,1,0:T(8,128)S(1)}, f32[32,128]{1,0:T(8,128)S(1)}) custom-call(f32[6,2,144,128]{3,2,1,0:T(8,128)S(1)} %get-tuple-element.22.own, f32[6,160,128]{2,1,0:T(8,128)S(1)} %get-tuple-element.23.keep, f32[6,160,128]{2,1,0:T(8,128)S(1)} %get-tuple-element.24.curl, f32[2,128,128]{2,1,0:T(8,128)S(1)} %get-tuple-element.25.phase_in, ...), custom_call_target="tpu_custom_call" | custom-call | tf_op jit(solution)/shard_map/pallas_call | solution.py:48
  62.7 5.4 %collective-permute-start.10 = (f32[32,128]{1,0:T(8,128)S(1)}, f32[32,128]{1,0:T(8,128)S(1)}, u32[]{:S(2)}, u32[]{:S(2)}) collective-permute-start(f32[32,128]{1,0:T(8,128)S(1)} %get-tuple-element.28.refs_0_), channel_id=1, source_target_pairs={{0,3},{1,0},{2,1},{3,2},{4,7},{5,4},{6,5},{7,6},{8,11},{9,8},{10,9... | collective-permute-start | bytes 49160 | tf_op jit(solution)/shard_map/ppermute | solution.py:74
  68.1 1.2 %collective-permute-start.9 = (f32[32,128]{1,0:T(8,128)S(1)}, f32[32,128]{1,0:T(8,128)S(1)}, u32[]{:S(2)}, u32[]{:S(2)}) collective-permute-start(f32[32,128]{1,0:T(8,128)S(1)} %get-tuple-element.28.refs_0_), channel_id=1, source_target_pairs={{0,2},{1,3},{2,0},{3,1},{4,6},{5,7},{6,4},{7,5},{8,10},{9,11},{10,... | collective-permute-start | bytes 49160 | tf_op jit(solution)/shard_map/ppermute | solution.py:74
  69.6 4.0 %collective-permute-done.8.refs_1_ = f32[32,128]{1,0:T(8,128)S(1)} collective-permute-done((f32[32,128]{1,0:T(8,128)S(1)}, f32[32,128]{1,0:T(8,128)S(1)}, u32[]{:S(2)}, u32[]{:S(2)}) %collective-permute-start.8) | collective-permute-done | bytes 16416 | tf_op jit(solution)/shard_map/ppermute | solution.py:74
  73.7 0.9 shard_map.135
  74.6 0.4 collective-permute-start.11
  75.0 2.8 %collective-permute-start.12 = (f32[16,256]{1,0:T(8,128)S(1)}, f32[16,256]{1,0:T(8,128)S(1)}, u32[]{:S(2)}, u32[]{:S(2)}) collective-permute-start(f32[16,256]{1,0:T(8,128)S(1)} %get-tuple-element.31.refs_0_), channel_id=1, source_target_pairs={{0,8},{4,12},{8,0},{12,4},{1,9},{5,13},{9,1},{13,5},{2,10},{6,14},... | collective-permute-start | bytes 49160 | tf_op jit(solution)/shard_map/ppermute | solution.py:74
  77.8 1.4 %collective-permute-start.13 = (f32[16,256]{1,0:T(8,128)S(1)}, f32[16,256]{1,0:T(8,128)S(1)}, u32[]{:S(2)}, u32[]{:S(2)}) collective-permute-start(f32[16,256]{1,0:T(8,128)S(1)} %get-tuple-element.31.refs_0_), channel_id=1, source_target_pairs={{0,12},{4,0},{8,4},{12,8},{1,13},{5,1},{9,5},{13,9},{2,14},{6,2},{... | collective-permute-start | bytes 49160 | tf_op jit(solution)/shard_map/ppermute | solution.py:74
  79.5 1.1 %collective-permute-done.13.refs_3_ = f32[16,256]{1,0:T(8,128)S(1)} collective-permute-done((f32[16,256]{1,0:T(8,128)S(1)}, f32[16,256]{1,0:T(8,128)S(1)}, u32[]{:S(2)}, u32[]{:S(2)}) %collective-permute-start.13) | collective-permute-done | bytes 16416 | tf_op jit(solution)/shard_map/ppermute | solution.py:74
  80.6 6.3 %shard_map.137 = (f32[32,512]{1,0:T(8,128)S(1)}, f32[32,512]{1,0:T(8,128)S(1)}, f32[32,512]{1,0:T(8,128)S(1)}, f32[32,512]{1,0:T(8,128)S(1)}) custom-call(f32[16,256]{1,0:T(8,128)S(1)} %get-tuple-element.31.refs_0_, f32[16,256]{1,0:T(8,128)S(1)} %collective-permute-done.11.refs_1_, f32[16,256]{1,0:T(8,128)S(1)} %collective-permute-done.12.refs_2_, ...), custom_call_target="tpu_custom_call" | custom-call | tf_op jit(solution)/shard_map/pallas_call | solution.py:48
  86.9 0.4 collective-permute-start.17
  87.3 1.7 %collective-permute-start.18 = (f32[32,512]{1,0:T(8,128)S(1)}, f32[32,512]{1,0:T(8,128)S(1)}, u32[]{:S(2)}, u32[]{:S(2)}) collective-permute-start(f32[32,512]{1,0:T(8,128)S(1)} %get-tuple-element.34), channel_id=1, source_target_pairs={{0,8},{4,12},{8,0},{12,4},{1,9},{5,13},{9,1},{13,5},{2,10},{6,14},... | collective-permute-start | bytes 196616 | tf_op jit(solution)/shard_map/ppermute | solution.py:74
  89.3 1.3 %collective-permute-done.17 = f32[32,512]{1,0:T(8,128)S(1)} collective-permute-done((f32[32,512]{1,0:T(8,128)S(1)}, f32[32,512]{1,0:T(8,128)S(1)}, u32[]{:S(2)}, u32[]{:S(2)}) %collective-permute-start.17) | collective-permute-done | bytes 65568 | tf_op jit(solution)/shard_map/ppermute | solution.py:74
  90.6 1.4 %collective-permute-done.18 = f32[32,512]{1,0:T(8,128)S(1)} collective-permute-done((f32[32,512]{1,0:T(8,128)S(1)}, f32[32,512]{1,0:T(8,128)S(1)}, u32[]{:S(2)}, u32[]{:S(2)}) %collective-permute-start.18) | collective-permute-done | bytes 65568 | tf_op jit(solution)/shard_map/ppermute | solution.py:74
  92.1 0.6 add_add_fusion
  (45 shorter events, 1.4 us)
Async XLA Ops:
  2.1 10.0 %collective-permute-start = (f32[7,2,128,128]{3,2,1,0:T(8,128)S(1)}, f32[7,2,128,128]{3,2,1,0:T(8,128)S(1)}, u32[]{:S(2)}, u32[]{:S(2)}) collective-permute-start(f32[7,2,128,128]{3,2,1,0:T(8,128)S(1)} %get-tuple-element.19.tile), channel_id=1, source_target_pairs={{0,4},{4,0},{8,12},{12,8},{1,5},{5,1},{9,13},{13,9},{2,6},{6,2},{1... | collective-permute-start | bytes 2752520 | tf_op jit(solution)/shard_map/ppermute | solution.py:69
  2.7 9.5 %collective-permute-start.1 = (f32[7,2,128,128]{3,2,1,0:T(8,128)S(1)}, f32[7,2,128,128]{3,2,1,0:T(8,128)S(1)}, u32[]{:S(2)}, u32[]{:S(2)}) collective-permute-start(f32[7,2,128,128]{3,2,1,0:T(8,128)S(1)} %get-tuple-element.19.tile), channel_id=1, source_target_pairs={{4,8},{8,4},{5,9},{9,5},{6,10},{10,6},{7,11},{11,7},{20,24},{24,20... | collective-permute-start | bytes 2752520 | tf_op jit(solution)/shard_map/ppermute | solution.py:69
  3.4 5.4 %collective-permute-start.2 = (f32[7,2,16,128]{3,2,1,0:T(8,128)S(1)}, f32[7,2,16,128]{3,2,1,0:T(8,128)S(1)}, u32[]{:S(2)}, u32[]{:S(2)}) collective-permute-start(f32[7,2,16,128]{3,2,1,0:T(8,128)S(1)} %get-tuple-element.20), channel_id=1, source_target_pairs={{0,1},{1,0},{2,3},{3,2},{4,5},{5,4},{6,7},{7,6},{8,9},{9,8},{10,11... | collective-permute-start | bytes 344072 | tf_op jit(solution)/shard_map/ppermute | solution.py:69
  6.0 5.7 %copy-start.8 = (f32[4]{0:T(128)S(1)}, f32[4]{0:T(128)}, u32[]{:S(2)}) copy-start(f32[4]{0:T(128)} %param.15) | copy-start | bytes 52
  6.0 5.7 %copy-start.9 = (f32[4]{0:T(128)S(1)}, f32[4]{0:T(128)}, u32[]{:S(2)}) copy-start(f32[4]{0:T(128)} %param.14) | copy-start | bytes 52
  6.0 2.8 %collective-permute-start.3 = (f32[7,2,16,128]{3,2,1,0:T(8,128)S(1)}, f32[7,2,16,128]{3,2,1,0:T(8,128)S(1)}, u32[]{:S(2)}, u32[]{:S(2)}) collective-permute-start(f32[7,2,16,128]{3,2,1,0:T(8,128)S(1)} %get-tuple-element.21), channel_id=1, source_target_pairs={{1,2},{2,1},{5,6},{6,5},{9,10},{10,9},{13,14},{14,13},{17,18},{18,... | collective-permute-start | bytes 344072 | tf_op jit(solution)/shard_map/ppermute | solution.py:69
  8.8 3.3 %copy-start.5 = (f32[12,2]{1,0:T(8,128)S(1)}, f32[12,2]{1,0:T(8,128)}, u32[]{:S(2)}) copy-start(f32[12,2]{1,0:T(8,128)} %constant.14.clone.moments) | copy-start | bytes 292
  8.8 3.3 %collective-permute-start.4 = (f32[7,2,32,128]{3,2,1,0:T(8,128)S(1)}, f32[7,2,32,128]{3,2,1,0:T(8,128)S(1)}, u32[]{:S(2)}, u32[]{:S(2)}) collective-permute-start(f32[7,2,32,128]{3,2,1,0:T(8,128)S(1)} %shard_map.132), channel_id=1, source_target_pairs={{0,4},{4,0},{8,12},{12,8},{1,5},{5,1},{9,13},{13,9},{2,6},{6,2},{1... | collective-permute-start | bytes 688136 | tf_op jit(solution)/shard_map/ppermute | solution.py:69
  11.0 1.1 %collective-permute-start.5 = (f32[7,2,32,128]{3,2,1,0:T(8,128)S(1)}, f32[7,2,32,128]{3,2,1,0:T(8,128)S(1)}, u32[]{:S(2)}, u32[]{:S(2)}) collective-permute-start(f32[7,2,32,128]{3,2,1,0:T(8,128)S(1)} %shard_map.132), channel_id=1, source_target_pairs={{4,8},{8,4},{5,9},{9,5},{6,10},{10,6},{7,11},{11,7},{20,24},{24,20... | collective-permute-start | bytes 688136 | tf_op jit(solution)/shard_map/ppermute | solution.py:69
  11.7 24.4 %copy-start.3 = (s32[4,96,96]{2,1,0:T(8,128)S(1)}, s32[4,96,96]{2,1,0:T(8,128)}, u32[]{:S(2)}) copy-start(s32[4,96,96]{2,1,0:T(8,128)} %masks.1) | copy-start | bytes 442372
  26.8 29.5 %collective-permute-start.6 = (f32[6,144,128]{2,1,0:T(8,128)S(1)}, f32[6,144,128]{2,1,0:T(8,128)S(1)}, u32[]{:S(2)}, u32[]{:S(2)}) collective-permute-start(f32[6,144,128]{2,1,0:T(8,128)S(1)} %get-tuple-element.26), channel_id=1, source_target_pairs={{0,4},{4,0},{8,12},{12,8},{1,5},{5,1},{9,13},{13,9},{2,6},{6,2},{1... | collective-permute-start | bytes 1327112 | tf_op jit(solution)/shard_map/ppermute | solution.py:69
  35.3 0.8 copy-start.6
  35.3 0.8 copy-start.7
  35.3 21.0 %collective-permute-start.7 = (f32[6,144,128]{2,1,0:T(8,128)S(1)}, f32[6,144,128]{2,1,0:T(8,128)S(1)}, u32[]{:S(2)}, u32[]{:S(2)}) collective-permute-start(f32[6,144,128]{2,1,0:T(8,128)S(1)} %get-tuple-element.27), channel_id=1, source_target_pairs={{4,8},{8,4},{5,9},{9,5},{6,10},{10,6},{7,11},{11,7},{20,24},{24,20... | collective-permute-start | bytes 1327112 | tf_op jit(solution)/shard_map/ppermute | solution.py:69
  36.9 8.9 %collective-permute-start.14 = (f32[4,104,128]{2,1,0:T(8,128)S(1)}, f32[4,104,128]{2,1,0:T(8,128)S(1)}, u32[]{:S(2)}, u32[]{:S(2)}) collective-permute-start(f32[4,104,128]{2,1,0:T(8,128)S(1)} %shard_map.136.refs_4_), channel_id=1, source_target_pairs={{0,1},{1,2},{2,3},{3,0},{4,5},{5,6},{6,7},{7,4},{8,9},{9,10},{10,1... | collective-permute-start | bytes 638984 | tf_op jit(solution)/shard_map/ppermute | solution.py:74
  39.3 16.9 %collective-permute-start.15 = (f32[4,104,128]{2,1,0:T(8,128)S(1)}, f32[4,104,128]{2,1,0:T(8,128)S(1)}, u32[]{:S(2)}, u32[]{:S(2)}) collective-permute-start(f32[4,104,128]{2,1,0:T(8,128)S(1)} %shard_map.136.refs_4_), channel_id=1, source_target_pairs={{0,2},{1,3},{2,0},{3,1},{4,6},{5,7},{6,4},{7,5},{8,10},{9,11},{10,... | collective-permute-start | bytes 638984 | tf_op jit(solution)/shard_map/ppermute | solution.py:74
  41.7 14.6 %collective-permute-start.16 = (f32[4,104,128]{2,1,0:T(8,128)S(1)}, f32[4,104,128]{2,1,0:T(8,128)S(1)}, u32[]{:S(2)}, u32[]{:S(2)}) collective-permute-start(f32[4,104,128]{2,1,0:T(8,128)S(1)} %shard_map.136.refs_4_), channel_id=1, source_target_pairs={{0,3},{1,0},{2,1},{3,2},{4,7},{5,4},{6,5},{7,6},{8,11},{9,8},{10,9... | collective-permute-start | bytes 638984 | tf_op jit(solution)/shard_map/ppermute | solution.py:74
  56.3 17.3 %copy-start.2 = (f32[4,128,256]{2,1,0:T(8,128)S(1)}, f32[4,128,256]{2,1,0:T(8,128)}, u32[]{:S(2)}) copy-start(f32[4,128,256]{2,1,0:T(8,128)} %constant.15.clone.refs_4_) | copy-start | bytes 1572868
  62.7 6.9 %collective-permute-start.10 = (f32[32,128]{1,0:T(8,128)S(1)}, f32[32,128]{1,0:T(8,128)S(1)}, u32[]{:S(2)}, u32[]{:S(2)}) collective-permute-start(f32[32,128]{1,0:T(8,128)S(1)} %get-tuple-element.28.refs_0_), channel_id=1, source_target_pairs={{0,3},{1,0},{2,1},{3,2},{4,7},{5,4},{6,5},{7,6},{8,11},{9,8},{10,9... | collective-permute-start | bytes 49160 | tf_op jit(solution)/shard_map/ppermute | solution.py:74
  68.1 5.5 %collective-permute-start.8 = (f32[32,128]{1,0:T(8,128)S(1)}, f32[32,128]{1,0:T(8,128)S(1)}, u32[]{:S(2)}, u32[]{:S(2)}) collective-permute-start(f32[32,128]{1,0:T(8,128)S(1)} %get-tuple-element.28.refs_0_), channel_id=1, source_target_pairs={{0,1},{1,2},{2,3},{3,0},{4,5},{5,6},{6,7},{7,4},{8,9},{9,10},{10,1... | collective-permute-start | bytes 49160 | tf_op jit(solution)/shard_map/ppermute | solution.py:74
  68.1 5.5 %collective-permute-start.9 = (f32[32,128]{1,0:T(8,128)S(1)}, f32[32,128]{1,0:T(8,128)S(1)}, u32[]{:S(2)}, u32[]{:S(2)}) collective-permute-start(f32[32,128]{1,0:T(8,128)S(1)} %get-tuple-element.28.refs_0_), channel_id=1, source_target_pairs={{0,2},{1,3},{2,0},{3,1},{4,6},{5,7},{6,4},{7,5},{8,10},{9,11},{10,... | collective-permute-start | bytes 49160 | tf_op jit(solution)/shard_map/ppermute | solution.py:74
  73.7 6.9 %copy-start = (bf16[1024,256]{1,0:T(8,128)(2,1)S(1)}, bf16[1024,256]{1,0:T(8,128)(2,1)}, u32[]{:S(2)}) copy-start(bf16[1024,256]{1,0:T(8,128)(2,1)} %constant.17.clone.refs_9_) | copy-start | bytes 1572868
  73.7 6.9 %copy-start.1 = (f32[2,16,32,128]{3,2,1,0:T(8,128)S(1)}, f32[2,16,32,128]{3,2,1,0:T(8,128)}, u32[]{:S(2)}) copy-start(f32[2,16,32,128]{3,2,1,0:T(8,128)} %constant.18.clone.refs_10_) | copy-start | bytes 1572868
  73.7 6.9 %copy-start.4 = (f32[256,32]{1,0:T(8,128)S(1)}, f32[256,32]{1,0:T(8,128)}, u32[]{:S(2)}) copy-start(f32[256,32]{1,0:T(8,128)} %constant.16.clone.refs_8_) | copy-start | bytes 98308
  74.6 4.7 %collective-permute-start.11 = (f32[16,256]{1,0:T(8,128)S(1)}, f32[16,256]{1,0:T(8,128)S(1)}, u32[]{:S(2)}, u32[]{:S(2)}) collective-permute-start(f32[16,256]{1,0:T(8,128)S(1)} %get-tuple-element.31.refs_0_), channel_id=1, source_target_pairs={{0,4},{4,8},{8,12},{12,0},{1,5},{5,9},{9,13},{13,1},{2,6},{6,10},{... | collective-permute-start | bytes 49160 | tf_op jit(solution)/shard_map/ppermute | solution.py:74
  75.0 4.5 %collective-permute-start.12 = (f32[16,256]{1,0:T(8,128)S(1)}, f32[16,256]{1,0:T(8,128)S(1)}, u32[]{:S(2)}, u32[]{:S(2)}) collective-permute-start(f32[16,256]{1,0:T(8,128)S(1)} %get-tuple-element.31.refs_0_), channel_id=1, source_target_pairs={{0,8},{4,12},{8,0},{12,4},{1,9},{5,13},{9,1},{13,5},{2,10},{6,14},... | collective-permute-start | bytes 49160 | tf_op jit(solution)/shard_map/ppermute | solution.py:74
  77.8 2.8 %collective-permute-start.13 = (f32[16,256]{1,0:T(8,128)S(1)}, f32[16,256]{1,0:T(8,128)S(1)}, u32[]{:S(2)}, u32[]{:S(2)}) collective-permute-start(f32[16,256]{1,0:T(8,128)S(1)} %get-tuple-element.31.refs_0_), channel_id=1, source_target_pairs={{0,12},{4,0},{8,4},{12,8},{1,13},{5,1},{9,5},{13,9},{2,14},{6,2},{... | collective-permute-start | bytes 49160 | tf_op jit(solution)/shard_map/ppermute | solution.py:74
  86.9 3.7 %collective-permute-start.17 = (f32[32,512]{1,0:T(8,128)S(1)}, f32[32,512]{1,0:T(8,128)S(1)}, u32[]{:S(2)}, u32[]{:S(2)}) collective-permute-start(f32[32,512]{1,0:T(8,128)S(1)} %get-tuple-element.33), channel_id=1, source_target_pairs={{0,4},{4,8},{8,12},{12,0},{1,5},{5,9},{9,13},{13,1},{2,6},{6,10},{... | collective-permute-start | bytes 196616 | tf_op jit(solution)/shard_map/ppermute | solution.py:74
  87.3 4.7 %collective-permute-start.18 = (f32[32,512]{1,0:T(8,128)S(1)}, f32[32,512]{1,0:T(8,128)S(1)}, u32[]{:S(2)}, u32[]{:S(2)}) collective-permute-start(f32[32,512]{1,0:T(8,128)S(1)} %get-tuple-element.34), channel_id=1, source_target_pairs={{0,8},{4,12},{8,0},{12,4},{1,9},{5,13},{9,1},{13,5},{2,10},{6,14},... | collective-permute-start | bytes 196616 | tf_op jit(solution)/shard_map/ppermute | solution.py:74
  89.1 3.0 %collective-permute-start.19 = (f32[32,512]{1,0:T(8,128)S(1)}, f32[32,512]{1,0:T(8,128)S(1)}, u32[]{:S(2)}, u32[]{:S(2)}) collective-permute-start(f32[32,512]{1,0:T(8,128)S(1)} %get-tuple-element.35), channel_id=1, source_target_pairs={{0,12},{4,0},{8,4},{12,8},{1,13},{5,1},{9,5},{13,9},{2,14},{6,2},{... | collective-permute-start | bytes 196616 | tf_op jit(solution)/shard_map/ppermute | solution.py:74
